TPU v7x, 32 devices: a whole 2x2x4 slice. The times are simulated.
32 devices in a mesh: seq: 4 (over y, x), ctx: 8 (over z, core).
Axes of the slice: x: 2, y: 2, z: 4, core: 2. Of those that a mesh axis runs over, the one named last changes fastest.
Arguments:
- hidden_in: bfloat16 [4, 2048, 2048], P('seq', 'ctx'), may hold values from -6 to 6
- attn_gain: bfloat16 [2048], P(('seq', 'ctx')), may hold values from 0.5 to 1.5
- w_query: bfloat16 [2048, 2048], P(('seq', 'ctx')), may hold values from -0.125 to 0.125
- w_key: bfloat16 [2048, 256], P(('seq', 'ctx')), may hold values from -0.125 to 0.125
- w_value: bfloat16 [2048, 256], P(('seq', 'ctx')), may hold values from -0.125 to 0.125
- w_out: bfloat16 [2048, 2048], P(('seq', 'ctx')), may hold values from -1 to 1
- ffn_gain: bfloat16 [2048], P(('seq', 'ctx')), may hold values from 0.5 to 1.5
- w_gate: bfloat16 [2048, 5632], P(('seq', 'ctx')), may hold values from -0.125 to 0.125
- w_up: bfloat16 [2048, 5632], P(('seq', 'ctx')), may hold values from -0.125 to 0.125
- w_down: bfloat16 [5632, 2048], P(('seq', 'ctx')), may hold values from -0.078125 to 0.078125
- cotangent: bfloat16 [4, 2048, 2048], P('seq', 'ctx'), may hold values from -6 to 6
- doc_lengths: int32 [4, 8], P('seq'), may hold values from 1 to 1024, 2048 in all within a row
- selected: int32 [4, 2048], P('seq', 'ctx'), may hold values 0 or 1
- block_order: int32 [16], replicated, may hold values from 0 to 15, each once
Outputs:
- output: bfloat16 [4, 2048, 2048], P('seq', 'ctx')
- grad_input: float32 [4, 2048, 2048], P('seq', 'ctx')
- grad_attn_gain: float32 [2048], P(('seq', 'ctx'))
- grad_w_query: float32 [2048, 2048], P(('seq', 'ctx'))
- grad_w_key: float32 [2048, 256], P(('seq', 'ctx'))
- grad_w_value: float32 [2048, 256], P(('seq', 'ctx'))
- grad_w_out: float32 [2048, 2048], P(('seq', 'ctx'))
- grad_ffn_gain: float32 [2048], P(('seq', 'ctx'))
- grad_w_gate: float32 [2048, 5632], P(('seq', 'ctx'))
- grad_w_up: float32 [2048, 5632], P(('seq', 'ctx'))
- grad_w_down: float32 [5632, 2048], P(('seq', 'ctx'))
Inputs may be any that keep to these rules, and one draw needn't show every extreme that they name: `doc_lengths`: each row holds 8 lengths that sum to 2048; the largest is exactly 1024. `block_order`: each number appears once.
All inputs are finite; a program needn't handle non-finite values. No bound on the sum of `selected` on one device may be relied on, other than what follows from the above.
Results may differ from a plain program's by a relative error of at most 0.014.
Values may be sent and summed in bfloat16 or wider, within the bound.
A program may use at most 384 MiB of HBM per device.

v0:
```python
import math

import jax
import jax.numpy as jnp
from jax import lax
from jax.sharding import PartitionSpec as P

HEADS = 32
KV_HEADS = 4
HEAD_DIM = 64


EPS = 1e-05
ROPE_BASE = 10000.0
NEG = -1e30


def rotate(values):
    half = values.shape[-1] // 2
    return jnp.concatenate([-values[..., half:], values[..., :half]], axis=-1)


def rope_tables(positions, head_size):
    half = head_size // 2
    inverse = ROPE_BASE ** (-(jnp.arange(half, dtype=jnp.float32) * 2.0 / head_size))
    angle = positions.astype(jnp.float32)[:, None] * inverse[None, :]
    cosine = jnp.concatenate([jnp.cos(angle), jnp.cos(angle)], axis=1)
    sine = jnp.concatenate([jnp.sin(angle), jnp.sin(angle)], axis=1)
    return (cosine, sine)


def score_part(queries, key_part, scale):
    return (
        jnp.einsum("rkgd,skd->kgrs", queries, key_part, preferred_element_type=jnp.float32) * scale
    )


def mix_part(prob_part, value_part):
    return jnp.einsum("kgrs,skd->rkgd", prob_part, value_part, preferred_element_type=jnp.float32)


def spread_part(grad_part, queries, scale):
    return (
        jnp.einsum("kgrs,rkgd->skd", grad_part, queries, preferred_element_type=jnp.float32) * scale
    )


def all_scores(queries, keys, key_block, scale):
    block_count = keys.shape[0] // key_block
    pieces = []
    for number in range(block_count):
        key_part = keys[number * key_block : (number + 1) * key_block]
        pieces.append(score_part(queries, key_part, scale))
    return jnp.concatenate(pieces, axis=-1)


def attend_forward(queries, keys, values, allowed, key_block):
    row_count, kv_count, group, head_size = queries.shape
    scale = 1.0 / math.sqrt(head_size)
    scores = all_scores(queries, keys, key_block, scale)
    scores = jnp.where(allowed[None, None], scores, NEG)
    top_score = jnp.max(scores, axis=-1, keepdims=True)
    expo = jnp.exp(scores - top_score)
    total = jnp.sum(expo, axis=-1, keepdims=True)
    p_low = (expo / total).astype(jnp.bfloat16)
    mixed = jnp.zeros((row_count, kv_count, group, head_size), jnp.float32)
    for number in range(keys.shape[0] // key_block):
        lower = number * key_block
        upper = lower + key_block
        mixed = mixed + mix_part(p_low[..., lower:upper], values[lower:upper])
    return (mixed, top_score, total)


def attend_backward(queries, keys, values, allowed, top_score, total, grad_mix, key_block):
    row_count, kv_count, group, head_size = queries.shape
    scale = 1.0 / math.sqrt(head_size)
    scores = all_scores(queries, keys, key_block, scale)
    scores = jnp.where(allowed[None, None], scores, NEG)
    probs = jnp.exp(scores - top_score) / total
    p_low = probs.astype(jnp.bfloat16)
    grad_probs = all_scores(grad_mix, values, key_block, 1.0)
    delta = jnp.sum(probs * grad_probs, axis=-1, keepdims=True)
    grad_scores = (probs * (grad_probs - delta)).astype(jnp.bfloat16)
    grad_q_rot = jnp.zeros((row_count, kv_count, group, head_size), jnp.float32)
    key_terms = []
    value_terms = []
    for number in range(keys.shape[0] // key_block):
        lower = number * key_block
        upper = lower + key_block
        grad_q_rot = grad_q_rot + mix_part(grad_scores[..., lower:upper], keys[lower:upper]) * scale
        key_terms.append(spread_part(grad_scores[..., lower:upper], queries, scale))
        value_terms.append(spread_part(p_low[..., lower:upper], grad_mix, 1.0))
    return (grad_q_rot, jnp.concatenate(key_terms, axis=0), jnp.concatenate(value_terms, axis=0))


def norm_back(grad_normed, source, rms_val, gain_val, normed):
    grad_gain = jnp.sum(grad_normed * normed, axis=0)
    scaled = grad_normed * gain_val
    grad_source = rms_val * scaled - source * (rms_val * rms_val * rms_val) * jnp.mean(
        scaled * source, axis=1, keepdims=True
    )
    return (grad_gain, grad_source)


def local(
    hidden_in,
    attn_gain,
    w_query,
    w_key,
    w_value,
    w_out,
    ffn_gain,
    w_gate,
    w_up,
    w_down,
    cotangent,
    doc_lengths,
    selected,
    block_order,
):
    seq_count, row_count, model_width = hidden_in.shape
    ctx_count = lax.axis_size("ctx")
    length = row_count * ctx_count
    span_len = length // block_order.shape[0]
    key_block = min(512, length)
    head_size = HEAD_DIM
    kv_count = KV_HEADS
    group = HEADS // KV_HEADS
    tok_count = seq_count * row_count
    positions = (
        block_order[:, None] * span_len + jnp.arange(span_len, dtype=jnp.int32)[None, :]
    ).reshape(length)
    local_pos = lax.dynamic_slice_in_dim(positions, lax.axis_index("ctx") * row_count, row_count)
    ends = jnp.cumsum(doc_lengths, axis=1)
    key_docs = jnp.sum((positions[None, :, None] >= ends[:, None, :]).astype(jnp.int32), axis=2)
    query_docs = jnp.sum((local_pos[None, :, None] >= ends[:, None, :]).astype(jnp.int32), axis=2)
    allowed = (positions[None, None, :] <= local_pos[None, :, None]) & (
        key_docs[:, None, :] == query_docs[:, :, None]
    )
    cosine, sine = rope_tables(local_pos, head_size)
    cos_q = cosine[None, :, None, None, :]
    sin_q = sine[None, :, None, None, :]
    cos_k = cosine[None, :, None, :]
    sin_k = sine[None, :, None, :]
    attn_params = (
        lax.all_gather(attn_gain, ("seq", "ctx"), axis=0, tiled=True),
        lax.all_gather(w_query, ("seq", "ctx"), axis=0, tiled=True),
        lax.all_gather(w_key, ("seq", "ctx"), axis=0, tiled=True),
        lax.all_gather(w_value, ("seq", "ctx"), axis=0, tiled=True),
        lax.all_gather(w_out, ("seq", "ctx"), axis=0, tiled=True),
    )
    gain_a, full_query, full_key, full_value, full_out = attn_params
    tokens_f = hidden_in.reshape(tok_count, model_width).astype(jnp.float32)
    rms_a = lax.rsqrt(jnp.mean(tokens_f * tokens_f, axis=1, keepdims=True) + EPS)
    normed_a = tokens_f * rms_a
    gain_af = gain_a.astype(jnp.float32)
    x_norm = (normed_a * gain_af).astype(jnp.bfloat16)
    queries = jnp.dot(x_norm, full_query, preferred_element_type=jnp.float32).reshape(
        seq_count, row_count, kv_count, group, head_size
    )
    q_rot = (queries * cos_q + rotate(queries) * sin_q).astype(jnp.bfloat16)
    keys = jnp.dot(x_norm, full_key, preferred_element_type=jnp.float32).reshape(
        seq_count, row_count, kv_count, head_size
    )
    k_rot = (
        (keys * cos_k + rotate(keys) * sin_k)
        .astype(jnp.bfloat16)
        .reshape(seq_count, row_count, kv_count * head_size)
    )
    v_low = (
        jnp.dot(x_norm, full_value, preferred_element_type=jnp.float32)
        .astype(jnp.bfloat16)
        .reshape(seq_count, row_count, kv_count * head_size)
    )
    keys_all, values_all = (
        lax.all_gather(k_rot, "ctx", axis=1, tiled=True),
        lax.all_gather(v_low, "ctx", axis=1, tiled=True),
    )
    keys_all = keys_all.reshape(seq_count, length, kv_count, head_size)
    values_all = values_all.reshape(seq_count, length, kv_count, head_size)

    def forward_one(items):
        return attend_forward(items[0], items[1], items[2], items[3], key_block)

    mixed, top_scores, totals = lax.map(forward_one, (q_rot, keys_all, values_all, allowed))
    attn_mix = mixed.reshape(tok_count, HEADS * head_size).astype(jnp.bfloat16)
    middle = tokens_f + jnp.dot(attn_mix, full_out, preferred_element_type=jnp.float32)
    rms_f = lax.rsqrt(jnp.mean(middle * middle, axis=1, keepdims=True) + EPS)
    normed_f = middle * rms_f
    ffn_params = (
        lax.all_gather(ffn_gain, ("seq", "ctx"), axis=0, tiled=True),
        lax.all_gather(w_gate, ("seq", "ctx"), axis=0, tiled=True),
        lax.all_gather(w_up, ("seq", "ctx"), axis=0, tiled=True),
        lax.all_gather(w_down, ("seq", "ctx"), axis=0, tiled=True),
    )
    gain_f, full_gate, full_up, full_down = ffn_params
    gain_ff = gain_f.astype(jnp.float32)
    f_norm = (normed_f * gain_ff).astype(jnp.bfloat16)
    gate = jnp.dot(f_norm, full_gate, preferred_element_type=jnp.float32)
    up_val = jnp.dot(f_norm, full_up, preferred_element_type=jnp.float32)
    sigma_gate = jax.nn.sigmoid(gate)
    activated = gate * sigma_gate
    hidden_act = (activated * up_val).astype(jnp.bfloat16)
    result = middle + jnp.dot(hidden_act, full_down, preferred_element_type=jnp.float32)
    output = result.astype(jnp.bfloat16).reshape(seq_count, row_count, model_width)
    grad_y = (
        cotangent.reshape(tok_count, model_width).astype(jnp.float32)
        * selected.reshape(tok_count).astype(jnp.float32)[:, None]
    )
    g_branch = grad_y.astype(jnp.bfloat16)
    back_ffn = (
        lax.all_gather(ffn_gain, ("seq", "ctx"), axis=0, tiled=True),
        lax.all_gather(w_gate, ("seq", "ctx"), axis=0, tiled=True),
        lax.all_gather(w_up, ("seq", "ctx"), axis=0, tiled=True),
        lax.all_gather(w_down, ("seq", "ctx"), axis=0, tiled=True),
    )
    gain_fb, gate_back, up_back, down_back = back_ffn
    grad_w_down = jnp.einsum("tf,td->fd", hidden_act, g_branch, preferred_element_type=jnp.float32)
    grad_hidden = jnp.einsum("td,fd->tf", g_branch, down_back, preferred_element_type=jnp.float32)
    grad_gate = (
        grad_hidden * up_val * (sigma_gate + gate * sigma_gate * (1.0 - sigma_gate))
    ).astype(jnp.bfloat16)
    grad_up = (grad_hidden * activated).astype(jnp.bfloat16)
    grad_w_gate = jnp.einsum("td,tf->df", f_norm, grad_gate, preferred_element_type=jnp.float32)
    grad_w_up = jnp.einsum("td,tf->df", f_norm, grad_up, preferred_element_type=jnp.float32)
    grad_f_norm = jnp.einsum(
        "tf,df->td", grad_gate, gate_back, preferred_element_type=jnp.float32
    ) + jnp.einsum("tf,df->td", grad_up, up_back, preferred_element_type=jnp.float32)
    grad_ffn_gain, grad_from_f = norm_back(
        grad_f_norm, middle, rms_f, gain_fb.astype(jnp.float32), normed_f
    )
    ffn_grads = (
        lax.psum_scatter(grad_ffn_gain, ("seq", "ctx"), scatter_dimension=0, tiled=True),
        lax.psum_scatter(grad_w_gate, ("seq", "ctx"), scatter_dimension=0, tiled=True),
        lax.psum_scatter(grad_w_up, ("seq", "ctx"), scatter_dimension=0, tiled=True),
        lax.psum_scatter(grad_w_down, ("seq", "ctx"), scatter_dimension=0, tiled=True),
    )
    grad_middle = grad_y + grad_from_f
    back_attn = (
        lax.all_gather(attn_gain, ("seq", "ctx"), axis=0, tiled=True),
        lax.all_gather(w_query, ("seq", "ctx"), axis=0, tiled=True),
        lax.all_gather(w_key, ("seq", "ctx"), axis=0, tiled=True),
        lax.all_gather(w_value, ("seq", "ctx"), axis=0, tiled=True),
        lax.all_gather(w_out, ("seq", "ctx"), axis=0, tiled=True),
    )
    gain_ab, query_back, key_back, value_back, out_back = back_attn
    g_attn = grad_middle.astype(jnp.bfloat16)
    grad_w_out = jnp.einsum("th,td->hd", attn_mix, g_attn, preferred_element_type=jnp.float32)
    grad_mix = jnp.einsum("td,hd->th", g_attn, out_back, preferred_element_type=jnp.float32).astype(
        jnp.bfloat16
    )
    grad_mix = grad_mix.reshape(seq_count, row_count, kv_count, group, head_size)

    def backward_one(items):
        return attend_backward(
            items[0], items[1], items[2], items[3], items[4], items[5], items[6], key_block
        )

    grad_q_rot, key_terms, value_terms = lax.map(
        backward_one, (q_rot, keys_all, values_all, allowed, top_scores, totals, grad_mix)
    )
    key_terms = key_terms.reshape(seq_count, length, kv_count * head_size)
    value_terms = value_terms.reshape(seq_count, length, kv_count * head_size)
    grad_k_rot, grad_v = (
        lax.psum_scatter(key_terms, "ctx", scatter_dimension=1, tiled=True),
        lax.psum_scatter(value_terms, "ctx", scatter_dimension=1, tiled=True),
    )
    grad_k_rot = grad_k_rot.reshape(seq_count, row_count, kv_count, head_size)
    grad_queries = (
        (grad_q_rot * cos_q - rotate(grad_q_rot * sin_q))
        .astype(jnp.bfloat16)
        .reshape(tok_count, HEADS * head_size)
    )
    grad_keys = (
        (grad_k_rot * cos_k - rotate(grad_k_rot * sin_k))
        .astype(jnp.bfloat16)
        .reshape(tok_count, kv_count * head_size)
    )
    grad_values = grad_v.astype(jnp.bfloat16).reshape(tok_count, kv_count * head_size)
    grad_w_query = jnp.einsum("td,th->dh", x_norm, grad_queries, preferred_element_type=jnp.float32)
    grad_w_key = jnp.einsum("td,th->dh", x_norm, grad_keys, preferred_element_type=jnp.float32)
    grad_w_value = jnp.einsum("td,th->dh", x_norm, grad_values, preferred_element_type=jnp.float32)
    grad_x_norm = (
        jnp.einsum("th,dh->td", grad_queries, query_back, preferred_element_type=jnp.float32)
        + jnp.einsum("th,dh->td", grad_keys, key_back, preferred_element_type=jnp.float32)
        + jnp.einsum("th,dh->td", grad_values, value_back, preferred_element_type=jnp.float32)
    )
    grad_attn_gain, grad_from_a = norm_back(
        grad_x_norm, tokens_f, rms_a, gain_ab.astype(jnp.float32), normed_a
    )
    grad_input = (grad_middle + grad_from_a).reshape(seq_count, row_count, model_width)
    attn_grads = (
        lax.psum_scatter(grad_attn_gain, ("seq", "ctx"), scatter_dimension=0, tiled=True),
        lax.psum_scatter(grad_w_query, ("seq", "ctx"), scatter_dimension=0, tiled=True),
        lax.psum_scatter(grad_w_key, ("seq", "ctx"), scatter_dimension=0, tiled=True),
        lax.psum_scatter(grad_w_value, ("seq", "ctx"), scatter_dimension=0, tiled=True),
        lax.psum_scatter(grad_w_out, ("seq", "ctx"), scatter_dimension=0, tiled=True),
    )
    return (
        output,
        grad_input,
        attn_grads[0],
        attn_grads[1],
        attn_grads[2],
        attn_grads[3],
        attn_grads[4],
        ffn_grads[0],
        ffn_grads[1],
        ffn_grads[2],
        ffn_grads[3],
    )


def solution(mesh):
    return jax.shard_map(
        local,
        mesh=mesh,
        in_specs=(
            P("seq", "ctx", None),
            P(("seq", "ctx")),
            P(("seq", "ctx"), None),
            P(("seq", "ctx"), None),
            P(("seq", "ctx"), None),
            P(("seq", "ctx"), None),
            P(("seq", "ctx")),
            P(("seq", "ctx"), None),
            P(("seq", "ctx"), None),
            P(("seq", "ctx"), None),
            P("seq", "ctx", None),
            P("seq", None),
            P("seq", "ctx"),
            P(),
        ),
        out_specs=(
            P("seq", "ctx", None),
            P("seq", "ctx", None),
            P(("seq", "ctx")),
            P(("seq", "ctx"), None),
            P(("seq", "ctx"), None),
            P(("seq", "ctx"), None),
            P(("seq", "ctx"), None),
            P(("seq", "ctx")),
            P(("seq", "ctx"), None),
            P(("seq", "ctx"), None),
            P(("seq", "ctx"), None),
        ),
        check_vma=False,
    )
```

profile of v0, /device:TPU:0, one launch (start us, length us, event | category | flops | bytes accessed | tf_op | source)
XLA Modules:
  0.0 3164.8 jit_solution(14818300779089221585)
XLA Ops:
  10.5 42.1 %all-reduce.5 = (bf16[2048]{0:T(1024)(128)(2,1)S(1)}, bf16[2048]{0:T(1024)(128)(2,1)S(1)}) all-reduce(bf16[2048]{0:T(1024)(128)(2,1)S(1)} %dynamic-update-slice, bf16[2048]{0:T(1024)(128)(2,1)S(1)} %dynamic-update-slice.1), channel_id=1, replica_groups=mesh['seq'=4,'ctx'=8] {'seq','ctx'}, use_global_device_ids=true, to_apply=%add | all-reduce | flops 4096 | bytes 16384
  54.7 12.9 all-gather.12.cloned.1.call-done
  71.4 51.9 %all-gather.14.cloned.1.call-done = bf16[2048,256]{1,0:T(8,128)(2,1)} async-done(((bf16[64,256]{1,0:T(8,128)(2,1)}), bf16[2048,256]{1,0:T(8,128)(2,1)}) %all-gather.14.cloned.1.call-update) | async-done | bytes 1048592 | tf_op jit(solution)/shard_map/all_gather | solution.py:148
  132.8 13.8 all-gather.26.cloned.1.call-done
  148.5 23.8 all-gather.28.cloned.1.call-done
  173.6 77.6 %all-gather.16.cloned.1.call-done = bf16[2048,2048]{1,0:T(8,128)(2,1)} async-done(((bf16[64,2048]{1,0:T(8,128)(2,1)}), bf16[2048,2048]{1,0:T(8,128)(2,1)}) %all-gather.16.cloned.1.call-update) | async-done | bytes 8388624 | tf_op jit(solution)/shard_map/all_gather | solution.py:147
  251.2 6.8 fusion.145
  258.7 8.2 multiply_bitcast_fusion
  266.9 8.2 multiply_bitcast_fusion.1
  275.2 8.6 multiply_bitcast_fusion.2
  283.8 8.2 multiply_bitcast_fusion.3
  292.0 47.6 %fusion.154 = (f32[4,8,256]{2,1,0:T(8,128)S(1)}, f32[4,8,256,2048]{2,3,1,0:T(8,128)}) fusion(f32[4,8,256,512]{2,3,1,0:T(8,128)} %multiply_bitcast_fusion, f32[4,8,256,512]{2,3,1,0:T(8,128)} %multiply_bitcast_fusion.1, f32[4,8,256,512]{2,3,1,0:T(8,128)} %multiply_bitcast_fusion.2, f32[4,8,256,512]{2,3,1,0:T(8,128)} %multiply_bitcast_fusion.3, ...), kind=kOutput, calls=%fused_computation.178 | output fusion | flops 100665344 | bytes 134774784 | tf_op jit(solution)/shard_map/while/body/eval_jaxpr/sub | solution.py:63
  339.6 33.2 %fusion.150 = bf16[4,8,256,2048]{2,3,1,0:T(8,128)(2,1)} fusion(f32[4,8,256,2048]{2,3,1,0:T(8,128)} %get-tuple-element.110, f32[4,8,256]{2,1,0:T(8,128)S(1)} %get-tuple-element.109), kind=kLoop, calls=%fused_computation.174 | loop fusion | flops 33554432 | bytes 100696064 | tf_op jit(solution)/shard_map/while/body/eval_jaxpr/convert_element_type | solution.py:65
  387.9 6.2 add_convert_fusion
  394.1 6.2 multiply_reduce_fusion.3
  400.5 75.5 %all-gather.22.cloned.1.call-done = bf16[2048,5632]{1,0:T(8,128)(2,1)} async-done(((bf16[64,5632]{1,0:T(8,128)(2,1)}), bf16[2048,5632]{1,0:T(8,128)(2,1)}) %all-gather.22.cloned.1.call-update) | async-done | bytes 23068688 | tf_op jit(solution)/shard_map/all_gather | solution.py:193
  476.0 13.2 fusion.156
  489.2 132.5 %all-gather.20.cloned.1.call-done = bf16[2048,5632]{1,0:T(8,128)(2,1)} async-done(((bf16[64,5632]{1,0:T(8,128)(2,1)}), bf16[2048,5632]{1,0:T(8,128)(2,1)}) %all-gather.20.cloned.1.call-update) | async-done | bytes 23068688 | tf_op jit(solution)/shard_map/all_gather | solution.py:192
  621.7 13.1 fusion.155
  634.8 132.6 %all-gather.24.cloned.1.call-done = bf16[5632,2048]{1,0:T(8,128)(2,1)} async-done(((bf16[176,2048]{1,0:T(8,128)(2,1)}), bf16[5632,2048]{1,0:T(8,128)(2,1)}) %all-gather.24.cloned.1.call-update) | async-done | bytes 23068688 | tf_op jit(solution)/shard_map/all_gather | solution.py:194
  767.4 18.6 multiply_convert_fusion.1
  786.0 12.6 fusion.157
  798.5 13.9 multiply_reduce_fusion.1
  840.6 6.1 fusion.70
  846.7 8.1 convolution_bitcast_fusion
  854.8 8.1 convolution_bitcast_fusion.1
  862.9 8.2 convolution_bitcast_fusion.2
  871.2 8.7 convolution_bitcast_fusion.3
  881.4 94.2 %multiply_convert_fusion = bf16[4,8,256,2048]{2,3,1,0:T(8,128)(2,1)} fusion(f32[4,8,256,512]{2,3,1,0:T(8,128)} %convolution_bitcast_fusion, f32[4,8,256,512]{2,3,1,0:T(8,128)} %convolution_bitcast_fusion.1, f32[4,8,256,512]{2,3,1,0:T(8,128)} %convolution_bitcast_fusion.2, f32[4,8,256,512]{2,3,1,0:T(8,128)} %convolution_bitcast_fusion.3, ...), kind=kOutput, calls=%fused_computation.4 | output fusion | flops 201336832 | bytes 167804928 | tf_op jit(solution)/shard_map/while/body/eval_jaxpr/sub | solution.py:83
  975.6 6.0 fusion.115
  981.6 6.0 fusion.109
  987.7 6.0 fusion.103
  993.7 6.0 fusion.97
  1004.4 31.0 reduce-scatter.10.cloned.1.call-done
  1040.2 9.4 fusion.121
  1072.8 8.4 fusion.143
  1081.8 20.0 fusion.124
  1101.9 19.6 fusion.160
  1121.8 19.6 fusion.159
  1141.5 6.3 fusion.158
  1147.8 12.3 fusion.49
  1163.7 38.3 %all-reduce.4 = (f32[2048]{0:T(1024)S(1)}, f32[2048]{0:T(1024)S(1)}) all-reduce(f32[2048]{0:T(1024)S(1)} %get-tuple-element.59, f32[2048]{0:T(1024)S(1)} %copy-done.43), channel_id=6, replica_groups=mesh['seq'=4,'ctx'=8] {'seq','ctx'}, use_global_device_ids=true, to_apply=%region_13.14.clone | all-reduce | flops 4096 | bytes 32768
  1206.6 103.4 %reduce-scatter.16.cloned.1.call-done = f32[64,256]{1,0:T(8,128)} async-done(((f32[2048,256]{1,0:T(8,128)}), f32[64,256]{1,0:T(8,128)}) %reduce-scatter.16.cloned.1.call-update) | async-done | bytes 65552 | tf_op jit(solution)/shard_map/reduce_scatter | solution.py:295
  1310.0 185.9 %reduce-scatter.20.cloned.1.call-done = f32[64,2048]{1,0:T(8,128)} async-done(((f32[2048,2048]{1,0:T(8,128)}), f32[64,2048]{1,0:T(8,128)}) %reduce-scatter.20.cloned.1.call-update) | async-done | bytes 524304 | tf_op jit(solution)/shard_map/reduce_scatter | solution.py:297
  1495.9 187.1 %reduce-scatter.14.cloned.1.call-done = f32[64,2048]{1,0:T(8,128)} async-done(((f32[2048,2048]{1,0:T(8,128)}), f32[64,2048]{1,0:T(8,128)}) %reduce-scatter.14.cloned.1.call-update) | async-done | bytes 524304 | tf_op jit(solution)/shard_map/reduce_scatter | solution.py:294
  1683.0 492.4 %reduce-scatter.26.cloned.1.call-done = f32[176,2048]{1,0:T(8,128)} async-done(((f32[5632,2048]{1,0:T(8,128)}), f32[176,2048]{1,0:T(8,128)}) %reduce-scatter.26.cloned.1.call-update) | async-done | bytes 1441808 | tf_op jit(solution)/shard_map/reduce_scatter | solution.py:236
  2175.3 491.2 %reduce-scatter.24.cloned.1.call-done = f32[64,5632]{1,0:T(8,128)} async-done(((f32[2048,5632]{1,0:T(8,128)}), f32[64,5632]{1,0:T(8,128)}) %reduce-scatter.24.cloned.1.call-update) | async-done | bytes 1441808 | tf_op jit(solution)/shard_map/reduce_scatter | solution.py:235
  2666.5 491.2 %reduce-scatter.22.cloned.1.call-done = f32[64,5632]{1,0:T(8,128)} async-done(((f32[2048,5632]{1,0:T(8,128)}), f32[64,5632]{1,0:T(8,128)}) %reduce-scatter.22.cloned.1.call-update) | async-done | bytes 1441808 | tf_op jit(solution)/shard_map/reduce_scatter | solution.py:234
  (200 shorter events, 108.7 us)
Async XLA Ops:
  7.2 116.2 %copy-start = (bf16[1,256,2048]{2,1,0:T(8,128)(2,1)S(1)}, bf16[1,256,2048]{2,1,0:T(8,128)(2,1)}, u32[]{:S(2)}) copy-start(bf16[1,256,2048]{2,1,0:T(8,128)(2,1)} %param.14) | copy-start | bytes 3145732
  7.2 63.2 %copy-start.46 = (s32[16]{0:T(128)S(1)}, s32[16]{0:T(128)}, u32[]{:S(2)}) copy-start(s32[16]{0:T(128)} %param.27) | copy-start | bytes 196
  7.2 60.4 %all-gather.12.cloned.1.call-start = ((), (), s32[]{:S(2)}) async-start(), calls=%async_computation.9 | async-start | bytes 1081344 | tf_op jit(solution)/shard_map/all_gather | solution.py:149
  7.9 115.4 %all-gather.14.cloned.1.call-start = ((), (), s32[]{:S(2)}) async-start(), calls=%async_computation.10 | async-start | bytes 1081344 | tf_op jit(solution)/shard_map/all_gather | solution.py:148
  8.7 138.0 %all-gather.26.cloned.1.call-start = ((), (), s32[]{:S(2)}) async-start(), calls=%async_computation.25 | async-start | bytes 1179648 | tf_op jit(solution)/shard_map/all_gather | solution.py:177
  52.6 198.6 %copy-start.35 = (f32[2048]{0:T(1024)}, f32[2048]{0:T(1024)S(1)}, u32[]{:S(2)}) copy-start(f32[2048]{0:T(1024)S(1)} %convert_element_type.163) | copy-start | bytes 24580
  54.7 196.5 %copy-start.39 = (f32[256]{0:T(256)}, f32[256]{0:T(256)S(1)}, u32[]{:S(2)}) copy-start(f32[256]{0:T(256)S(1)} %get-tuple-element.106) | copy-start | bytes 3076
  70.3 102.0 %all-gather.28.cloned.1.call-start = ((), (), s32[]{:S(2)}) async-start(), calls=%async_computation.26 | async-start | bytes 1179648 | tf_op jit(solution)/shard_map/all_gather | solution.py:176
  71.4 186.8 %copy-start.26 = (f32[256,64]{0,1:T(8,128)}, f32[256,64]{0,1:T(8,128)S(1)}, u32[]{:S(2)}) copy-start(f32[256,64]{0,1:T(8,128)S(1)} %get-tuple-element.115) | copy-start | bytes 196612
  71.4 186.8 %copy-start.28 = (f32[256,64]{0,1:T(8,128)}, f32[256,64]{0,1:T(8,128)S(1)}, u32[]{:S(2)}) copy-start(f32[256,64]{0,1:T(8,128)S(1)} %get-tuple-element.102) | copy-start | bytes 196612
  126.0 125.1 %all-gather.16.cloned.1.call-start = ((), (), s32[]{:S(2)}) async-start(), calls=%async_computation.11 | async-start | bytes 8650752 | tf_op jit(solution)/shard_map/all_gather | solution.py:147
  126.6 267.5 %all-gather.18.cloned.1.call-start = ((), (), s32[]{:S(2)}) async-start(), calls=%async_computation.12 | async-start | bytes 8650752 | tf_op jit(solution)/shard_map/all_gather | solution.py:150
  127.2 348.8 %all-gather.22.cloned.1.call-start = ((), (), s32[]{:S(2)}) async-start(), calls=%async_computation.14 | async-start | bytes 23789568 | tf_op jit(solution)/shard_map/all_gather | solution.py:193
  128.0 493.7 %all-gather.20.cloned.1.call-start = ((), (), s32[]{:S(2)}) async-start(), calls=%async_computation.13 | async-start | bytes 23789568 | tf_op jit(solution)/shard_map/all_gather | solution.py:192
  128.7 638.7 %all-gather.24.cloned.1.call-start = ((), (), s32[]{:S(2)}) async-start(), calls=%async_computation.15 | async-start | bytes 23789568 | tf_op jit(solution)/shard_map/all_gather | solution.py:194
  129.4 871.9 %reduce-scatter.12.cloned.1.call-start = ((), (), s32[]{:S(2)}) async-start(), calls=%async_computation.17 | async-start | bytes 2359296 | tf_op jit(solution)/shard_map/reduce_scatter | solution.py:266
  148.2 224.7 %copy-start.14 = (bf16[1,512,256]{1,2,0:T(8,128)(2,1)}, bf16[1,512,256]{1,2,0:T(8,128)(2,1)S(1)}, u32[]{:S(2)}) copy-start(bf16[1,512,256]{1,2,0:T(8,128)(2,1)S(1)} %copy.114) | copy-start | bytes 786436
  148.4 229.5 %copy-start.16 = (bf16[1,512,256]{1,2,0:T(8,128)(2,1)}, bf16[1,512,256]{1,2,0:T(8,128)(2,1)S(1)}, u32[]{:S(2)}) copy-start(bf16[1,512,256]{1,2,0:T(8,128)(2,1)S(1)} %copy.112) | copy-start | bytes 786436
  148.5 234.3 %copy-start.18 = (bf16[1,512,256]{1,2,0:T(8,128)(2,1)}, bf16[1,512,256]{1,2,0:T(8,128)(2,1)S(1)}, u32[]{:S(2)}) copy-start(bf16[1,512,256]{1,2,0:T(8,128)(2,1)S(1)} %copy.110) | copy-start | bytes 786436
  173.6 85.1 %copy-start.24 = (bf16[1,512,256]{1,2,0:T(8,128)(2,1)}, bf16[1,512,256]{1,2,0:T(8,128)(2,1)S(1)}, u32[]{:S(2)}) copy-start(bf16[1,512,256]{1,2,0:T(8,128)(2,1)S(1)} %get-tuple-element.90) | copy-start | bytes 786436
  173.6 93.4 %copy-start.22 = (bf16[1,512,256]{1,2,0:T(8,128)(2,1)}, bf16[1,512,256]{1,2,0:T(8,128)(2,1)S(1)}, u32[]{:S(2)}) copy-start(bf16[1,512,256]{1,2,0:T(8,128)(2,1)S(1)} %get-tuple-element.91) | copy-start | bytes 786436
  173.6 101.6 %copy-start.20 = (bf16[1,512,256]{1,2,0:T(8,128)(2,1)}, bf16[1,512,256]{1,2,0:T(8,128)(2,1)S(1)}, u32[]{:S(2)}) copy-start(bf16[1,512,256]{1,2,0:T(8,128)(2,1)S(1)} %get-tuple-element.92) | copy-start | bytes 786436
  173.6 110.2 %copy-start.12 = (bf16[1,512,256]{1,2,0:T(8,128)(2,1)}, bf16[1,512,256]{1,2,0:T(8,128)(2,1)S(1)}, u32[]{:S(2)}) copy-start(bf16[1,512,256]{1,2,0:T(8,128)(2,1)S(1)} %get-tuple-element.89) | copy-start | bytes 786436
  258.7 25.1 copy-start.2
  283.8 8.2 copy-start.34
  400.3 412.2 %copy-start.6 = (f32[256,2048]{1,0:T(8,128)}, f32[256,2048]{1,0:T(8,128)S(1)}, u32[]{:S(2)}) copy-start(f32[256,2048]{1,0:T(8,128)S(1)} %get-tuple-element.112) | copy-start | bytes 6291460
  400.5 221.2 %copy-start.8 = (bf16[256,2048]{1,0:T(8,128)(2,1)}, bf16[256,2048]{1,0:T(8,128)(2,1)S(1)}, u32[]{:S(2)}) copy-start(bf16[256,2048]{1,0:T(8,128)(2,1)S(1)} %multiply_convert_fusion.4) | copy-start | bytes 3145732
  489.2 278.2 %copy-start.41 = (f32[1,256]{1,0:T(1,128)S(1)}, f32[1,256]{1,0:T(1,128)}, u32[]{:S(2)}) copy-start(f32[1,256]{1,0:T(1,128)} %convert_element_type.182) | copy-start | bytes 3076
  798.5 13.9 copy-start.10
  846.7 8.1 copy-start.17
  854.8 8.1 copy-start.19
  881.4 154.0 %reduce-scatter.10.cloned.1.call-start = ((), (), s32[]{:S(2)}) async-start(), calls=%async_computation.16 | async-start | bytes 2359296 | tf_op jit(solution)/shard_map/reduce_scatter | solution.py:265
  881.4 94.2 %copy-start.3 = (bf16[256,4,8,64]{0,3,2,1:T(8,128)(2,1)S(1)}, bf16[256,4,8,64]{0,3,2,1:T(8,128)(2,1)}, u32[]{:S(2)}) copy-start(bf16[256,4,8,64]{0,3,2,1:T(8,128)(2,1)} %copy-done.2) | copy-start | bytes 3145732
  1001.3 34.2 %copy-start.29 = (f32[256,64]{0,1:T(8,128)S(1)}, f32[256,64]{0,1:T(8,128)}, u32[]{:S(2)}) copy-start(f32[256,64]{0,1:T(8,128)} %copy-done.28) | copy-start | bytes 196612
  1001.3 35.2 %copy-start.27 = (f32[256,64]{0,1:T(8,128)S(1)}, f32[256,64]{0,1:T(8,128)}, u32[]{:S(2)}) copy-start(f32[256,64]{0,1:T(8,128)} %copy-done.26) | copy-start | bytes 196612
  1001.3 205.3 %reduce-scatter.18.cloned.1.call-start = ((), (), s32[]{:S(2)}) async-start(), calls=%async_computation.20 | async-start | bytes 2162688 | tf_op jit(solution)/shard_map/reduce_scatter | solution.py:296
  1004.3 305.6 %reduce-scatter.16.cloned.1.call-start = ((), (), s32[]{:S(2)}) async-start(), calls=%async_computation.19 | async-start | bytes 2162688 | tf_op jit(solution)/shard_map/reduce_scatter | solution.py:295
  1040.1 455.8 %reduce-scatter.20.cloned.1.call-start = ((), (), s32[]{:S(2)}) async-start(), calls=%async_computation.21 | async-start | bytes 17301504 | tf_op jit(solution)/shard_map/reduce_scatter | solution.py:297
  1049.6 633.3 %reduce-scatter.14.cloned.1.call-start = ((), (), s32[]{:S(2)}) async-start(), calls=%async_computation.18 | async-start | bytes 17301504 | tf_op jit(solution)/shard_map/reduce_scatter | solution.py:294
  1081.2 1094.1 %reduce-scatter.26.cloned.1.call-start = ((), (), s32[]{:S(2)}) async-start(), calls=%async_computation.24 | async-start | bytes 47579136 | tf_op jit(solution)/shard_map/reduce_scatter | solution.py:236
  1101.9 1564.7 %reduce-scatter.24.cloned.1.call-start = ((), (), s32[]{:S(2)}) async-start(), calls=%async_computation.23 | async-start | bytes 47579136 | tf_op jit(solution)/shard_map/reduce_scatter | solution.py:235
  1121.5 2036.2 %reduce-scatter.22.cloned.1.call-start = ((), (), s32[]{:S(2)}) async-start(), calls=%async_computation.22 | async-start | bytes 47579136 | tf_op jit(solution)/shard_map/reduce_scatter | solution.py:234
  1141.5 6.3 copy-start.7
  1141.5 6.3 copy-start.9
  1147.8 12.3 copy-start.25
  1147.8 12.3 copy-start.33
  1147.8 12.4 copy-start.32
  1161.4 41.7 %copy-start.44 = (f32[256]{0:T(256)S(1)}, f32[256]{0:T(256)}, u32[]{:S(2)}) copy-start(f32[256]{0:T(256)} %get-tuple-element.105) | copy-start | bytes 3076
  (18 other events, 50.6 us)
Sparse Core Ops, SparseCore 0:
  11.0 56.4 all-gather.11
  70.6 52.7 all-gather.13
  125.5 21.0 all-gather.25
  148.7 23.5 all-gather.27
  175.1 75.9 all-gather.15
  254.0 75.8 all-gather.17
  332.8 143.2 all-gather.21
  478.9 142.7 all-gather.19
  624.6 142.7 all-gather.23
  881.5 33.9 reduce-scatter.11
  1001.4 33.9 reduce-scatter.9
  1038.1 135.4 reduce-scatter.17
  1176.6 133.3 reduce-scatter.15
  1312.7 183.1 reduce-scatter.19
  1498.6 184.3 reduce-scatter.13
  1685.7 489.5 reduce-scatter.25
  2178.1 488.4 reduce-scatter.23
  2669.3 488.4 reduce-scatter.21
where the time goes:
time: 3170 us; the launch traced here: 3160 us
  waiting for transfers between devices  2510 us (79%)
  matrix products  354 us (11%)
  other arithmetic  196 us (6%)
  blocking collectives  80.4 us (3%)
    reduce_scatter x1, waiting for transfers between devices, local(): lax.psum_scatter(grad_w_down, ('seq', 'ctx'), scatter_dimension=0, tiled=...  492 us
    reduce_scatter x1, waiting for transfers between devices, local(): lax.psum_scatter(grad_w_gate, ('seq', 'ctx'), scatter_dimension=0, tiled=...  491 us
    reduce_scatter x1, waiting for transfers between devices, local(): lax.psum_scatter(grad_w_up, ('seq', 'ctx'), scatter_dimension=0, tiled=True)  491 us
    reduce_scatter x1, waiting for transfers between devices, local(): lax.psum_scatter(grad_w_query, ('seq', 'ctx'), scatter_dimension=0, tiled...  187 us
    reduce_scatter x1, waiting for transfers between devices, local(): lax.psum_scatter(grad_w_out, ('seq', 'ctx'), scatter_dimension=0, tiled=T...  186 us
    all_gather x1, waiting for transfers between devices, local(): lax.all_gather(w_down, ('seq', 'ctx'), axis=0, tiled=True)  133 us
    all_gather x1, waiting for transfers between devices, local(): lax.all_gather(w_gate, ('seq', 'ctx'), axis=0, tiled=True)  133 us
    reduce_scatter x1, waiting for transfers between devices, local(): lax.psum_scatter(grad_w_key, ('seq', 'ctx'), scatter_dimension=0, tiled=T...  103 us
  transfers between devices with their start and end apart: 18, of which 15 were waited for; matrix products, arithmetic and copies ran while one was open for 14% of the time, Pallas kernels for 0%

commit v1 on v0

v1 whole, which is shorter than its diff:
```python
import functools
import math

import jax
import jax.numpy as jnp
from jax import lax
from jax.experimental import pallas as pl
from jax.experimental.pallas import tpu as pltpu
from jax.sharding import PartitionSpec as P

HEADS = 32
KV_HEADS = 4
HEAD_DIM = 64
GROUP = HEADS // KV_HEADS
SCALE = 1.0 / math.sqrt(HEAD_DIM)
LOG2E = math.log2(math.e)


EPS = 1e-05
ROPE_BASE = 10000.0
NEG = -1e30

F32 = jnp.float32
BF16 = jnp.bfloat16
VMEM_MOST = 56 * 1024 * 1024


def dot32(left, right, dims):
    return lax.dot_general(left, right, (dims, ((), ())), preferred_element_type=F32)


def span_bounds(order_ref, lens_ref, span_len, spans, own_first, own):
    docs = lens_ref.shape[1]
    base = order_ref[own_first + own] * span_len
    pos = lax.broadcasted_iota(jnp.int32, (1, span_len), 1) + base
    start = jnp.zeros((1, span_len), jnp.int32)
    first_start = jnp.int32(0)
    end = jnp.int32(0)
    for number in range(docs):
        end = end + lens_ref[0, number]
        start = jnp.where(pos >= end, end, start)
        first_start = jnp.where(base >= end, end, first_start)
    return base, pos, start, first_start


def allowed_tile(key_base, span_len, pos, start):
    key_pos = lax.broadcasted_iota(jnp.int32, (span_len, span_len), 0) + key_base
    tile = (key_pos <= pos) & (key_pos >= start)
    return jnp.concatenate([tile.astype(F32)] * GROUP, axis=1) > 0.5


def stack_heads(ref, head, own, span_len):
    pieces = []
    for member in range(GROUP):
        row = (head * GROUP + member) * HEAD_DIM
        pieces.append(ref[row : row + HEAD_DIM, own * span_len : (own + 1) * span_len])
    return jnp.concatenate(pieces, axis=1)


def unstack_heads(ref, value, head, own, span_len):
    for member in range(GROUP):
        row = (head * GROUP + member) * HEAD_DIM
        ref[row : row + HEAD_DIM, own * span_len : (own + 1) * span_len] = value[
            :, member * span_len : (member + 1) * span_len
        ].astype(ref.dtype)


def attend_forward_kernel(
    span_len, spans, place_ref, order_ref, lens_ref, q_ref, kv_ref, o_ref, lse_ref, top_ref, sum_ref, acc_ref
):
    own_count = q_ref.shape[1] // span_len
    own_first = place_ref[0] * own_count
    width = KV_HEADS * HEAD_DIM
    for own in range(own_count):
        base, pos, start, first_start = span_bounds(
            order_ref, lens_ref, span_len, spans, own_first, own
        )
        top_ref[...] = jnp.full(top_ref.shape, NEG, F32)
        sum_ref[...] = jnp.zeros(sum_ref.shape, F32)
        acc_ref[...] = jnp.zeros(acc_ref.shape, F32)
        stacked = [stack_heads(q_ref, head, own, span_len) for head in range(KV_HEADS)]

        @pl.loop(0, spans)
        def _(number):
            key_base = order_ref[number] * span_len

            @pl.when((key_base <= base) & (key_base + span_len > first_start))
            def _():
                allowed = allowed_tile(key_base, span_len, pos, start)
                rows = pl.ds(pl.multiple_of(number * span_len, span_len), span_len)
                for head in range(KV_HEADS):
                    lower = head * HEAD_DIM
                    key = kv_ref[rows, lower : lower + HEAD_DIM]
                    value = kv_ref[rows, width + lower : width + lower + HEAD_DIM]
                    scores = dot32(key, stacked[head], ((1,), (0,))) * (SCALE * LOG2E)
                    scores = jnp.where(allowed, scores, NEG)
                    old = top_ref[head : head + 1, :]
                    new = jnp.maximum(old, jnp.max(scores, axis=0, keepdims=True))
                    decay = jnp.exp2(old - new)
                    expo = jnp.exp2(scores - new)
                    top_ref[head : head + 1, :] = new
                    sum_ref[head : head + 1, :] = sum_ref[head : head + 1, :] * decay + jnp.sum(
                        expo, axis=0, keepdims=True
                    )
                    part = dot32(value, expo.astype(BF16), ((0,), (0,)))
                    acc_ref[head] = acc_ref[head] * decay + part

        for head in range(KV_HEADS):
            total = sum_ref[head : head + 1, :]
            mixed = acc_ref[head] / total
            unstack_heads(o_ref, mixed, head, own, span_len)
            lse_ref[own, head : head + 1, :] = top_ref[head : head + 1, :] + jnp.log2(total)


def attend_backward_kernel(
    span_len,
    spans,
    place_ref,
    order_ref,
    lens_ref,
    q_ref,
    kv_ref,
    o_ref,
    lse_ref,
    do_ref,
    dq_ref,
    dkv_ref,
    dkv_acc,
    dq_acc,
    delta_ref,
):
    own_count = q_ref.shape[1] // span_len
    own_first = place_ref[0] * own_count
    width = KV_HEADS * HEAD_DIM
    dkv_acc[...] = jnp.zeros(dkv_acc.shape, F32)
    for own in range(own_count):
        base, pos, start, first_start = span_bounds(
            order_ref, lens_ref, span_len, spans, own_first, own
        )
        dq_acc[...] = jnp.zeros(dq_acc.shape, F32)
        queries = [stack_heads(q_ref, head, own, span_len) for head in range(KV_HEADS)]
        grads = [stack_heads(do_ref, head, own, span_len) for head in range(KV_HEADS)]
        for head in range(KV_HEADS):
            mixed = stack_heads(o_ref, head, own, span_len)
            delta_ref[head : head + 1, :] = jnp.sum(
                mixed.astype(F32) * grads[head].astype(F32), axis=0, keepdims=True
            )

        @pl.loop(0, spans)
        def _(number):
            key_base = order_ref[number] * span_len

            @pl.when((key_base <= base) & (key_base + span_len > first_start))
            def _():
                allowed = allowed_tile(key_base, span_len, pos, start)
                rows = pl.ds(pl.multiple_of(number * span_len, span_len), span_len)
                for head in range(KV_HEADS):
                    lower = head * HEAD_DIM
                    key = kv_ref[rows, lower : lower + HEAD_DIM]
                    value = kv_ref[rows, width + lower : width + lower + HEAD_DIM]
                    scores = dot32(key, queries[head], ((1,), (0,))) * (SCALE * LOG2E)
                    probs = jnp.where(
                        allowed, jnp.exp2(scores - lse_ref[own, head : head + 1, :]), 0.0
                    )
                    grad_probs = dot32(value, grads[head], ((1,), (0,)))
                    grad_scores = (probs * (grad_probs - delta_ref[head : head + 1, :])).astype(BF16)
                    probs = probs.astype(BF16)
                    dq_acc[head] = dq_acc[head] + dot32(key, grad_scores, ((0,), (0,)))
                    dkv_acc[rows, lower : lower + HEAD_DIM] = (
                        dkv_acc[rows, lower : lower + HEAD_DIM]
                        + dot32(grad_scores, queries[head], ((1,), (1,))) * SCALE
                    )
                    dkv_acc[rows, width + lower : width + lower + HEAD_DIM] = dkv_acc[
                        rows, width + lower : width + lower + HEAD_DIM
                    ] + dot32(probs, grads[head], ((1,), (1,)))

        for head in range(KV_HEADS):
            unstack_heads(dq_ref, dq_acc[head] * SCALE, head, own, span_len)
    dkv_ref[...] = dkv_acc[...].astype(dkv_ref.dtype)


def smem():
    return pl.BlockSpec(memory_space=pltpu.SMEM)


def vmem():
    return pl.BlockSpec(memory_space=pltpu.VMEM)


def attend_forward(place, block_order, doc_lengths, q_t, kv):
    spans = block_order.shape[0]
    span_len = kv.shape[0] // spans
    own_count = q_t.shape[1] // span_len
    lanes = GROUP * span_len
    return pl.pallas_call(
        functools.partial(attend_forward_kernel, span_len, spans),
        out_shape=(
            jax.ShapeDtypeStruct(q_t.shape, BF16),
            jax.ShapeDtypeStruct((own_count, KV_HEADS, lanes), F32),
        ),
        in_specs=[smem(), smem(), smem(), vmem(), vmem()],
        out_specs=(vmem(), vmem()),
        scratch_shapes=[
            pltpu.VMEM((KV_HEADS, lanes), F32),
            pltpu.VMEM((KV_HEADS, lanes), F32),
            pltpu.VMEM((KV_HEADS, HEAD_DIM, lanes), F32),
        ],
        compiler_params=pltpu.CompilerParams(vmem_limit_bytes=VMEM_MOST),
        cost_estimate=pl.CostEstimate(
            flops=2 * HEADS * HEAD_DIM * kv.shape[0] * q_t.shape[1],
            transcendentals=HEADS * kv.shape[0] * q_t.shape[1] // 2,
            bytes_accessed=4 * q_t.size + 2 * kv.size,
        ),
        name="attend_forward",
    )(place, block_order, doc_lengths, q_t, kv)


def attend_backward(place, block_order, doc_lengths, q_t, kv, o_t, lse, do_t):
    spans = block_order.shape[0]
    span_len = kv.shape[0] // spans
    lanes = GROUP * span_len
    return pl.pallas_call(
        functools.partial(attend_backward_kernel, span_len, spans),
        out_shape=(
            jax.ShapeDtypeStruct(q_t.shape, F32),
            jax.ShapeDtypeStruct(kv.shape, BF16),
        ),
        in_specs=[smem(), smem(), smem(), vmem(), vmem(), vmem(), vmem(), vmem()],
        out_specs=(vmem(), vmem()),
        scratch_shapes=[
            pltpu.VMEM(kv.shape, F32),
            pltpu.VMEM((KV_HEADS, HEAD_DIM, lanes), F32),
            pltpu.VMEM((KV_HEADS, lanes), F32),
        ],
        compiler_params=pltpu.CompilerParams(vmem_limit_bytes=VMEM_MOST),
        cost_estimate=pl.CostEstimate(
            flops=5 * HEADS * HEAD_DIM * kv.shape[0] * q_t.shape[1],
            transcendentals=HEADS * kv.shape[0] * q_t.shape[1] // 2,
            bytes_accessed=10 * q_t.size + 4 * kv.size,
        ),
        name="attend_backward",
    )(place, block_order, doc_lengths, q_t, kv, o_t, lse, do_t)


EVERY = ("seq", "ctx")


def gather(value, axes, dim=0):
    return lax.all_gather(value, axes, axis=dim, tiled=True)


def scatter_sum(value, axes, dim=0):
    return lax.psum_scatter(value, axes, scatter_dimension=dim, tiled=True)


def rotate_t(value):
    half = HEAD_DIM // 2
    heads = value.reshape(-1, HEAD_DIM, value.shape[1])
    return jnp.concatenate([-heads[:, half:], heads[:, :half]], axis=1)


def rope_t(value, cosine, sine):
    heads = value.reshape(-1, HEAD_DIM, value.shape[1])
    return (heads * cosine[None] + rotate_t(value) * sine[None]).reshape(value.shape)


def rope_back_t(value, cosine, sine):
    heads = value.reshape(-1, HEAD_DIM, value.shape[1])
    turned = rotate_t((heads * sine[None]).reshape(value.shape))
    return (heads * cosine[None] - turned).reshape(value.shape)


def norm_back(grad_normed, source, rms_val, gain_val, normed):
    grad_gain = jnp.sum(grad_normed * normed, axis=0)
    scaled = grad_normed * gain_val
    grad_source = rms_val * scaled - source * (rms_val * rms_val * rms_val) * jnp.mean(
        scaled * source, axis=1, keepdims=True
    )
    return (grad_gain, grad_source)


def local(
    hidden_in,
    attn_gain,
    w_query,
    w_key,
    w_value,
    w_out,
    ffn_gain,
    w_gate,
    w_up,
    w_down,
    cotangent,
    doc_lengths,
    selected,
    block_order,
):
    one, rows, model = hidden_in.shape
    seq_count = lax.axis_size("seq")
    ctx_count = lax.axis_size("ctx")
    place = lax.axis_index("ctx").astype(jnp.int32).reshape(1)
    length = rows * ctx_count
    span_len = length // block_order.shape[0]
    q_width = HEADS * HEAD_DIM
    kv_width = KV_HEADS * HEAD_DIM
    own_rows = w_gate.shape[0]
    ff_part = w_gate.shape[1] // seq_count

    def ffn_columns(weight):
        split = weight.reshape(own_rows, seq_count, ff_part).transpose(1, 0, 2)
        mine = lax.all_to_all(split, "seq", 0, 0, tiled=True)
        return gather(mine, "ctx", 1).reshape(model, ff_part)

    own_spans = lax.dynamic_slice_in_dim(block_order, place[0] * (rows // span_len), rows // span_len)
    local_pos = (
        own_spans[:, None] * span_len + jnp.arange(span_len, dtype=jnp.int32)[None, :]
    ).reshape(rows)
    half = HEAD_DIM // 2
    inverse = ROPE_BASE ** (-(jnp.arange(half, dtype=F32) * 2.0 / HEAD_DIM))
    angle = inverse[:, None] * local_pos.astype(F32)[None, :]
    cosine = jnp.concatenate([jnp.cos(angle)] * 2, axis=0)
    sine = jnp.concatenate([jnp.sin(angle)] * 2, axis=0)

    gains = gather(jnp.stack([attn_gain, ffn_gain])[None], EVERY)
    gain_a = gains[:, 0].reshape(model).astype(F32)
    gain_f = gains[:, 1].reshape(model).astype(F32)
    w_qkv = gather(jnp.concatenate([w_query, w_key, w_value], axis=1), EVERY)
    full_out = gather(w_out, EVERY)
    full_gate = ffn_columns(w_gate)
    full_up = ffn_columns(w_up)
    full_down = gather(w_down, "ctx")

    tokens = hidden_in.reshape(rows, model).astype(F32)
    rms_a = lax.rsqrt(jnp.mean(tokens * tokens, axis=1, keepdims=True) + EPS)
    normed_a = tokens * rms_a
    x_norm = (normed_a * gain_a).astype(BF16)
    qkv_t = jnp.einsum("td,dh->ht", x_norm, w_qkv, preferred_element_type=F32)
    q_t = rope_t(qkv_t[:q_width], cosine, sine).astype(BF16)
    k_t = rope_t(qkv_t[q_width : q_width + kv_width], cosine, sine).astype(BF16)
    v_t = qkv_t[q_width + kv_width :].astype(BF16)
    kv = gather(jnp.concatenate([k_t, v_t], axis=0).T, "ctx")
    o_t, lse = attend_forward(place, block_order, doc_lengths, q_t, kv)

    middle = tokens + jnp.einsum("ht,hd->td", o_t, full_out, preferred_element_type=F32)
    rms_f = lax.rsqrt(jnp.mean(middle * middle, axis=1, keepdims=True) + EPS)
    normed_f = middle * rms_f
    f_norm = (normed_f * gain_f).astype(BF16)

    grad_y = (
        cotangent.reshape(rows, model).astype(F32) * selected.reshape(rows).astype(F32)[:, None]
    )
    g_all = gather(grad_y.astype(BF16), "seq")
    f_all = gather(f_norm, "seq")
    gate = jnp.dot(f_all, full_gate, preferred_element_type=F32)
    up_val = jnp.dot(f_all, full_up, preferred_element_type=F32)
    sigma = jax.nn.sigmoid(gate)
    activated = gate * sigma
    hidden_act = (activated * up_val).astype(BF16)
    ffn_out = scatter_sum(
        jnp.dot(hidden_act, full_down, preferred_element_type=F32).astype(BF16), "seq"
    )
    output = (middle + ffn_out.astype(F32)).astype(BF16).reshape(one, rows, model)

    grad_hidden = jnp.einsum("td,fd->tf", g_all, full_down, preferred_element_type=F32)
    grad_gate = (grad_hidden * up_val * (sigma + activated * (1.0 - sigma))).astype(BF16)
    grad_up = (grad_hidden * activated).astype(BF16)
    grad_f_part = jnp.einsum(
        "tf,df->td", grad_gate, full_gate, preferred_element_type=F32
    ) + jnp.einsum("tf,df->td", grad_up, full_up, preferred_element_type=F32)
    grad_f_norm = scatter_sum(grad_f_part.astype(BF16), "seq").astype(F32)
    part_down = jnp.einsum("tf,td->fd", hidden_act, g_all, preferred_element_type=F32).astype(BF16)
    part_gate = jnp.einsum("td,tf->df", f_all, grad_gate, preferred_element_type=F32).astype(BF16)
    part_up = jnp.einsum("td,tf->df", f_all, grad_up, preferred_element_type=F32).astype(BF16)

    def ffn_rows(part):
        mine = scatter_sum(part.reshape(seq_count, model // seq_count, ff_part), "ctx", 1)
        return (
            lax.all_to_all(mine, "seq", 0, 0, tiled=True)
            .transpose(1, 0, 2)
            .reshape(own_rows, seq_count * ff_part)
            .astype(F32)
        )

    grad_w_down = scatter_sum(part_down, "ctx").astype(F32)
    grad_w_gate = ffn_rows(part_gate)
    grad_w_up = ffn_rows(part_up)

    grad_ffn_gain, grad_from_f = norm_back(grad_f_norm, middle, rms_f, gain_f, normed_f)
    grad_middle = grad_y + grad_from_f
    g_attn = grad_middle.astype(BF16)
    do_t = jnp.einsum("td,hd->ht", g_attn, full_out, preferred_element_type=F32).astype(BF16)
    part_out = jnp.einsum("ht,td->hd", o_t, g_attn, preferred_element_type=F32).astype(BF16)
    dq_t, dkv = attend_backward(place, block_order, doc_lengths, q_t, kv, o_t, lse, do_t)
    dkv_t = scatter_sum(dkv, "ctx").astype(F32).T
    grad_qkv_t = jnp.concatenate(
        [
            rope_back_t(dq_t, cosine, sine).astype(BF16),
            rope_back_t(dkv_t[:kv_width], cosine, sine).astype(BF16),
            dkv_t[kv_width:].astype(BF16),
        ],
        axis=0,
    )
    part_qkv = jnp.einsum("td,ht->dh", x_norm, grad_qkv_t, preferred_element_type=F32).astype(BF16)
    grad_x_norm = jnp.einsum("ht,dh->td", grad_qkv_t, w_qkv, preferred_element_type=F32)
    grad_attn_gain, grad_from_a = norm_back(grad_x_norm, tokens, rms_a, gain_a, normed_a)
    grad_input = (grad_middle + grad_from_a).reshape(one, rows, model)
    grad_w_out = scatter_sum(part_out, EVERY).astype(F32)
    grad_w_qkv = scatter_sum(part_qkv, EVERY).astype(F32)
    grad_gains = scatter_sum(jnp.stack([grad_attn_gain, grad_ffn_gain], axis=1), EVERY)
    return (
        output,
        grad_input,
        grad_gains[:, 0],
        grad_w_qkv[:, :q_width],
        grad_w_qkv[:, q_width : q_width + kv_width],
        grad_w_qkv[:, q_width + kv_width :],
        grad_w_out,
        grad_gains[:, 1],
        grad_w_gate,
        grad_w_up,
        grad_w_down,
    )


def solution(mesh):
    return jax.shard_map(
        local,
        mesh=mesh,
        in_specs=(
            P("seq", "ctx", None),
            P(("seq", "ctx")),
            P(("seq", "ctx"), None),
            P(("seq", "ctx"), None),
            P(("seq", "ctx"), None),
            P(("seq", "ctx"), None),
            P(("seq", "ctx")),
            P(("seq", "ctx"), None),
            P(("seq", "ctx"), None),
            P(("seq", "ctx"), None),
            P("seq", "ctx", None),
            P("seq", None),
            P("seq", "ctx"),
            P(),
        ),
        out_specs=(
            P("seq", "ctx", None),
            P("seq", "ctx", None),
            P(("seq", "ctx")),
            P(("seq", "ctx"), None),
            P(("seq", "ctx"), None),
            P(("seq", "ctx"), None),
            P(("seq", "ctx"), None),
            P(("seq", "ctx")),
            P(("seq", "ctx"), None),
            P(("seq", "ctx"), None),
            P(("seq", "ctx"), None),
        ),
        check_vma=False,
    )
```

time: 3170 us -> 1400 us (0.44)
  waiting for transfers between devices: 2510 us -> 1070 us
  matrix products: 354 us -> 144 us
  other arithmetic: 196 us -> 28.9 us
    reduce_scatter x9 -> x8, waiting for transfers between devices: 1980 us -> 581 us  [scatter_sum(): return lax.psum_scatter(value, axes, scatter_dimension=dim, tiled=True)]
    dot_general x45 -> x15, matrix products: 354 us -> 144 us  [the longest x1 15.3 us: local(): jnp.einsum('td,fd->tf', g_all, full_down, preferred_element_type=F32)]
    all_gather x9 -> x8, waiting for transfers between devices: 521 us -> 359 us  [gather(): return lax.all_gather(value, axes, axis=dim, tiled=True)]
    sub x2 -> x0, other arithmetic: 142 us -> none  [the longest x1 94.2 us: attend_backward(): grad_scores = (probs * (grad_probs - delta)).astype(jnp.bfloat16)]
    unnamed x18, waiting for transfers between devices: 4.69 us -> 128 us
    unnamed x2 -> x0, blocking collectives: 80.4 us -> none
    all_gather x0 -> x1, blocking collectives: none -> 43.1 us  [gather(): return lax.all_gather(value, axes, axis=dim, tiled=True)]
  transfers between devices with their start and end apart: 18 -> 19, of which waited for: 15 -> 16; matrix products, arithmetic and copies ran while one was open for 14% -> 10% of each run, Pallas kernels for 0% -> 1%
where the time goes in v1:
time: 1400 us; the launch traced here: 1390 us
  waiting for transfers between devices  1070 us (76%)
  matrix products  144 us (10%)
  blocking collectives  70 us (5%)
  local copies, waits for them, and re-layouts  36.3 us (3%)
  other arithmetic  28.9 us (2%)
  Pallas kernels  20.1 us (1%)
  between operations  14.9 us (1%)
    reduce_scatter x8, waiting for transfers between devices, scatter_sum(): return lax.psum_scatter(value, axes, scatter_dimension=dim, tiled=True)  581 us
    all_gather x8, waiting for transfers between devices, gather(): return lax.all_gather(value, axes, axis=dim, tiled=True)  359 us
    unnamed x18, waiting for transfers between devices  128 us
    all_gather x1, blocking collectives, gather(): return lax.all_gather(value, axes, axis=dim, tiled=True)  43.1 us
  transfers between devices with their start and end apart: 19, of which 16 were waited for; matrix products, arithmetic and copies ran while one was open for 10% of the time, Pallas kernels for 1%

profile of v1, /device:TPU:0, one launch (start us, length us, event | category | flops | bytes accessed | tf_op | source)
XLA Modules:
  0.0 1390.8 jit_solution(16342254405778081701)
XLA Ops:
  7.2 1.8 pad_maximum_fusion.4
  9.8 43.1 %all-gather.1 = bf16[32,2,64]{2,1,0:T(2,128)(2,1)S(1)} all-gather(bf16[1,2,64]{2,1,0:T(2,128)(2,1)S(1)} %maximum_bitcast_fusion.1), channel_id=2, replica_groups=mesh['seq'=4,'ctx'=8] {'seq','ctx'}, dimensions={0}, use_global_device_ids=true | all-gather | bytes 8448 | tf_op jit(solution)/shard_map/all_gather | solution.py:249
  55.2 45.8 %all-gather.11.cloned.1.call-done = bf16[2048,2560]{1,0:T(8,128)(2,1)} async-done(((bf16[64,2560]{1,0:T(8,128)(2,1)}), bf16[2048,2560]{1,0:T(8,128)(2,1)}) %all-gather.11.cloned.1.call-update) | async-done | bytes 10485776 | tf_op jit(solution)/shard_map/all_gather | solution.py:249
  101.0 5.8 fusion.28
  110.7 14.0 %all_to_all.20 = bf16[4,64,1408]{2,1,0:T(8,128)(2,1)S(1)} all-to-all(bf16[4,64,1408]{2,1,0:T(8,128)(2,1)S(1)} %copy.59), channel_id=1, replica_groups=mesh['seq'=4,'ctx'=8] {'seq'}, dimensions={0} | all-to-all | bytes 1441792 | tf_op jit(solution)/shard_map/all_to_all | solution.py:311
  126.6 12.8 all_to_all.21
  145.8 8.1 attend_forward.1
  153.8 63.4 %all-gather.15.cloned.1.call-done = bf16[2048,2048]{1,0:T(8,128)(2,1)} async-done(((bf16[64,2048]{1,0:T(8,128)(2,1)}), bf16[2048,2048]{1,0:T(8,128)(2,1)}) %all-gather.15.cloned.1.call-update) | async-done | bytes 8388624 | tf_op jit(solution)/shard_map/all_gather | solution.py:249
  217.2 6.2 multiply_reduce_fusion
  224.7 2.5 fusion.22
  228.1 50.3 %all-gather.19.cloned.1.call-done = bf16[4,512,1408]{2,0,1:T(4,128)(2,1)} async-done(((bf16[4,64,1408]{2,0,1:T(4,128)(2,1)}), bf16[4,512,1408]{2,0,1:T(4,128)(2,1)}) %all-gather.19.cloned.1.call-update) | async-done | bytes 5767184 | tf_op jit(solution)/shard_map/all_gather | solution.py:249
  278.4 5.9 copy.61
  284.3 54.7 %all-gather.21.cloned.1.call-done = bf16[4,512,1408]{2,0,1:T(4,128)(2,1)} async-done(((bf16[4,64,1408]{2,0,1:T(4,128)(2,1)}), bf16[4,512,1408]{2,0,1:T(4,128)(2,1)}) %all-gather.21.cloned.1.call-update) | async-done | bytes 5767184 | tf_op jit(solution)/shard_map/all_gather | solution.py:249
  339.0 5.8 copy.64
  344.8 47.9 %all-gather.17.cloned.1.call-done = bf16[1024,2048]{1,0:T(8,128)(2,1)} async-done(((bf16[256,2048]{1,0:T(8,128)(2,1)}), bf16[1024,2048]{1,0:T(8,128)(2,1)}) %all-gather.17.cloned.1.call-update) | async-done | bytes 4194320 | tf_op jit(solution)/shard_map/all_gather | solution.py:249
  392.7 12.4 fusion.38
  405.1 8.4 fusion.37
  413.5 34.3 %all-gather.25.cloned.1.call-done = bf16[1024,2048]{1,0:T(8,128)(2,1)} async-done(((bf16[256,2048]{1,0:T(8,128)(2,1)}), bf16[1024,2048]{1,0:T(8,128)(2,1)}) %all-gather.25.cloned.1.call-update) | async-done | bytes 4194320 | tf_op jit(solution)/shard_map/all_gather | solution.py:249
  447.9 62.1 %all-gather.23.cloned.1.call-done = bf16[1408,2048]{1,0:T(8,128)(2,1)} async-done(((bf16[176,2048]{1,0:T(8,128)(2,1)}), bf16[1408,2048]{1,0:T(8,128)(2,1)}) %all-gather.23.cloned.1.call-update) | async-done | bytes 5767184 | tf_op jit(solution)/shard_map/all_gather | solution.py:249
  509.9 15.3 %multiply_convert_fusion = (bf16[1024,1408]{1,0:T(8,128)(2,1)S(1)}, bf16[1024,1408]{1,0:T(8,128)(2,1)S(1)}, bf16[1024,1408]{1,0:T(8,128)(2,1)}) fusion(f32[1024,1408]{1,0:T(8,128)} %fusion.37, f32[1024,1408]{1,0:T(8,128)} %fusion.38, bf16[1024,2048]{1,0:T(8,128)(2,1)} %all-gather.25.cloned.1.call-done, bf16[1408,2048]{1,0:T(8,128)(2,1)} %all-gather.23.cloned.1.call-done), kind=kOutput, calls=%fused_computation.6 | convolution fusion | flops 5925765120 | bytes 30146560 | tf_op jit(solution)/shard_map/td,fd->tf/dot_general | solution.py:364
  525.3 10.8 fusion.39
  536.1 11.0 add_convert_fusion
  547.2 11.1 convolution_convert_fusion.5
  558.4 40.3 %reduce-scatter.14.cloned.1.call-done = bf16[256,2048]{1,0:T(8,128)(2,1)} async-done(((bf16[1024,2048]{1,0:T(8,128)(2,1)}), bf16[256,2048]{1,0:T(8,128)(2,1)}) %reduce-scatter.14.cloned.1.call-update) | async-done | bytes 1048592 | tf_op jit(solution)/shard_map/reduce_scatter | solution.py:253
  598.7 1.9 fusion.11
  600.6 53.9 %reduce-scatter.12.cloned.1.call-done = bf16[256,2048]{1,0:T(8,128)(2,1)} async-done(((bf16[1024,2048]{1,0:T(8,128)(2,1)}), bf16[256,2048]{1,0:T(8,128)(2,1)}) %reduce-scatter.12.cloned.1.call-update) | async-done | bytes 1048592 | tf_op jit(solution)/shard_map/reduce_scatter | solution.py:253
  654.5 3.5 fusion.9
  658.0 7.5 fusion.5.do_ref
  665.5 12.1 attend_backward.1
  677.6 4.0 copy.66
  681.6 11.2 convolution_convert_fusion.2
  692.9 11.1 convolution_convert_fusion.3
  704.1 10.5 convolution_convert_fusion.1
  718.8 21.3 %reduce-scatter.16.cloned.1.call-done = bf16[256,512]{0,1:T(8,128)(2,1)} async-done(((bf16[2048,512]{0,1:T(8,128)(2,1)}), bf16[256,512]{0,1:T(8,128)(2,1)}) %reduce-scatter.16.cloned.1.call-update) | async-done | bytes 262160 | tf_op jit(solution)/shard_map/reduce_scatter | solution.py:253
  742.2 8.4 fusion.7
  752.6 6.9 convolution_convert_fusion.4
  760.2 7.1 convolution_convert_fusion
  767.3 38.6 %reduce-scatter.24.cloned.1.call-done = bf16[4,64,1408]{2,1,0:T(8,128)(2,1)} async-done(((bf16[4,512,1408]{2,1,0:T(8,128)(2,1)}), bf16[4,64,1408]{2,1,0:T(8,128)(2,1)}) %reduce-scatter.24.cloned.1.call-update) | async-done | bytes 720912 | tf_op jit(solution)/shard_map/reduce_scatter | solution.py:253
  805.9 4.2 all-to-all-start.3
  810.1 61.4 %reduce-scatter.22.cloned.1.call-done = bf16[4,64,1408]{2,1,0:T(8,128)(2,1)} async-done(((bf16[4,512,1408]{2,1,0:T(8,128)(2,1)}), bf16[4,64,1408]{2,1,0:T(8,128)(2,1)}) %reduce-scatter.22.cloned.1.call-update) | async-done | bytes 720912 | tf_op jit(solution)/shard_map/reduce_scatter | solution.py:253
  871.5 4.2 all-to-all-start.2
  875.7 61.2 %reduce-scatter.26.cloned.1.call-done = bf16[176,2048]{1,0:T(8,128)(2,1)} async-done(((bf16[1408,2048]{1,0:T(8,128)(2,1)}), bf16[176,2048]{1,0:T(8,128)(2,1)}) %reduce-scatter.26.cloned.1.call-update) | async-done | bytes 720912 | tf_op jit(solution)/shard_map/reduce_scatter | solution.py:253
  936.9 2.4 convert_element_type.193
  944.3 1.9 fusion.20
  946.2 126.0 %reduce-scatter.28.cloned.1.call-done = f32[64,2]{1,0:T(8,128)} async-done(((f32[2048,2]{1,0:T(8,128)}), f32[64,2]{1,0:T(8,128)}) %reduce-scatter.28.cloned.1.call-update) | async-done | bytes 528
  1074.3 148.2 %reduce-scatter.20.cloned.1.call-done = bf16[64,2048]{1,0:T(8,128)(2,1)} async-done(((bf16[2048,2048]{1,0:T(8,128)(2,1)}), bf16[64,2048]{1,0:T(8,128)(2,1)}) %reduce-scatter.20.cloned.1.call-update) | async-done | bytes 262160 | tf_op jit(solution)/shard_map/reduce_scatter | solution.py:253
  1222.5 1.8 convert_element_type.183
  1224.3 156.4 %reduce-scatter.18.cloned.1.call-done = bf16[64,2560]{1,0:T(8,128)(2,1)} async-done(((bf16[2048,2560]{1,0:T(8,128)(2,1)}), bf16[64,2560]{1,0:T(8,128)(2,1)}) %reduce-scatter.18.cloned.1.call-update) | async-done | bytes 327696 | tf_op jit(solution)/shard_map/reduce_scatter | solution.py:253
  (146 shorter events, 36.3 us)
Async XLA Ops:
  7.2 47.1 %copy-start = (bf16[1,256,2048]{2,1,0:T(8,128)(2,1)S(1)}, bf16[1,256,2048]{2,1,0:T(8,128)(2,1)}, u32[]{:S(2)}) copy-start(bf16[1,256,2048]{2,1,0:T(8,128)(2,1)} %param.14) | copy-start | bytes 3145732
  7.2 93.8 %all-gather.11.cloned.1.call-start = ((), (), s32[]{:S(2)}) async-start(), calls=%async_computation.13 | async-start | bytes 10813440 | tf_op jit(solution)/shard_map/all_gather | solution.py:249
  9.1 136.7 %all-gather.13.cloned.1.call-start = ((), (), s32[]{:S(2)}) async-start(), calls=%async_computation.14 | async-start | bytes 2359296 | tf_op jit(solution)/shard_map/all_gather | solution.py:249
  53.1 53.8 %copy-start.15 = (f32[2048]{0:T(1024)}, f32[2048]{0:T(1024)S(1)}, u32[]{:S(2)}) copy-start(f32[2048]{0:T(1024)S(1)} %reshape.187) | copy-start | bytes 24580
  54.1 88.7 %copy-start.11 = (f32[64,256]{1,0:T(8,128)}, f32[64,256]{1,0:T(8,128)S(1)}, u32[]{:S(2)}) copy-start(f32[64,256]{1,0:T(8,128)S(1)} %pad_maximum_fusion.6) | copy-start | bytes 196612
  54.3 88.4 %copy-start.9 = (f32[64,256]{1,0:T(8,128)}, f32[64,256]{1,0:T(8,128)S(1)}, u32[]{:S(2)}) copy-start(f32[64,256]{1,0:T(8,128)S(1)} %pad_maximum_fusion.7) | copy-start | bytes 196612
  55.2 51.6 %copy-start.17 = (f32[256]{0:T(256)}, f32[256]{0:T(256)S(1)}, u32[]{:S(2)}) copy-start(f32[256]{0:T(256)S(1)} %get-tuple-element.47) | copy-start | bytes 3076
  106.9 1.5 copy-start.3
  106.9 3.6 copy-start.13
  109.7 107.6 %all-gather.15.cloned.1.call-start = ((), (), s32[]{:S(2)}) async-start(), calls=%async_computation.15 | async-start | bytes 8650752 | tf_op jit(solution)/shard_map/all_gather | solution.py:249
  110.4 168.0 %all-gather.19.cloned.1.call-start = ((), (), s32[]{:S(2)}) async-start(), calls=%async_computation.17 | async-start | bytes 6488064 | tf_op jit(solution)/shard_map/all_gather | solution.py:249
  110.7 15.6 %copy-start.14 = (bf16[64,5632]{1,0:T(8,128)(2,1)S(1)}, bf16[64,5632]{1,0:T(8,128)(2,1)}, u32[]{:S(2)}) copy-start(bf16[64,5632]{1,0:T(8,128)(2,1)} %param.22) | copy-start | bytes 2162692
  126.2 212.8 %all-gather.21.cloned.1.call-start = ((), (), s32[]{:S(2)}) async-start(), calls=%async_computation.18 | async-start | bytes 6488064 | tf_op jit(solution)/shard_map/all_gather | solution.py:249
  140.8 1.6 slice-start
  140.9 251.8 %all-gather.17.cloned.1.call-start = ((), (), s32[]{:S(2)}) async-start(), calls=%async_computation.16 | async-start | bytes 5242880 | tf_op jit(solution)/shard_map/all_gather | solution.py:249
  142.7 1.7 copy-start.4
  223.4 1.3 copy-start.21
  224.7 223.2 %all-gather.25.cloned.1.call-start = ((), (), s32[]{:S(2)}) async-start(), calls=%async_computation.21 | async-start | bytes 5242880 | tf_op jit(solution)/shard_map/all_gather | solution.py:249
  227.3 282.6 %all-gather.23.cloned.1.call-start = ((), (), s32[]{:S(2)}) async-start(), calls=%async_computation.19 | async-start | bytes 6488064 | tf_op jit(solution)/shard_map/all_gather | solution.py:249
  228.1 370.7 %reduce-scatter.14.cloned.1.call-start = ((), (), s32[]{:S(2)}) async-start(), calls=%async_computation.22 | async-start | bytes 5242880 | tf_op jit(solution)/shard_map/reduce_scatter | solution.py:253
  392.7 12.4 copy-start.6
  392.7 12.4 copy-start.22
  525.3 10.8 copy-start.23
  525.3 10.8 copy-start.24
  547.2 107.3 %reduce-scatter.12.cloned.1.call-start = ((), (), s32[]{:S(2)}) async-start(), calls=%async_computation.20 | async-start | bytes 5242880 | tf_op jit(solution)/shard_map/reduce_scatter | solution.py:253
  558.3 181.8 %reduce-scatter.16.cloned.1.call-start = ((), (), s32[]{:S(2)}) async-start(), calls=%async_computation.23 | async-start | bytes 2359296 | tf_op jit(solution)/shard_map/reduce_scatter | solution.py:253
  658.0 7.5 copy-start.1
  681.6 124.4 %reduce-scatter.24.cloned.1.call-start = ((), (), s32[]{:S(2)}) async-start(), calls=%async_computation.27 | async-start | bytes 6488064 | tf_op jit(solution)/shard_map/reduce_scatter | solution.py:253
  692.9 178.6 %reduce-scatter.22.cloned.1.call-start = ((), (), s32[]{:S(2)}) async-start(), calls=%async_computation.26 | async-start | bytes 6488064 | tf_op jit(solution)/shard_map/reduce_scatter | solution.py:253
  704.0 232.9 %reduce-scatter.26.cloned.1.call-start = ((), (), s32[]{:S(2)}) async-start(), calls=%async_computation.28 | async-start | bytes 6488064 | tf_op jit(solution)/shard_map/reduce_scatter | solution.py:253
  714.6 1.6 copy-start.5
  714.6 1.6 copy-start.10
  714.6 357.6 %reduce-scatter.28.cloned.1.call-start = ((), (), s32[]{:S(2)}) async-start(), calls=%async_computation.29 | async-start | bytes 1081344
  716.6 0.8 copy-start.12
  718.8 23.4 %copy-start.7 = (bf16[2048,256]{1,0:T(8,128)(2,1)S(1)}, bf16[2048,256]{1,0:T(8,128)(2,1)}, u32[]{:S(2)}) copy-start(bf16[2048,256]{1,0:T(8,128)(2,1)} %fusion.15) | copy-start | bytes 3145732
  718.8 23.4 %copy-start.16 = (f32[2048]{0:T(1024)S(1)}, f32[2048]{0:T(1024)}, u32[]{:S(2)}) copy-start(f32[2048]{0:T(1024)} %copy-done.15) | copy-start | bytes 24580
  718.8 23.4 %copy-start.18 = (f32[256]{0:T(256)S(1)}, f32[256]{0:T(256)}, u32[]{:S(2)}) copy-start(f32[256]{0:T(256)} %copy-done.17) | copy-start | bytes 3076
  750.7 2.0 copy-start.2
  752.0 470.5 %reduce-scatter.20.cloned.1.call-start = ((), (), s32[]{:S(2)}) async-start(), calls=%async_computation.25 | async-start | bytes 8650752 | tf_op jit(solution)/shard_map/reduce_scatter | solution.py:253
  759.5 0.7 copy-start.19
  759.6 621.1 %reduce-scatter.18.cloned.1.call-start = ((), (), s32[]{:S(2)}) async-start(), calls=%async_computation.24 | async-start | bytes 10813440 | tf_op jit(solution)/shard_map/reduce_scatter | solution.py:253
  805.9 65.6 %all-to-all-start.3 = ((bf16[4,64,1408]{2,1,0:T(8,128)(2,1)}), bf16[4,64,1408]{2,1,0:T(8,128)(2,1)}, u32[]{:S(2)}, u32[]{:S(2)}) async-start(bf16[4,64,1408]{2,1,0:T(8,128)(2,1)} %reduce-scatter.24.cloned.1.call-done), calls=%async_computation.10 | async-start | bytes 1441792 | tf_op jit(solution)/shard_map/all_to_all | solution.py:378
  871.5 70.2 %all-to-all-start.2 = ((bf16[4,64,1408]{2,1,0:T(8,128)(2,1)}), bf16[4,64,1408]{2,1,0:T(8,128)(2,1)}, u32[]{:S(2)}, u32[]{:S(2)}) async-start(bf16[4,64,1408]{2,1,0:T(8,128)(2,1)} %reduce-scatter.22.cloned.1.call-done), calls=%async_computation.8 | async-start | bytes 1441792 | tf_op jit(solution)/shard_map/all_to_all | solution.py:378
  941.7 2.6 copy-start.20
  941.7 2.6 copy-start.8
Sparse Core Ops, SparseCore 0:
  11.5 89.5 all-gather.10
  109.8 27.5 all-gather.12
  140.4 76.7 all-gather.14
  219.3 59.0 all-gather.18
  279.9 59.0 all-gather.20
  341.3 51.3 all-gather.16
  395.1 52.6 all-gather.24
  449.5 60.4 all-gather.22
  547.3 51.3 reduce-scatter.13
  601.8 52.6 reduce-scatter.11
  681.7 58.4 reduce-scatter.15
  742.3 63.5 reduce-scatter.23
  808.2 63.2 reduce-scatter.21
  873.7 63.2 reduce-scatter.25
  939.0 133.1 reduce-scatter.27
  1074.5 148.0 reduce-scatter.19
  1224.8 155.8 reduce-scatter.17

commit v2 on v1

--- a/solution.py
+++ b/solution.py
@@ -242,6 +242,320 @@
     )(place, block_order, doc_lengths, q_t, kv, o_t, lse, do_t)
 
 
+MESH = pl.DeviceIdType.MESH
+
+
+def coords():
+    ctx = lax.axis_index("ctx")
+    return lax.axis_index("seq"), ctx // 2, lax.rem(ctx, 2)
+
+
+def other(place, step, count):
+    return lax.rem(place + step, count)
+
+
+def meet(devices):
+    barrier = pltpu.get_barrier_semaphore()
+    for device in devices:
+        pl.semaphore_signal(barrier, inc=1, device_id=device, device_id_type=MESH)
+    pl.semaphore_wait(barrier, len(devices))
+
+
+def remote(source, target, send_sem, recv_sem, device):
+    return pltpu.make_async_remote_copy(
+        src_ref=source,
+        dst_ref=target,
+        send_sem=send_sem,
+        recv_sem=recv_sem,
+        device_id=device,
+        device_id_type=MESH,
+    )
+
+
+def spread_kernel(scopes, seq_count, chip_count, *refs):
+    count = len(scopes)
+    sources, results = refs[:count], refs[count : 2 * count]
+    sends, recvs, local_sem = refs[2 * count : 3 * count], refs[3 * count : 4 * count], refs[4 * count]
+    seq, chip, core = coords()
+    ctx = lax.axis_index("ctx")
+    planes = [other(seq, step, seq_count) for step in range(1, seq_count)]
+    chips = [other(chip, step, chip_count) for step in range(1, chip_count)]
+    use_plane = any(scope != "ctx" for scope in scopes)
+    use_ctx = any(scope in ("ctx", "all") for scope in scopes)
+    sibling = {"ctx": chip * 2 + 1 - core}
+    peers = []
+    if use_plane:
+        peers += [{"seq": place} for place in planes]
+    if use_ctx:
+        peers += [{"ctx": place * 2 + core} for place in chips] + [sibling]
+    meet(peers)
+
+    ctx_count = 2 * chip_count
+    started = []
+    numbers = [0] * count
+
+    def block(item, at_seq, at_ctx):
+        scope = scopes[item]
+        if scope == "all":
+            return results[item].at[at_seq, at_ctx], at_seq * ctx_count + at_ctx
+        if scope == "ctx":
+            return results[item].at[at_ctx], at_ctx
+        return results[item].at[at_seq], at_seq
+
+    def send(item, at_seq, at_ctx, device, source=None):
+        target, number = block(item, at_seq, at_ctx)
+        copy = remote(
+            target if source is None else source,
+            target,
+            sends[item].at[numbers[item]],
+            recvs[item].at[number],
+            device,
+        )
+        numbers[item] += 1
+        copy.start()
+        started.append(copy)
+
+    def arrive(item, at_seq, at_ctx):
+        target, number = block(item, at_seq, at_ctx)
+        remote(target, target, sends[item].at[0], recvs[item].at[number], sibling).wait_recv()
+
+    locals_ = []
+    for item, scope in enumerate(scopes):
+        target, _ = block(item, seq, ctx)
+        own = sources[item].at[seq] if scope == "swap" else sources[item]
+        copy = pltpu.make_async_copy(own, target, local_sem.at[item])
+        copy.start()
+        locals_.append(copy)
+    for item, scope in enumerate(scopes):
+        if scope in ("seq", "swap"):
+            for place in planes:
+                source = sources[item].at[place] if scope == "swap" else sources[item]
+                send(item, seq, ctx, {"seq": place}, source)
+    for item, scope in enumerate(scopes):
+        if scope in ("ctx", "all"):
+            for place in chips:
+                send(item, seq, ctx, {"ctx": place * 2 + core}, sources[item])
+            if scope == "all":
+                for place in planes:
+                    send(item, seq, ctx, {"seq": place}, sources[item])
+            send(item, seq, ctx, sibling, sources[item])
+    for item, scope in enumerate(scopes):
+        if scope in ("ctx", "all"):
+            for place in chips:
+                arrive(item, seq, place * 2 + core)
+                if scope == "all":
+                    for at_seq in planes:
+                        send(item, seq, place * 2 + core, {"seq": at_seq})
+                send(item, seq, place * 2 + core, sibling)
+    for item, scope in enumerate(scopes):
+        if scope == "all":
+            for place in [chip] + chips:
+                for at_seq in planes:
+                    arrive(item, at_seq, place * 2 + core)
+                    send(item, at_seq, place * 2 + core, sibling)
+        elif scope in ("seq", "swap"):
+            for at_seq in planes:
+                arrive(item, at_seq, ctx)
+    for item, scope in enumerate(scopes):
+        if scope in ("ctx", "all"):
+            for at_seq in [seq] + (planes if scope == "all" else []):
+                for place in [chip] + chips:
+                    arrive(item, at_seq, place * 2 + 1 - core)
+    for copy in locals_:
+        copy.wait()
+    for copy in started:
+        copy.wait_send()
+
+
+def spread(name, collective_id, arrays, scopes, micros):
+    seq_count, ctx_count = lax.axis_size("seq"), lax.axis_size("ctx")
+    chip_count = ctx_count // 2
+    shapes, send_sems, recv_sems = [], [], []
+    for array, scope in zip(arrays, scopes):
+        if scope == "all":
+            lead, sends = (seq_count, ctx_count), seq_count * ctx_count - 1
+        elif scope == "ctx":
+            lead, sends = (ctx_count,), chip_count - 1 + chip_count
+        elif scope == "seq":
+            lead, sends = (seq_count,), seq_count - 1
+        else:
+            lead, sends = (), seq_count - 1
+        shapes.append(jax.ShapeDtypeStruct(lead + array.shape, array.dtype))
+        send_sems.append(pltpu.SemaphoreType.DMA((sends,)))
+        recv_sems.append(pltpu.SemaphoreType.DMA((max(1, math.prod(lead)) if scope != "swap" else seq_count,)))
+    anywhere = pl.BlockSpec(memory_space=pl.ANY)
+    return pl.pallas_call(
+        functools.partial(spread_kernel, scopes, seq_count, chip_count),
+        out_shape=tuple(shapes),
+        in_specs=[anywhere] * len(arrays),
+        out_specs=(anywhere,) * len(arrays),
+        scratch_shapes=send_sems + recv_sems + [pltpu.SemaphoreType.DMA((len(arrays),))],
+        compiler_params=pltpu.CompilerParams(collective_id=collective_id, has_side_effects=True),
+        cost_estimate=pl.CostEstimate(
+            flops=0, transcendentals=0, bytes_accessed=int(micros * 3_000_000)
+        ),
+        name=name,
+    )(*arrays)
+
+
+def fold_kernel(plans, seq_count, chip_count, *refs):
+    count = len(plans)
+    sources, results = refs[:count], refs[count : 2 * count]
+    rest = refs[2 * count :]
+    per = 8
+    seq, chip, core = coords()
+    planes = [other(seq, step, seq_count) for step in range(1, seq_count)]
+    chips = [other(chip, step, chip_count) for step in range(1, chip_count)]
+    sibling = {"ctx": chip * 2 + 1 - core}
+    peers = [{"ctx": place * 2 + core} for place in chips] + [sibling]
+    if any(parts > 1 for parts, _ in plans):
+        peers += [{"seq": place} for place in planes]
+    meet(peers)
+
+    waits = []
+    firsts = []
+    for item, (parts, chunks) in enumerate(plans):
+        got1, _, _, _, _, _, sem_s, sem_r = rest[item * per : (item + 1) * per]
+        width = sources[item].shape[-1] // chunks
+        row = []
+        for chunk in range(chunks):
+            cols = slice(chunk * width, (chunk + 1) * width)
+            copy = remote(
+                sources[item].at[:, :, 1 - core, :, cols],
+                got1.at[:, :, :, cols],
+                sem_s.at[0, chunk, 0],
+                sem_r.at[0, chunk, 0],
+                sibling,
+            )
+            copy.start()
+            row.append(copy)
+        firsts.append(row)
+        waits += row
+
+    seconds = []
+    for item, (parts, chunks) in enumerate(plans):
+        got1, pass2, got2, keep, pass3, got3, sem_s, sem_r = rest[item * per : (item + 1) * per]
+        width = sources[item].shape[-1] // chunks
+        rows_of = []
+        for chunk in range(chunks):
+            cols = slice(chunk * width, (chunk + 1) * width)
+            firsts[item][chunk].wait_recv()
+            mine = []
+            if parts > 1:
+                for step, place in enumerate(planes):
+                    pass2[step, :, :, cols] = (
+                        sources[item][place, :, core, :, cols].astype(F32)
+                        + got1[place, :, :, cols].astype(F32)
+                    ).astype(BF16)
+                    copy = remote(
+                        pass2.at[step, :, :, cols],
+                        got2.at[step, :, :, cols],
+                        sem_s.at[1, chunk, step],
+                        sem_r.at[1, chunk, step],
+                        {"seq": place},
+                    )
+                    copy.start()
+                    mine.append(copy)
+                own = seq
+            else:
+                own = 0
+            keep[:, :, cols] = sources[item][own, :, core, :, cols].astype(F32) + got1[
+                own, :, :, cols
+            ].astype(F32)
+            rows_of.append(mine)
+            waits += mine
+        seconds.append(rows_of)
+
+    thirds = []
+    for item, (parts, chunks) in enumerate(plans):
+        got1, pass2, got2, keep, pass3, got3, sem_s, sem_r = rest[item * per : (item + 1) * per]
+        width = sources[item].shape[-1] // chunks
+        rows_of = []
+        for chunk in range(chunks):
+            cols = slice(chunk * width, (chunk + 1) * width)
+            if parts > 1:
+                for copy in seconds[item][chunk]:
+                    copy.wait_recv()
+
+            def total(place):
+                value = keep[place, :, cols]
+                if parts > 1:
+                    for step in range(seq_count - 1):
+                        value = value + got2[step, place, :, cols].astype(F32)
+                return value
+
+            mine = []
+            for step, place in enumerate(chips):
+                pass3[step, :, cols] = total(place).astype(BF16)
+                copy = remote(
+                    pass3.at[step, :, cols],
+                    got3.at[step, :, cols],
+                    sem_s.at[2, chunk, step],
+                    sem_r.at[2, chunk, step],
+                    {"ctx": place * 2 + core},
+                )
+                copy.start()
+                mine.append(copy)
+            results[item][:, cols] = total(chip)
+            rows_of.append(mine)
+            waits += mine
+        thirds.append(rows_of)
+
+    for item, (parts, chunks) in enumerate(plans):
+        got3 = rest[item * per + 5]
+        width = sources[item].shape[-1] // chunks
+        for chunk in range(chunks):
+            cols = slice(chunk * width, (chunk + 1) * width)
+            for copy in thirds[item][chunk]:
+                copy.wait_recv()
+            value = results[item][:, cols]
+            for step in range(chip_count - 1):
+                value = value + got3[step, :, cols].astype(F32)
+            results[item][:, cols] = value
+    for copy in waits:
+        copy.wait_send()
+
+
+def fold(name, collective_id, arrays, over_all, chunk_counts, micros):
+    seq_count, ctx_count = lax.axis_size("seq"), lax.axis_size("ctx")
+    chip_count = ctx_count // 2
+    plans, inputs, shapes, scratch = [], [], [], []
+    for array, every, chunks in zip(arrays, over_all, chunk_counts):
+        parts = seq_count if every else 1
+        rows = array.shape[0] // (parts * ctx_count)
+        cols = array.shape[1]
+        plans.append((parts, chunks))
+        inputs.append(array.reshape(parts, chip_count, 2, rows, cols))
+        shapes.append(jax.ShapeDtypeStruct((rows, cols), F32))
+        many = max(parts - 1, 1)
+        most = max(many, chip_count - 1)
+        lines = chip_count if every else 1
+        scratch += [
+            pltpu.VMEM((parts, chip_count, rows, cols), BF16),
+            pltpu.VMEM((many, lines, rows, cols), BF16),
+            pltpu.VMEM((many, lines, rows, cols), BF16),
+            pltpu.VMEM((chip_count, rows, cols), F32),
+            pltpu.VMEM((chip_count - 1, rows, cols), BF16),
+            pltpu.VMEM((chip_count - 1, rows, cols), BF16),
+            pltpu.SemaphoreType.DMA((3, chunks, most)),
+            pltpu.SemaphoreType.DMA((3, chunks, most)),
+        ]
+    return pl.pallas_call(
+        functools.partial(fold_kernel, tuple(plans), seq_count, chip_count),
+        out_shape=tuple(shapes),
+        in_specs=[vmem()] * len(arrays),
+        out_specs=(vmem(),) * len(arrays),
+        scratch_shapes=scratch,
+        compiler_params=pltpu.CompilerParams(
+            collective_id=collective_id, has_side_effects=True, vmem_limit_bytes=VMEM_MOST
+        ),
+        cost_estimate=pl.CostEstimate(
+            flops=0, transcendentals=0, bytes_accessed=int(micros * 3_000_000)
+        ),
+        name=name,
+    )(*inputs)
+
+
 EVERY = ("seq", "ctx")
 
 
@@ -306,10 +620,8 @@
     own_rows = w_gate.shape[0]
     ff_part = w_gate.shape[1] // seq_count
 
-    def ffn_columns(weight):
-        split = weight.reshape(own_rows, seq_count, ff_part).transpose(1, 0, 2)
-        mine = lax.all_to_all(split, "seq", 0, 0, tiled=True)
-        return gather(mine, "ctx", 1).reshape(model, ff_part)
+    def split_columns(weight):
+        return weight.reshape(own_rows, seq_count, ff_part).transpose(1, 0, 2)
 
     own_spans = lax.dynamic_slice_in_dim(block_order, place[0] * (rows // span_len), rows // span_len)
     local_pos = (
@@ -321,14 +633,25 @@
     cosine = jnp.concatenate([jnp.cos(angle)] * 2, axis=0)
     sine = jnp.concatenate([jnp.sin(angle)] * 2, axis=0)
 
-    gains = gather(jnp.stack([attn_gain, ffn_gain])[None], EVERY)
-    gain_a = gains[:, 0].reshape(model).astype(F32)
-    gain_f = gains[:, 1].reshape(model).astype(F32)
-    w_qkv = gather(jnp.concatenate([w_query, w_key, w_value], axis=1), EVERY)
-    full_out = gather(w_out, EVERY)
-    full_gate = ffn_columns(w_gate)
-    full_up = ffn_columns(w_up)
     full_down = gather(w_down, "ctx")
+    gain_row = jnp.pad(jnp.concatenate([attn_gain, ffn_gain])[None], ((0, 15), (0, 128 - 2 * own_rows)))
+    gains, w_qkv, gate_mine, up_mine = spread(
+        "gather_qkv",
+        0,
+        [
+            gain_row,
+            jnp.concatenate([w_query, w_key, w_value], axis=1),
+            split_columns(w_gate),
+            split_columns(w_up),
+        ],
+        ("all", "all", "swap", "swap"),
+        85,
+    )
+    gain_a = gains[:, :, 0, :own_rows].reshape(model).astype(F32)
+    gain_f = gains[:, :, 0, own_rows : 2 * own_rows].reshape(model).astype(F32)
+    w_qkv = w_qkv.reshape(model, q_width + 2 * kv_width)
+    full_gate = gather(gate_mine, "ctx", 1).reshape(model, ff_part)
+    full_up = gather(up_mine, "ctx", 1).reshape(model, ff_part)
 
     tokens = hidden_in.reshape(rows, model).astype(F32)
     rms_a = lax.rsqrt(jnp.mean(tokens * tokens, axis=1, keepdims=True) + EPS)
@@ -338,7 +661,11 @@
     q_t = rope_t(qkv_t[:q_width], cosine, sine).astype(BF16)
     k_t = rope_t(qkv_t[q_width : q_width + kv_width], cosine, sine).astype(BF16)
     v_t = qkv_t[q_width + kv_width :].astype(BF16)
-    kv = gather(jnp.concatenate([k_t, v_t], axis=0).T, "ctx")
+    kv, full_out = spread(
+        "gather_kv_out", 1, [jnp.concatenate([k_t, v_t], axis=0).T, w_out], ("ctx", "all"), 85
+    )
+    kv = kv.reshape(length, 2 * kv_width)
+    full_out = full_out.reshape(q_width, model)
     o_t, lse = attend_forward(place, block_order, doc_lengths, q_t, kv)
 
     middle = tokens + jnp.einsum("ht,hd->td", o_t, full_out, preferred_element_type=F32)
@@ -350,7 +677,8 @@
         cotangent.reshape(rows, model).astype(F32) * selected.reshape(rows).astype(F32)[:, None]
     )
     g_all = gather(grad_y.astype(BF16), "seq")
-    f_all = gather(f_norm, "seq")
+    (f_all,) = spread("gather_f", 2, [f_norm], ("seq",), 45)
+    f_all = f_all.reshape(seq_count * rows, model)
     gate = jnp.dot(f_all, full_gate, preferred_element_type=F32)
     up_val = jnp.dot(f_all, full_up, preferred_element_type=F32)
     sigma = jax.nn.sigmoid(gate)
@@ -367,7 +695,10 @@
     grad_f_part = jnp.einsum(
         "tf,df->td", grad_gate, full_gate, preferred_element_type=F32
     ) + jnp.einsum("tf,df->td", grad_up, full_up, preferred_element_type=F32)
-    grad_f_norm = scatter_sum(grad_f_part.astype(BF16), "seq").astype(F32)
+    (grad_f_parts,) = spread(
+        "swap_grad_f", 3, [grad_f_part.astype(BF16).reshape(seq_count, rows, model)], ("swap",), 45
+    )
+    grad_f_norm = jnp.sum(grad_f_parts.astype(F32), axis=0)
     part_down = jnp.einsum("tf,td->fd", hidden_act, g_all, preferred_element_type=F32).astype(BF16)
     part_gate = jnp.einsum("td,tf->df", f_all, grad_gate, preferred_element_type=F32).astype(BF16)
     part_up = jnp.einsum("td,tf->df", f_all, grad_up, preferred_element_type=F32).astype(BF16)
@@ -391,7 +722,8 @@
     do_t = jnp.einsum("td,hd->ht", g_attn, full_out, preferred_element_type=F32).astype(BF16)
     part_out = jnp.einsum("ht,td->hd", o_t, g_attn, preferred_element_type=F32).astype(BF16)
     dq_t, dkv = attend_backward(place, block_order, doc_lengths, q_t, kv, o_t, lse, do_t)
-    dkv_t = scatter_sum(dkv, "ctx").astype(F32).T
+    dkv_own, grad_w_out = fold("fold_kv_out", 4, [dkv, part_out], (False, True), (1, 4), 75)
+    dkv_t = dkv_own.T
     grad_qkv_t = jnp.concatenate(
         [
             rope_back_t(dq_t, cosine, sine).astype(BF16),
@@ -404,18 +736,22 @@
     grad_x_norm = jnp.einsum("ht,dh->td", grad_qkv_t, w_qkv, preferred_element_type=F32)
     grad_attn_gain, grad_from_a = norm_back(grad_x_norm, tokens, rms_a, gain_a, normed_a)
     grad_input = (grad_middle + grad_from_a).reshape(one, rows, model)
-    grad_w_out = scatter_sum(part_out, EVERY).astype(F32)
-    grad_w_qkv = scatter_sum(part_qkv, EVERY).astype(F32)
-    grad_gains = scatter_sum(jnp.stack([grad_attn_gain, grad_ffn_gain], axis=1), EVERY)
+    part_gains = jnp.concatenate(
+        [grad_attn_gain.reshape(-1, own_rows), grad_ffn_gain.reshape(-1, own_rows)], axis=1
+    )
+    part_gains = jnp.pad(part_gains[:, None], ((0, 0), (0, 15), (0, 128 - 2 * own_rows)))
+    grad_w_qkv, grad_gains = fold(
+        "fold_qkv", 5, [part_qkv, part_gains.reshape(-1, 128).astype(BF16)], (True, True), (5, 1), 80
+    )
     return (
         output,
         grad_input,
-        grad_gains[:, 0],
+        grad_gains[0, :own_rows],
         grad_w_qkv[:, :q_width],
         grad_w_qkv[:, q_width : q_width + kv_width],
         grad_w_qkv[:, q_width + kv_width :],
         grad_w_out,
-        grad_gains[:, 1],
+        grad_gains[0, own_rows : 2 * own_rows],
         grad_w_gate,
         grad_w_up,
         grad_w_down,

time: 1400 us -> 814 us (0.58)
  waiting for transfers between devices: 1070 us -> 88.9 us
  Pallas kernels: 20.1 us -> 488 us
  blocking collectives: 70 us -> 0 us
    reduce_scatter x8 -> x4, waiting for transfers between devices: 581 us -> 0.01 us  [scatter_sum(): return lax.psum_scatter(value, axes, scatter_dimension=dim, tiled=True)]
    pallas_call x0 -> x6, Pallas kernels: none -> 461 us  [the longest x4 289 us: spread(): pl.pallas_call(functools.partial(spread_kernel, scopes, seq_count, chip_c...]
    all_gather x8 -> x4, waiting for transfers between devices: 359 us -> 78.1 us  [gather(): return lax.all_gather(value, axes, axis=dim, tiled=True)]
    unnamed x18 -> x8, waiting for transfers between devices: 128 us -> 1.32 us
    all_gather x1 -> x0, blocking collectives: 43.1 us -> none  [gather(): return lax.all_gather(value, axes, axis=dim, tiled=True)]
    all_to_all x2 -> x0, blocking collectives: 26.9 us -> none  [ffn_columns(): mine = lax.all_to_all(split, 'seq', 0, 0, tiled=True)]
  transfers between devices with their start and end apart: 19 -> 10, of which waited for: 16 -> 4; matrix products, arithmetic and copies ran while one was open for 10% -> 21% of each run, Pallas kernels for 1% -> 50%
where the time goes in v2:
time: 814 us; the launch traced here: 801 us
  Pallas kernels  488 us (60%)
  matrix products  144 us (18%)
  waiting for transfers between devices  88.9 us (11%)
  local copies, waits for them, and re-layouts  30.6 us (4%)
  other arithmetic  26.9 us (3%)
  between operations  15.2 us (2%)
    pallas_call x4, Pallas kernels, spread(): pl.pallas_call(functools.partial(spread_kernel, scopes, seq_count, chip_c...  289 us
    pallas_call x2, Pallas kernels, fold(): pl.pallas_call(functools.partial(fold_kernel, tuple(plans), seq_count, ch...  172 us
    all_gather x4, waiting for transfers between devices, gather(): return lax.all_gather(value, axes, axis=dim, tiled=True)  78.1 us
  transfers between devices with their start and end apart: 10, of which 4 were waited for; matrix products, arithmetic and copies ran while one was open for 21% of the time, Pallas kernels for 50%

profile of v2, /device:TPU:0, one launch (start us, length us, event | category | flops | bytes accessed | tf_op | source)
XLA Modules:
  0.0 801.1 jit_solution(10028440341704110335)
XLA Ops:
  8.6 2.6 bitcast_bitcast_fusion
  12.0 83.6 %gather_qkv.1 = (bf16[4,8,16,128]{3,2,1,0:T(8,128)(2,1)}, bf16[4,8,64,2560]{3,2,1,0:T(8,128)(2,1)}, bf16[4,64,1408]{2,1,0:T(8,128)(2,1)}, bf16[4,64,1408]{2,1,0:T(8,128)(2,1)}) custom-call(bf16[16,128]{1,0:T(8,128)(2,1)} %pad.9.refs_0_, bf16[64,2560]{1,0:T(8,128)(2,1)} %pad_maximum_fusion.4.refs_1_, bf16[4,64,1408]{2,1,0:T(8,128)(2,1)} %get-tuple-element.72.refs_2_, ...), custom_call_target="tpu_custom_call" | custom-call | bytes 255000000 | tf_op jit(solution)/shard_map/gather_qkv/pallas_call | solution.py:387
  98.3 1.7 convert_reduce_fusion.1
  100.9 6.6 fusion.26
  112.4 1.7 copy.50
  114.0 1.8 copy.49
  117.5 1.8 copy.38
  119.8 1.6 copy-done.7
  121.4 1.3 fusion.19.q_ref
  123.5 97.8 %gather_kv_out.1 = (bf16[8,256,512]{2,1,0:T(8,128)(2,1)}, bf16[4,8,64,2048]{3,2,1,0:T(8,128)(2,1)}) custom-call(bf16[256,512]{1,0:T(8,128)(2,1)} %maximum_bitcast_fusion.refs_0_, bf16[64,2048]{1,0:T(8,128)(2,1)} %refs_1_.1), custom_call_target="tpu_custom_call" | custom-call | bytes 255000000 | tf_op jit(solution)/shard_map/gather_kv_out/pallas_call | solution.py:387
  221.3 10.9 %attend_forward.1 = (bf16[2048,256]{1,0:T(8,128)(2,1)}, f32[2,4,1024]{2,1,0:T(4,128)}) custom-call(s32[1]{0:T(128)} %bitcast.1.place_ref, s32[16]{0:T(128)} %order_ref.3, s32[1,8]{1,0:T(1,128)} %lens_ref.3, bf16[2048,256]{1,0:T(8,128)(2,1)} %fusion.19.q_ref, bf16[2048,512]{1,0:T(8,128)(2,1)} %bitcast.171), custom_call_target="tpu_custom_call" | custom-call | flops 2147483648 | bytes 4194304 | tf_op jit(solution)/shard_map/attend_forward/pallas_call | solution.py:195
  232.2 6.2 multiply_reduce_fusion.2
  238.4 1.2 multiply_convert_fusion.3.refs_0_
  239.6 58.0 %gather_f.1 = bf16[4,256,2048]{2,1,0:T(8,128)(2,1)} custom-call(bf16[256,2048]{1,0:T(8,128)(2,1)} %multiply_convert_fusion.3.refs_0_), custom_call_target="tpu_custom_call" | custom-call | bytes 135000000 | tf_op jit(solution)/shard_map/gather_f/pallas_call | solution.py:387
  297.7 11.7 %fusion.40 = f32[1024,1408]{1,0:T(8,128)} fusion(bf16[1024,2048]{1,0:T(8,128)(2,1)} %bitcast.144, bf16[2048,1408]{1,0:T(8,128)(2,1)} %bitcast.167), kind=kOutput, calls=%fused_computation.100 | convolution fusion | flops 5905580032 | bytes 15728640 | tf_op jit(solution)/shard_map/dot_general | solution.py:683
  309.4 12.0 %fusion.39 = f32[1024,1408]{1,0:T(8,128)} fusion(bf16[1024,2048]{1,0:T(8,128)(2,1)} %bitcast.145, bf16[2048,1408]{1,0:T(8,128)(2,1)} %bitcast.169), kind=kOutput, calls=%fused_computation.99 | convolution fusion | flops 5905580032 | bytes 15728640 | tf_op jit(solution)/shard_map/dot_general | solution.py:682
  321.4 11.5 %all-gather.11.cloned.1.call-done = bf16[1024,2048]{1,0:T(8,128)(2,1)} async-done(((bf16[256,2048]{1,0:T(8,128)(2,1)}), bf16[1024,2048]{1,0:T(8,128)(2,1)}) %all-gather.11.cloned.1.call-update) | async-done | bytes 4194320 | tf_op jit(solution)/shard_map/all_gather | solution.py:563
  332.8 66.6 %all-gather.9.cloned.1.call-done = bf16[1408,2048]{1,0:T(8,128)(2,1)} async-done(((bf16[176,2048]{1,0:T(8,128)(2,1)}), bf16[1408,2048]{1,0:T(8,128)(2,1)}) %all-gather.9.cloned.1.call-update) | async-done | bytes 5767184 | tf_op jit(solution)/shard_map/all_gather | solution.py:563
  399.4 16.0 %multiply_convert_fusion = (bf16[1024,1408]{1,0:T(8,128)(2,1)}, bf16[1024,1408]{1,0:T(8,128)(2,1)}, bf16[1024,1408]{1,0:T(8,128)(2,1)S(1)}) fusion(f32[1024,1408]{1,0:T(8,128)} %fusion.39, f32[1024,1408]{1,0:T(8,128)} %fusion.40, bf16[1024,2048]{1,0:T(8,128)(2,1)} %all-gather.11.cloned.1.call-done, bf16[1408,2048]{1,0:T(8,128)(2,1)} %all-gather.9.cloned.1.call-done), kind=kOutput, calls=%fused_computation.7 | convolution fusion | flops 5925765120 | bytes 30146560 | tf_op jit(solution)/shard_map/td,fd->tf/dot_general | solution.py:692
  415.4 1.6 copy-done.34
  417.0 8.2 %convolution_convert_fusion.5 = bf16[1024,2048]{1,0:T(8,128)(2,1)} fusion(bf16[1024,1408]{1,0:T(8,128)(2,1)S(1)} %get-tuple-element.47, bf16[1408,2048]{1,0:T(8,128)(2,1)S(1)} %copy-done.32), kind=kOutput, calls=%fused_computation.12 | convolution fusion | flops 5907677184 | bytes 12845056 | tf_op jit(solution)/shard_map/dot_general | solution.py:688
  425.3 11.0 %convolution_convert_fusion.2 = bf16[2048,1408]{1,0:T(8,128)(2,1)} fusion(bf16[1024,2048]{1,0:T(8,128)(2,1)} %bitcast.146, bf16[1024,1408]{1,0:T(8,128)(2,1)} %get-tuple-element.45), kind=kOutput, calls=%fused_computation.4 | convolution fusion | flops 5908463616 | bytes 12845056 | tf_op jit(solution)/shard_map/td,tf->df/dot_general | solution.py:704
  436.4 11.6 %convolution_convert_fusion.3 = bf16[2048,1408]{1,0:T(8,128)(2,1)} fusion(bf16[1024,2048]{1,0:T(8,128)(2,1)} %bitcast.147, bf16[1024,1408]{1,0:T(8,128)(2,1)} %get-tuple-element.46), kind=kOutput, calls=%fused_computation.5 | convolution fusion | flops 5908463616 | bytes 12845056 | tf_op jit(solution)/shard_map/td,tf->df/dot_general | solution.py:703
  448.0 10.5 %convolution_convert_fusion.1 = bf16[1408,2048]{1,0:T(8,128)(2,1)} fusion(bf16[1024,1408]{1,0:T(8,128)(2,1)} %copy-done.34, bf16[1024,2048]{1,0:T(8,128)(2,1)} %all-gather.11.cloned.1.call-done), kind=kOutput, calls=%fused_computation.3 | convolution fusion | flops 5908463616 | bytes 12845056 | tf_op jit(solution)/shard_map/tf,td->fd/dot_general | solution.py:702
  458.6 9.7 %fusion.41 = f32[1024,2048]{1,0:T(8,128)S(1)} fusion(bf16[1024,1408]{1,0:T(8,128)(2,1)} %get-tuple-element.46, bf16[2048,1408]{1,0:T(8,128)(2,1)} %bitcast.170), kind=kOutput, calls=%fused_computation.101 | convolution fusion | flops 5905580032 | bytes 17039360 | tf_op jit(solution)/shard_map/tf,df->td/dot_general | solution.py:695
  468.4 11.2 %add_convert_fusion = bf16[1024,2048]{1,0:T(8,128)(2,1)} fusion(f32[1024,2048]{1,0:T(8,128)S(1)} %fusion.41, bf16[1024,1408]{1,0:T(8,128)(2,1)S(1)} %copy-done.35, bf16[2048,1408]{1,0:T(8,128)(2,1)} %bitcast.168), kind=kOutput, calls=%fused_computation.2 | convolution fusion | flops 5909774336 | bytes 21233664 | tf_op jit(solution)/shard_map/tf,df->td/dot_general | solution.py:697
  479.5 49.5 %swap_grad_f.1 = bf16[4,256,2048]{2,1,0:T(8,128)(2,1)} custom-call(bf16[4,256,2048]{2,1,0:T(8,128)(2,1)} %bitcast.148), custom_call_target="tpu_custom_call" | custom-call | bytes 135000000 | tf_op jit(solution)/shard_map/swap_grad_f/pallas_call | solution.py:387
  529.1 3.3 convert_reduce_fusion
  532.4 1.3 copy-done.4
  535.0 3.5 fusion.22
  538.4 7.6 convolution_convert_fusion.6.do_ref
  546.0 16.2 %attend_backward.1 = (f32[2048,256]{1,0:T(8,128)}, bf16[2048,512]{1,0:T(8,128)(2,1)}) custom-call(s32[1]{0:T(128)} %bitcast.1.place_ref, s32[16]{0:T(128)} %order_ref.3, s32[1,8]{1,0:T(1,128)} %lens_ref.3, bf16[2048,256]{1,0:T(8,128)(2,1)} %fusion.19.q_ref, bf16[2048,512]{1,0:T(8,128)(2,1)} %bitcast.172, bf16[2048,256]{1,0:T(8,128)(2,1)} %get-tuple-element.28.o_ref, ...), custom_call_target="tpu_custom_call" | custom-call | flops 5368709120 | bytes 9437184 | tf_op jit(solution)/shard_map/attend_backward/pallas_call | solution.py:222
  562.3 5.7 convolution_convert_fusion.4
  567.9 88.6 %fold_kv_out.1 = (f32[256,512]{1,0:T(8,128)}, f32[64,2048]{1,0:T(8,128)}) custom-call(bf16[1,4,2,256,512]{4,3,2,1,0:T(8,128)(2,1)} %bitcast.150, bf16[4,4,2,64,2048]{4,3,2,1,0:T(8,128)(2,1)} %bitcast.137), custom_call_target="tpu_custom_call" | custom-call | bytes 225000000 | tf_op jit(solution)/shard_map/fold_kv_out/pallas_call | solution.py:543
  661.7 8.7 %fusion.9 = (bf16[2048]{0:T(1024)(128)(2,1)S(1)}, f32[256]{0:T(256)S(1)}, f32[256,2048]{1,0:T(8,128)}) fusion(bf16[1,256,2048]{2,1,0:T(8,128)(2,1)S(1)} %copy-done.1, f32[256]{0:T(256)S(1)} %copy-done.29, f32[2048]{0:T(1024)S(1)} %copy-done.25, bf16[2048,2560]{1,0:T(8,128)(2,1)} %bitcast.166, bf16[256,256]{1,0:T(8,128)(2,1)} %copy.44, ...), kind=kOutput, calls=%fused_computation.26 | convolution fusion | flops 2691954432 | bytes 14956544 | tf_op jit(solution)/shard_map/ht,dh->td/dot_general | solution.py:736
  671.3 7.0 convolution_convert_fusion
  678.3 83.2 %fold_qkv.1 = (f32[64,2560]{1,0:T(8,128)}, f32[16,128]{1,0:T(8,128)}) custom-call(bf16[4,4,2,64,2560]{4,3,2,1,0:T(8,128)(2,1)} %bitcast.136, bf16[4,4,2,16,128]{4,3,2,1,0:T(8,128)(2,1)} %bitcast.162), custom_call_target="tpu_custom_call" | custom-call | bytes 240000000 | tf_op jit(solution)/shard_map/fold_qkv/pallas_call | solution.py:543
  761.5 1.5 fusion.38
  763.0 4.2 all-to-all-start.1
  767.3 3.5 fusion.14
  770.8 7.2 all-to-all-done.1
  778.0 3.5 all-to-all-start
  781.5 1.3 slice_bitcast_fusion
  782.8 1.9 slice.78
  784.7 2.4 convert_element_type.202
  788.2 1.2 copy.54
  789.5 2.3 all-to-all-done
  791.8 1.2 copy.53
  (142 shorter events, 22.9 us)
Async XLA Ops:
  7.2 4.0 copy-start.26
  7.2 4.0 copy-start.27
  7.2 4.0 copy-start.23
  7.2 290.4 %all-gather.7.cloned.1.call-start = ((), (), s32[]{:S(2)}) async-start(), calls=%async_computation.7 | async-start | bytes 6488064 | tf_op jit(solution)/shard_map/all_gather | solution.py:563
  11.2 85.2 %copy-start.31 = (s32[1,256]{1,0:T(1,128)S(1)}, s32[1,256]{1,0:T(1,128)}, u32[]{:S(2)}) copy-start(s32[1,256]{1,0:T(1,128)} %param.26) | copy-start | bytes 3076
  11.2 85.2 %copy-start.9 = (bf16[1,256,2048]{2,1,0:T(8,128)(2,1)S(1)}, bf16[1,256,2048]{2,1,0:T(8,128)(2,1)}, u32[]{:S(2)}) copy-start(bf16[1,256,2048]{2,1,0:T(8,128)(2,1)} %param.24) | copy-start | bytes 3145732
  95.6 4.5 copy-start
  95.6 213.8 %all-gather.5.cloned.1.call-start = ((), (), s32[]{:S(2)}) async-start(), calls=%async_computation.6 | async-start | bytes 6488064 | tf_op jit(solution)/shard_map/all_gather | solution.py:563
  96.4 236.5 %all-gather.11.cloned.1.call-start = ((), (), s32[]{:S(2)}) async-start(), calls=%async_computation.10 | async-start | bytes 5242880 | tf_op jit(solution)/shard_map/all_gather | solution.py:563
  97.7 301.7 %all-gather.9.cloned.1.call-start = ((), (), s32[]{:S(2)}) async-start(), calls=%async_computation.8 | async-start | bytes 6488064 | tf_op jit(solution)/shard_map/all_gather | solution.py:563
  98.3 436.2 %reduce-scatter.5.cloned.1.call-start = ((), (), s32[]{:S(2)}) async-start(), calls=%async_computation.9 | async-start | bytes 5242880 | tf_op jit(solution)/shard_map/reduce_scatter | solution.py:567
  100.0 7.5 copy-start.24
  100.9 6.6 copy-start.28
  107.5 1.7 copy-start.6
  107.5 1.8 copy-start.33
  109.7 9.9 %copy-start.13 = (f32[64,256]{1,0:T(8,128)}, f32[64,256]{1,0:T(8,128)S(1)}, u32[]{:S(2)}) copy-start(f32[64,256]{1,0:T(8,128)S(1)} %get-tuple-element.74) | copy-start | bytes 196612
  109.7 10.0 %copy-start.17 = (f32[64,256]{1,0:T(8,128)}, f32[64,256]{1,0:T(8,128)S(1)}, u32[]{:S(2)}) copy-start(f32[64,256]{1,0:T(8,128)S(1)} %get-tuple-element.73) | copy-start | bytes 196612
  111.5 11.2 %copy-start.11 = (f32[256,256]{0,1:T(8,128)}, f32[256,256]{0,1:T(8,128)S(1)}, u32[]{:S(2)}) copy-start(f32[256,256]{0,1:T(8,128)S(1)} %copy.36) | copy-start | bytes 786436
  119.6 1.8 copy-start.7
  121.3 1.3 copy-start.15
  121.4 1.3 copy-start.16
  121.4 1.4 copy-start.22
  399.4 17.6 %copy-start.32 = (bf16[1408,2048]{1,0:T(8,128)(2,1)S(1)}, bf16[1408,2048]{1,0:T(8,128)(2,1)}, u32[]{:S(2)}) copy-start(bf16[1408,2048]{1,0:T(8,128)(2,1)} %all-gather.9.cloned.1.call-done) | copy-start | bytes 17301508
  415.4 1.6 copy-start.34
  425.2 337.8 %reduce-scatter.9.cloned.1.call-start = ((), (), s32[]{:S(2)}) async-start(), calls=%async_computation.12 | async-start | bytes 6488064 | tf_op jit(solution)/shard_map/reduce_scatter | solution.py:567
  436.3 334.4 %reduce-scatter.7.cloned.1.call-start = ((), (), s32[]{:S(2)}) async-start(), calls=%async_computation.11 | async-start | bytes 6488064 | tf_op jit(solution)/shard_map/reduce_scatter | solution.py:567
  448.0 336.7 %reduce-scatter.11.cloned.1.call-start = ((), (), s32[]{:S(2)}) async-start(), calls=%async_computation.13 | async-start | bytes 6488064 | tf_op jit(solution)/shard_map/reduce_scatter | solution.py:567
  458.6 9.8 %copy-start.35 = (bf16[1024,1408]{1,0:T(8,128)(2,1)S(1)}, bf16[1024,1408]{1,0:T(8,128)(2,1)}, u32[]{:S(2)}) copy-start(bf16[1024,1408]{1,0:T(8,128)(2,1)} %get-tuple-element.45) | copy-start | bytes 8650756
  532.4 1.3 copy-start.4
  533.7 1.3 copy-start.10
  538.4 23.8 %copy-start.2 = (f32[256,2048]{1,0:T(8,128)}, f32[256,2048]{1,0:T(8,128)S(1)}, u32[]{:S(2)}) copy-start(f32[256,2048]{1,0:T(8,128)S(1)} %get-tuple-element.50) | copy-start | bytes 6291460
  546.0 16.2 %copy-start.8 = (bf16[2048,256]{1,0:T(8,128)(2,1)S(1)}, bf16[2048,256]{1,0:T(8,128)(2,1)}, u32[]{:S(2)}) copy-start(bf16[2048,256]{1,0:T(8,128)(2,1)} %get-tuple-element.28.o_ref) | copy-start | bytes 3145732
  567.9 90.5 %copy-start.5 = (f32[2048,256]{1,0:T(8,128)S(1)}, f32[2048,256]{1,0:T(8,128)}, u32[]{:S(2)}) copy-start(f32[2048,256]{1,0:T(8,128)} %get-tuple-element.33) | copy-start | bytes 6291460
  567.9 90.5 %copy-start.14 = (f32[64,256]{1,0:T(8,128)S(1)}, f32[64,256]{1,0:T(8,128)}, u32[]{:S(2)}) copy-start(f32[64,256]{1,0:T(8,128)} %copy-done.13) | copy-start | bytes 196612
  658.9 0.8 copy-start.18
  660.1 1.2 copy-start.12
  660.2 1.2 copy-start.19
  660.2 1.5 copy-start.1
  660.2 1.5 copy-start.25
  660.2 1.5 copy-start.29
  661.7 9.6 %copy-start.20 = (bf16[256,256]{1,0:T(8,128)(2,1)S(1)}, bf16[256,256]{1,0:T(8,128)(2,1)}, u32[]{:S(2)}) copy-start(bf16[256,256]{1,0:T(8,128)(2,1)} %copy.44) | copy-start | bytes 393220
  678.3 89.0 %copy-start.3 = (f32[256,2048]{1,0:T(8,128)S(1)}, f32[256,2048]{1,0:T(8,128)}, u32[]{:S(2)}) copy-start(f32[256,2048]{1,0:T(8,128)} %copy-done.2) | copy-start | bytes 6291460
  678.3 89.0 %copy-start.30 = (f32[256]{0:T(256)S(1)}, f32[256]{0:T(256)}, u32[]{:S(2)}) copy-start(f32[256]{0:T(256)} %get-tuple-element.64) | copy-start | bytes 3076
  763.0 14.9 %all-to-all-start.1 = ((bf16[4,64,1408]{2,1,0:T(8,128)(2,1)}), bf16[4,64,1408]{2,1,0:T(8,128)(2,1)}, u32[]{:S(2)}, u32[]{:S(2)}) async-start(bf16[4,64,1408]{2,1,0:T(8,128)(2,1)} %reduce-scatter.9.cloned.1.call-done), calls=%async_computation.4 | async-start | bytes 1441792 | tf_op jit(solution)/shard_map/all_to_all | solution.py:709
  778.0 13.8 %all-to-all-start = ((bf16[4,64,1408]{2,1,0:T(8,128)(2,1)}), bf16[4,64,1408]{2,1,0:T(8,128)(2,1)S(1)}, u32[]{:S(2)}, u32[]{:S(2)}) async-start(bf16[4,64,1408]{2,1,0:T(8,128)(2,1)} %reduce-scatter.7.cloned.1.call-done), calls=%async_computation.2 | async-start | bytes 1441792 | tf_op jit(solution)/shard_map/all_to_all | solution.py:709
  789.5 3.6 copy-start.21
Sparse Core Ops, SparseCore 0:
  95.7 95.0 all-gather.6
  192.4 59.3 all-gather.4
  254.2 78.6 all-gather.10
  334.3 65.0 all-gather.8
  425.3 51.3 reduce-scatter.4
  479.0 64.8 reduce-scatter.8
  546.3 73.2 reduce-scatter.6
  622.1 80.6 reduce-scatter.10

commit v3 on v2

--- a/solution.py
+++ b/solution.py
@@ -272,40 +272,47 @@
     )
 
 
-def spread_kernel(scopes, seq_count, chip_count, *refs):
+def spread_kernel(scopes, halves, seq_count, chip_count, *refs):
     count = len(scopes)
     sources, results = refs[:count], refs[count : 2 * count]
     sends, recvs, local_sem = refs[2 * count : 3 * count], refs[3 * count : 4 * count], refs[4 * count]
     seq, chip, core = coords()
     ctx = lax.axis_index("ctx")
+    ctx_count = 2 * chip_count
     planes = [other(seq, step, seq_count) for step in range(1, seq_count)]
     chips = [other(chip, step, chip_count) for step in range(1, chip_count)]
-    use_plane = any(scope != "ctx" for scope in scopes)
-    use_ctx = any(scope in ("ctx", "all") for scope in scopes)
+    beside, above = seq + 1 - 2 * lax.rem(seq, 2), other(seq, 2, 4)
     sibling = {"ctx": chip * 2 + 1 - core}
     peers = []
-    if use_plane:
+    if any(scope != "ctx" for scope in scopes):
         peers += [{"seq": place} for place in planes]
-    if use_ctx:
+    if any(scope in ("ctx", "all") for scope in scopes):
         peers += [{"ctx": place * 2 + core} for place in chips] + [sibling]
     meet(peers)
 
-    ctx_count = 2 * chip_count
     started = []
     numbers = [0] * count
 
-    def block(item, at_seq, at_ctx):
+    def block(item, at_seq, at_ctx, half):
         scope = scopes[item]
         if scope == "all":
-            return results[item].at[at_seq, at_ctx], at_seq * ctx_count + at_ctx
-        if scope == "ctx":
-            return results[item].at[at_ctx], at_ctx
-        return results[item].at[at_seq], at_seq
-
-    def send(item, at_seq, at_ctx, device, source=None):
-        target, number = block(item, at_seq, at_ctx)
+            ref, number = results[item].at[at_seq, at_ctx], at_seq * ctx_count + at_ctx
+        elif scope == "ctx":
+            ref, number = results[item].at[at_ctx], at_ctx
+        else:
+            ref, number = results[item].at[at_seq], at_seq
+        return part(ref, item, half), 2 * number + (half or 0)
+
+    def part(ref, item, half):
+        if half is None:
+            return ref
+        rows = results[item].shape[-2] // 2
+        return ref.at[pl.ds(half * rows, rows)]
+
+    def send(item, at_seq, at_ctx, half, device, source=None):
+        target, number = block(item, at_seq, at_ctx, half)
         copy = remote(
-            target if source is None else source,
+            target if source is None else part(source, item, half),
             target,
             sends[item].at[numbers[item]],
             recvs[item].at[number],
@@ -315,52 +322,94 @@
         copy.start()
         started.append(copy)
 
-    def arrive(item, at_seq, at_ctx):
-        target, number = block(item, at_seq, at_ctx)
+    def arrive(item, at_seq, at_ctx, half):
+        target, number = block(item, at_seq, at_ctx, half)
         remote(target, target, sends[item].at[0], recvs[item].at[number], sibling).wait_recv()
 
+    def cut(item):
+        return (0, 1) if halves[item] else (None,)
+
+    def plane_send(item, at_ctx, half, source=None):
+        places = planes
+        if halves[item]:
+            places = (beside, above) if half == 0 else (above, beside)
+        for place in places:
+            send(item, seq, at_ctx, half, {"seq": place}, source)
+
+    def plane_relay(item, at_ctx):
+        if halves[item]:
+            arrive(item, beside, at_ctx, 0)
+            send(item, beside, at_ctx, 0, {"seq": above})
+            arrive(item, above, at_ctx, 1)
+            send(item, above, at_ctx, 1, {"seq": beside})
+
+    def plane_end(item, at_ctx):
+        if halves[item]:
+            arrive(item, beside, at_ctx, 1)
+            arrive(item, above, at_ctx, 0)
+            arrive(item, 3 - seq, at_ctx, 0)
+            arrive(item, 3 - seq, at_ctx, 1)
+        else:
+            for place in planes:
+                arrive(item, place, at_ctx, None)
+        if scopes[item] == "all":
+            for place in planes:
+                send(item, place, at_ctx, None, sibling)
+
+    items = range(count)
+    lines = [item for item in items if scopes[item] in ("ctx", "all")]
+    flats = [item for item in items if scopes[item] in ("seq", "all")]
+    everywhere = [item for item in items if scopes[item] == "all"]
+    swaps = [item for item in items if scopes[item] == "swap"]
     locals_ = []
-    for item, scope in enumerate(scopes):
-        target, _ = block(item, seq, ctx)
-        own = sources[item].at[seq] if scope == "swap" else sources[item]
+    for item in items:
+        target, _ = block(item, seq, ctx, None)
+        own = sources[item].at[seq] if scopes[item] == "swap" else sources[item]
         copy = pltpu.make_async_copy(own, target, local_sem.at[item])
         copy.start()
         locals_.append(copy)
-    for item, scope in enumerate(scopes):
-        if scope in ("seq", "swap"):
-            for place in planes:
-                source = sources[item].at[place] if scope == "swap" else sources[item]
-                send(item, seq, ctx, {"seq": place}, source)
-    for item, scope in enumerate(scopes):
-        if scope in ("ctx", "all"):
+    for item in lines:
+        for half in cut(item):
             for place in chips:
-                send(item, seq, ctx, {"ctx": place * 2 + core}, sources[item])
-            if scope == "all":
-                for place in planes:
-                    send(item, seq, ctx, {"seq": place}, sources[item])
-            send(item, seq, ctx, sibling, sources[item])
-    for item, scope in enumerate(scopes):
-        if scope in ("ctx", "all"):
-            for place in chips:
-                arrive(item, seq, place * 2 + core)
-                if scope == "all":
-                    for at_seq in planes:
-                        send(item, seq, place * 2 + core, {"seq": at_seq})
-                send(item, seq, place * 2 + core, sibling)
-    for item, scope in enumerate(scopes):
-        if scope == "all":
+                send(item, seq, ctx, half, {"ctx": place * 2 + core}, sources[item])
+    for item in swaps:
+        for place in planes:
+            send(item, seq, ctx, None, {"seq": place}, sources[item].at[place])
+    for item in flats:
+        for half in cut(item):
+            plane_send(item, ctx, half, sources[item])
+    for item in lines:
+        send(item, seq, ctx, None, sibling, sources[item])
+    for item in flats:
+        plane_relay(item, ctx)
+    for index, place in enumerate(chips):
+        at_ctx = place * 2 + core
+        for item in lines:
+            for half in cut(item):
+                arrive(item, seq, at_ctx, half)
+                if scopes[item] == "all":
+                    plane_send(item, at_ctx, half)
+            send(item, seq, at_ctx, None, sibling)
+        for item in everywhere:
+            if index:
+                plane_relay(item, chips[index - 1] * 2 + core)
+        if index == 0:
+            for item in flats:
+                plane_end(item, ctx)
+        elif index > 1:
+            for item in everywhere:
+                plane_end(item, chips[index - 2] * 2 + core)
+    for item in everywhere:
+        plane_relay(item, chips[-1] * 2 + core)
+        for place in chips[-2:]:
+            plane_end(item, place * 2 + core)
+    for item in swaps:
+        for place in planes:
+            arrive(item, place, ctx, None)
+    for item in lines:
+        for at_seq in [seq] + (planes if scopes[item] == "all" else []):
             for place in [chip] + chips:
-                for at_seq in planes:
-                    arrive(item, at_seq, place * 2 + core)
-                    send(item, at_seq, place * 2 + core, sibling)
-        elif scope in ("seq", "swap"):
-            for at_seq in planes:
-                arrive(item, at_seq, ctx)
-    for item, scope in enumerate(scopes):
-        if scope in ("ctx", "all"):
-            for at_seq in [seq] + (planes if scope == "all" else []):
-                for place in [chip] + chips:
-                    arrive(item, at_seq, place * 2 + 1 - core)
+                arrive(item, at_seq, place * 2 + 1 - core, None)
     for copy in locals_:
         copy.wait()
     for copy in started:
@@ -370,22 +419,25 @@
 def spread(name, collective_id, arrays, scopes, micros):
     seq_count, ctx_count = lax.axis_size("seq"), lax.axis_size("ctx")
     chip_count = ctx_count // 2
-    shapes, send_sems, recv_sems = [], [], []
+    shapes, send_sems, recv_sems, halves = [], [], [], []
     for array, scope in zip(arrays, scopes):
+        halved = seq_count == 4 and scope in ("all", "seq") and array.shape[0] % 32 == 0
+        across = 6 if halved else seq_count - 1
         if scope == "all":
-            lead, sends = (seq_count, ctx_count), seq_count * ctx_count - 1
+            lead = (seq_count, ctx_count)
+            sends = (2 if halved else 1) * (chip_count - 1) + across * chip_count + seq_count * chip_count
         elif scope == "ctx":
-            lead, sends = (ctx_count,), chip_count - 1 + chip_count
-        elif scope == "seq":
-            lead, sends = (seq_count,), seq_count - 1
+            lead, sends = (ctx_count,), 2 * chip_count - 1
         else:
-            lead, sends = (), seq_count - 1
-        shapes.append(jax.ShapeDtypeStruct(lead + array.shape, array.dtype))
+            lead, sends = (seq_count,), across
+        halves.append(halved)
+        shape = array.shape if scope == "swap" else lead + array.shape
+        shapes.append(jax.ShapeDtypeStruct(shape, array.dtype))
         send_sems.append(pltpu.SemaphoreType.DMA((sends,)))
-        recv_sems.append(pltpu.SemaphoreType.DMA((max(1, math.prod(lead)) if scope != "swap" else seq_count,)))
+        recv_sems.append(pltpu.SemaphoreType.DMA((2 * math.prod(lead),)))
     anywhere = pl.BlockSpec(memory_space=pl.ANY)
     return pl.pallas_call(
-        functools.partial(spread_kernel, scopes, seq_count, chip_count),
+        functools.partial(spread_kernel, scopes, tuple(halves), seq_count, chip_count),
         out_shape=tuple(shapes),
         in_specs=[anywhere] * len(arrays),
         out_specs=(anywhere,) * len(arrays),
@@ -398,21 +450,40 @@
     )(*arrays)
 
 
-def fold_kernel(plans, seq_count, chip_count, *refs):
+def fold_kernel(plans, swap_count, sum_count, seq_count, chip_count, *refs):
     count = len(plans)
-    sources, results = refs[:count], refs[count : 2 * count]
-    rest = refs[2 * count :]
+    every = count + swap_count + sum_count
+    sources, swap_sources = refs[:count], refs[count : count + swap_count]
+    sum_sources = refs[count + swap_count : every]
+    all_results = refs[every : 2 * every]
+    results, swap_results = all_results[:count], all_results[count : count + swap_count]
+    sum_results = all_results[count + swap_count :]
+    rest = refs[2 * every :]
     per = 8
+    swap_rest = rest[count * per :]
+    sum_rest = swap_rest[4 * swap_count :]
     seq, chip, core = coords()
     planes = [other(seq, step, seq_count) for step in range(1, seq_count)]
     chips = [other(chip, step, chip_count) for step in range(1, chip_count)]
     sibling = {"ctx": chip * 2 + 1 - core}
     peers = [{"ctx": place * 2 + core} for place in chips] + [sibling]
-    if any(parts > 1 for parts, _ in plans):
+    if swap_count or sum_count or any(parts > 1 for parts, _ in plans):
         peers += [{"seq": place} for place in planes]
     meet(peers)
 
     waits = []
+    swapped = []
+    for item in range(swap_count):
+        got, sem_s, sem_r, sem_own = swap_rest[4 * item : 4 * item + 4]
+        own = pltpu.make_async_copy(swap_sources[item].at[seq], got.at[seq], sem_own)
+        own.start()
+        swapped.append(own)
+        for step, place in enumerate(planes):
+            copy = remote(
+                swap_sources[item].at[place], got.at[seq], sem_s.at[step], sem_r.at[seq], {"seq": place}
+            )
+            copy.start()
+            waits.append(copy)
     firsts = []
     for item, (parts, chunks) in enumerate(plans):
         got1, _, _, _, _, _, sem_s, sem_r = rest[item * per : (item + 1) * per]
@@ -466,6 +537,23 @@
             waits += mine
         seconds.append(rows_of)
 
+    slots, there = plane_slots(seq_count)
+    summed = []
+    for item in range(sum_count):
+        got, sem_s, sem_r = sum_rest[3 * item : 3 * item + 3]
+        row = []
+        for slot in range(1, seq_count):
+            copy = remote(
+                sum_sources[item].at[slot],
+                got.at[there[slot] - 1],
+                sem_s.at[slot],
+                sem_r.at[there[slot]],
+                {"seq": slots[slot]},
+            )
+            copy.start()
+            row.append(copy)
+        summed.append(row)
+        waits += row
     thirds = []
     for item, (parts, chunks) in enumerate(plans):
         got1, pass2, got2, keep, pass3, got3, sem_s, sem_r = rest[item * per : (item + 1) * per]
@@ -512,11 +600,27 @@
             for step in range(chip_count - 1):
                 value = value + got3[step, :, cols].astype(F32)
             results[item][:, cols] = value
+    for item in range(sum_count):
+        got = sum_rest[3 * item]
+        for copy in summed[item]:
+            copy.wait_recv()
+        value = sum_sources[item][0].astype(F32)
+        for step in range(seq_count - 1):
+            value = value + got[step].astype(F32)
+        sum_results[item][...] = value
+    for item in range(swap_count):
+        got, sem_s, sem_r, _ = swap_rest[4 * item : 4 * item + 4]
+        swapped[item].wait()
+        for place in planes:
+            remote(got.at[place], got.at[place], sem_s.at[0], sem_r.at[place], sibling).wait_recv()
+        width = got.shape[-1]
+        for place in range(seq_count):
+            swap_results[item][:, place * width : (place + 1) * width] = got[place].astype(F32)
     for copy in waits:
         copy.wait_send()
 
 
-def fold(name, collective_id, arrays, over_all, chunk_counts, micros):
+def fold(name, collective_id, arrays, over_all, chunk_counts, micros, swaps=(), sums=()):
     seq_count, ctx_count = lax.axis_size("seq"), lax.axis_size("ctx")
     chip_count = ctx_count // 2
     plans, inputs, shapes, scratch = [], [], [], []
@@ -540,11 +644,30 @@
             pltpu.SemaphoreType.DMA((3, chunks, most)),
             pltpu.SemaphoreType.DMA((3, chunks, most)),
         ]
+    for array in swaps:
+        inputs.append(array)
+        shapes.append(jax.ShapeDtypeStruct((array.shape[1], seq_count * array.shape[2]), F32))
+        scratch += [
+            pltpu.VMEM(array.shape, BF16),
+            pltpu.SemaphoreType.DMA((seq_count - 1,)),
+            pltpu.SemaphoreType.DMA((seq_count,)),
+            pltpu.SemaphoreType.DMA,
+        ]
+    for array in sums:
+        inputs.append(array)
+        shapes.append(jax.ShapeDtypeStruct(array.shape[1:], F32))
+        scratch += [
+            pltpu.VMEM((seq_count - 1, *array.shape[1:]), BF16),
+            pltpu.SemaphoreType.DMA((seq_count,)),
+            pltpu.SemaphoreType.DMA((seq_count,)),
+        ]
     return pl.pallas_call(
-        functools.partial(fold_kernel, tuple(plans), seq_count, chip_count),
+        functools.partial(
+            fold_kernel, tuple(plans), len(swaps), len(sums), seq_count, chip_count
+        ),
         out_shape=tuple(shapes),
-        in_specs=[vmem()] * len(arrays),
-        out_specs=(vmem(),) * len(arrays),
+        in_specs=[vmem()] * len(inputs),
+        out_specs=(vmem(),) * len(inputs),
         scratch_shapes=scratch,
         compiler_params=pltpu.CompilerParams(
             collective_id=collective_id, has_side_effects=True, vmem_limit_bytes=VMEM_MOST
@@ -554,6 +677,298 @@
         ),
         name=name,
     )(*inputs)
+
+
+def tiles(extent, width, visit):
+    whole = extent // width
+
+    @pl.loop(0, whole)
+    def _(number):
+        visit(pl.ds(pl.multiple_of(number * width, width), width))
+
+    if extent % width:
+        visit(pl.ds(whole * width, extent % width))
+
+
+def stream_rows(extent, width, produce, stage, sem, target):
+    whole = extent // width
+
+    def leave(slot, rows, size):
+        return pltpu.make_async_copy(
+            stage.at[slot, pl.ds(0, size)], target.at[rows], sem.at[slot]
+        )
+
+    @pl.loop(0, whole)
+    def _(number):
+        slot = lax.rem(number, 2)
+        rows = pl.ds(pl.multiple_of(number * width, width), width)
+
+        @pl.when(number >= 2)
+        def _():
+            leave(slot, rows, width).wait()
+
+        stage[slot] = produce(rows).astype(stage.dtype)
+        leave(slot, rows, width).start()
+
+    for number in range(max(0, whole - 2), whole):
+        leave(number % 2, pl.ds(number * width, width), width).wait()
+    if extent % width:
+        size = extent % width
+        rows = pl.ds(whole * width, size)
+        stage[0, :size] = produce(rows).astype(stage.dtype)
+        leave(0, rows, size).start()
+        leave(0, rows, size).wait()
+
+
+def plane_slots(seq_count):
+    seq = lax.axis_index("seq")
+    if seq_count == 4:
+        beside, above = seq + 1 - 2 * lax.rem(seq, 2), other(seq, 2, 4)
+        return [seq, beside, above, 3 - seq], [0, 1, 2, 3]
+    return [seq] + [other(seq, step, seq_count) for step in range(1, seq_count)], [0] + [
+        seq_count - step for step in range(1, seq_count)
+    ]
+
+
+def ffn_kernel(
+    seq_count,
+    f_ref,
+    g_ref,
+    wg_ref,
+    wu_ref,
+    wd_ref,
+    gf_ref,
+    out_ref,
+    pg_ref,
+    pu_ref,
+    pd_ref,
+    f_s,
+    g_s,
+    wg,
+    wu,
+    wd,
+    gh,
+    hid,
+    gg,
+    gu,
+    parts,
+    got,
+    stage_f,
+    stage_d,
+    stage_o,
+    in_sem,
+    f_send,
+    f_recv,
+    x_send,
+    x_recv,
+    leave_sem,
+):
+    rows = f_ref.shape[0]
+    model, width = wg.shape
+    places, there = plane_slots(seq_count)
+    meet([{"seq": place} for place in places[1:]])
+
+    started = []
+
+    def f_block(slot, half):
+        if half is None:
+            return f_s.at[pl.ds(slot * rows, rows)]
+        return f_s.at[pl.ds(slot * rows + half * (rows // 2), rows // 2)]
+
+    def f_copy(source, to, slot, half):
+        copy = remote(
+            source,
+            f_block(slot, half),
+            f_send.at[len(started)],
+            f_recv.at[slot, half or 0],
+            {"seq": places[to]},
+        )
+        copy.start()
+        started.append(copy)
+
+    def f_arrive(slot, half):
+        block = f_block(slot, half)
+        remote(
+            block, block, f_send.at[0], f_recv.at[slot, half or 0], {"seq": places[1]}
+        ).wait_recv()
+
+    if seq_count == 4:
+        for half in (0, 1):
+            source = f_ref.at[pl.ds(half * (rows // 2), rows // 2)]
+            for to in (1, 2) if half == 0 else (2, 1):
+                f_copy(source, to, to, half)
+    else:
+        for to in range(1, seq_count):
+            f_copy(f_ref, to, there[to], None)
+    loads = []
+    for slot in range(seq_count):
+        loads.append(
+            pltpu.make_async_copy(
+                g_ref.at[places[slot]], g_s.at[pl.ds(slot * rows, rows)], in_sem.at[slot]
+            )
+        )
+    load_wd = pltpu.make_async_copy(wd_ref, wd, in_sem.at[seq_count])
+    load_f = pltpu.make_async_copy(f_ref, f_block(0, None), in_sem.at[seq_count + 1])
+    load_wg = pltpu.make_async_copy(wg_ref, wg, in_sem.at[seq_count + 2])
+    load_wu = pltpu.make_async_copy(wu_ref, wu, in_sem.at[seq_count + 3])
+    for load in [*loads, load_wd, load_f, load_wg, load_wu]:
+        load.start()
+    for load in [*loads, load_wd]:
+        load.wait()
+
+    def grad_hidden(cols):
+        gh[:, cols] = dot32(g_s[...], wd[cols, :], ((1,), (1,)))
+
+    tiles(width, 256, grad_hidden)
+    for load in (load_f, load_wg, load_wu):
+        load.wait()
+
+    def act(first, count, tile):
+        own = slice(first, first + count)
+
+        def visit(cols):
+            gate = dot32(f_s[own, :], wg[:, cols], ((1,), (0,)))
+            up_val = dot32(f_s[own, :], wu[:, cols], ((1,), (0,)))
+            grad = gh[own, cols]
+            sigma = jax.nn.sigmoid(gate)
+            activated = gate * sigma
+            hid[own, cols] = (activated * up_val).astype(BF16)
+            gg[own, cols] = (grad * up_val * (sigma + activated * (1.0 - sigma))).astype(BF16)
+            gu[own, cols] = (grad * activated).astype(BF16)
+
+        tiles(width, tile, visit)
+
+    act(0, rows, 256)
+    if seq_count == 4:
+        f_arrive(1, 0)
+        f_copy(f_block(1, 0), 2, 3, 0)
+        f_arrive(2, 1)
+        f_copy(f_block(2, 1), 1, 3, 1)
+        f_arrive(1, 1)
+        f_arrive(2, 0)
+        act(rows, 2 * rows, 256)
+        f_arrive(3, 0)
+        f_arrive(3, 1)
+        act(3 * rows, rows, 256)
+    else:
+        for slot in range(1, seq_count):
+            f_arrive(slot, None)
+        act(rows, (seq_count - 1) * rows, 256)
+
+    def part_copy(slot, cols):
+        return remote(
+            parts.at[pl.ds((slot - 1) * rows, rows), cols],
+            got.at[there[slot] - 1, :, cols],
+            x_send.at[slot],
+            x_recv.at[there[slot]],
+            {"seq": places[slot]},
+        )
+
+    def grad_f(cols):
+        part = dot32(gg[...], wg[cols, :], ((1,), (1,))) + dot32(gu[...], wu[cols, :], ((1,), (1,)))
+        gf_ref[:, cols] = part[:rows]
+        parts[:, cols] = part[rows:].astype(BF16)
+        for slot in range(1, seq_count):
+            part_copy(slot, cols).start()
+
+    tiles(model, 256, grad_f)
+    stream_rows(
+        width,
+        256,
+        lambda own: dot32(hid[:, own], g_s[...], ((0,), (0,))),
+        stage_d,
+        leave_sem.at[0],
+        pd_ref,
+    )
+    stream_rows(
+        model,
+        256,
+        lambda own: dot32(f_s[:, own], gg[...], ((0,), (0,))),
+        stage_f,
+        leave_sem.at[1],
+        pg_ref,
+    )
+    stream_rows(
+        model,
+        256,
+        lambda own: dot32(f_s[:, own], gu[...], ((0,), (0,))),
+        stage_f,
+        leave_sem.at[1],
+        pu_ref,
+    )
+
+    def out_copy(cols):
+        return pltpu.make_async_copy(stage_o.at[:, cols], out_ref.at[:, cols], leave_sem.at[2, 0])
+
+    def out_part(cols):
+        stage_o[:, cols] = dot32(hid[...], wd[:, cols], ((1,), (0,))).astype(BF16)
+        out_copy(cols).start()
+
+    tiles(model, 256, out_part)
+    everything = pl.ds(0, model)
+    out_copy(everything).wait()
+    for slot in range(1, seq_count):
+        part_copy(slot, everything).wait_recv()
+    total = gf_ref[...]
+    for slot in range(seq_count - 1):
+        total = total + got[slot].astype(F32)
+    gf_ref[...] = total
+    for slot in range(1, seq_count):
+        part_copy(slot, everything).wait_send()
+    for copy in started:
+        copy.wait_send()
+
+
+def feed_forward(collective_id, f_norm, g_all, w_gate, w_up, w_down):
+    seq_count = lax.axis_size("seq")
+    rows, model = f_norm.shape
+    width = w_gate.shape[1]
+    count = seq_count * rows
+    anywhere = pl.BlockSpec(memory_space=pl.ANY)
+    dma = pltpu.SemaphoreType.DMA
+    return pl.pallas_call(
+        functools.partial(ffn_kernel, seq_count),
+        out_shape=(
+            jax.ShapeDtypeStruct((rows, model), F32),
+            jax.ShapeDtypeStruct((count, model), BF16),
+            jax.ShapeDtypeStruct((model, width), BF16),
+            jax.ShapeDtypeStruct((model, width), BF16),
+            jax.ShapeDtypeStruct((width, model), BF16),
+        ),
+        in_specs=[anywhere] * 5,
+        out_specs=(vmem(), anywhere, anywhere, anywhere, anywhere),
+        scratch_shapes=[
+            pltpu.VMEM((count, model), BF16),
+            pltpu.VMEM((count, model), BF16),
+            pltpu.VMEM((model, width), BF16),
+            pltpu.VMEM((model, width), BF16),
+            pltpu.VMEM((width, model), BF16),
+            pltpu.VMEM((count, width), F32),
+            pltpu.VMEM((count, width), BF16),
+            pltpu.VMEM((count, width), BF16),
+            pltpu.VMEM((count, width), BF16),
+            pltpu.VMEM((count - rows, model), BF16),
+            pltpu.VMEM((seq_count - 1, rows, model), BF16),
+            pltpu.VMEM((2, 256, width), BF16),
+            pltpu.VMEM((2, 256, model), BF16),
+            pltpu.VMEM((count, model), BF16),
+            dma((seq_count + 4,)),
+            dma((max(6, seq_count),)),
+            dma((seq_count, 2)),
+            dma((seq_count,)),
+            dma((seq_count,)),
+            dma((3, 2)),
+        ],
+        compiler_params=pltpu.CompilerParams(
+            collective_id=collective_id, has_side_effects=True, vmem_limit_bytes=60 * 1024 * 1024
+        ),
+        cost_estimate=pl.CostEstimate(
+            flops=18 * count * model * width,
+            transcendentals=count * width,
+            bytes_accessed=4 * (3 * width * model + 3 * count * model),
+        ),
+        name="feed_forward",
+    )(f_norm, g_all.reshape(seq_count, rows, model), w_gate, w_up, w_down)
 
 
 EVERY = ("seq", "ctx")
@@ -650,9 +1065,13 @@
     gain_a = gains[:, :, 0, :own_rows].reshape(model).astype(F32)
     gain_f = gains[:, :, 0, own_rows : 2 * own_rows].reshape(model).astype(F32)
     w_qkv = w_qkv.reshape(model, q_width + 2 * kv_width)
+    full_down, gate_mine, up_mine = lax.optimization_barrier((full_down, gate_mine, up_mine))
     full_gate = gather(gate_mine, "ctx", 1).reshape(model, ff_part)
     full_up = gather(up_mine, "ctx", 1).reshape(model, ff_part)
 
+    grad_y = (
+        cotangent.reshape(rows, model).astype(F32) * selected.reshape(rows).astype(F32)[:, None]
+    )
     tokens = hidden_in.reshape(rows, model).astype(F32)
     rms_a = lax.rsqrt(jnp.mean(tokens * tokens, axis=1, keepdims=True) + EPS)
     normed_a = tokens * rms_a
@@ -661,9 +1080,14 @@
     q_t = rope_t(qkv_t[:q_width], cosine, sine).astype(BF16)
     k_t = rope_t(qkv_t[q_width : q_width + kv_width], cosine, sine).astype(BF16)
     v_t = qkv_t[q_width + kv_width :].astype(BF16)
-    kv, full_out = spread(
-        "gather_kv_out", 1, [jnp.concatenate([k_t, v_t], axis=0).T, w_out], ("ctx", "all"), 85
-    )
+    kv, full_out, g_all = spread(
+        "gather_kv_out",
+        1,
+        [jnp.concatenate([k_t, v_t], axis=0).T, w_out, grad_y.astype(BF16)],
+        ("ctx", "all", "seq"),
+        85,
+    )
+    g_all = g_all.reshape(seq_count * rows, model)
     kv = kv.reshape(length, 2 * kv_width)
     full_out = full_out.reshape(q_width, model)
     o_t, lse = attend_forward(place, block_order, doc_lengths, q_t, kv)
@@ -673,56 +1097,32 @@
     normed_f = middle * rms_f
     f_norm = (normed_f * gain_f).astype(BF16)
 
-    grad_y = (
-        cotangent.reshape(rows, model).astype(F32) * selected.reshape(rows).astype(F32)[:, None]
-    )
-    g_all = gather(grad_y.astype(BF16), "seq")
-    (f_all,) = spread("gather_f", 2, [f_norm], ("seq",), 45)
-    f_all = f_all.reshape(seq_count * rows, model)
-    gate = jnp.dot(f_all, full_gate, preferred_element_type=F32)
-    up_val = jnp.dot(f_all, full_up, preferred_element_type=F32)
-    sigma = jax.nn.sigmoid(gate)
-    activated = gate * sigma
-    hidden_act = (activated * up_val).astype(BF16)
-    ffn_out = scatter_sum(
-        jnp.dot(hidden_act, full_down, preferred_element_type=F32).astype(BF16), "seq"
-    )
-    output = (middle + ffn_out.astype(F32)).astype(BF16).reshape(one, rows, model)
-
-    grad_hidden = jnp.einsum("td,fd->tf", g_all, full_down, preferred_element_type=F32)
-    grad_gate = (grad_hidden * up_val * (sigma + activated * (1.0 - sigma))).astype(BF16)
-    grad_up = (grad_hidden * activated).astype(BF16)
-    grad_f_part = jnp.einsum(
-        "tf,df->td", grad_gate, full_gate, preferred_element_type=F32
-    ) + jnp.einsum("tf,df->td", grad_up, full_up, preferred_element_type=F32)
-    (grad_f_parts,) = spread(
-        "swap_grad_f", 3, [grad_f_part.astype(BF16).reshape(seq_count, rows, model)], ("swap",), 45
-    )
-    grad_f_norm = jnp.sum(grad_f_parts.astype(F32), axis=0)
-    part_down = jnp.einsum("tf,td->fd", hidden_act, g_all, preferred_element_type=F32).astype(BF16)
-    part_gate = jnp.einsum("td,tf->df", f_all, grad_gate, preferred_element_type=F32).astype(BF16)
-    part_up = jnp.einsum("td,tf->df", f_all, grad_up, preferred_element_type=F32).astype(BF16)
+    grad_f_norm, ffn_part, part_gate, part_up, part_down = feed_forward(
+        2, f_norm, g_all, full_gate, full_up, full_down
+    )
 
     def ffn_rows(part):
-        mine = scatter_sum(part.reshape(seq_count, model // seq_count, ff_part), "ctx", 1)
-        return (
-            lax.all_to_all(mine, "seq", 0, 0, tiled=True)
-            .transpose(1, 0, 2)
-            .reshape(own_rows, seq_count * ff_part)
-            .astype(F32)
-        )
+        return scatter_sum(part.reshape(seq_count, model // seq_count, ff_part), "ctx", 1)
 
     grad_w_down = scatter_sum(part_down, "ctx").astype(F32)
-    grad_w_gate = ffn_rows(part_gate)
-    grad_w_up = ffn_rows(part_up)
-
+    rows_gate = ffn_rows(part_gate)
+    rows_up = ffn_rows(part_up)
     grad_ffn_gain, grad_from_f = norm_back(grad_f_norm, middle, rms_f, gain_f, normed_f)
     grad_middle = grad_y + grad_from_f
     g_attn = grad_middle.astype(BF16)
     do_t = jnp.einsum("td,hd->ht", g_attn, full_out, preferred_element_type=F32).astype(BF16)
     part_out = jnp.einsum("ht,td->hd", o_t, g_attn, preferred_element_type=F32).astype(BF16)
     dq_t, dkv = attend_backward(place, block_order, doc_lengths, q_t, kv, o_t, lse, do_t)
-    dkv_own, grad_w_out = fold("fold_kv_out", 4, [dkv, part_out], (False, True), (1, 4), 75)
+    dkv_own, grad_w_out, ffn_out = fold(
+        "fold_kv_out",
+        4,
+        [dkv, part_out],
+        (False, True),
+        (1, 4),
+        100,
+        sums=[ffn_part.reshape(seq_count, rows, model)],
+    )
+    output = (middle + ffn_out).astype(BF16).reshape(one, rows, model)
     dkv_t = dkv_own.T
     grad_qkv_t = jnp.concatenate(
         [
@@ -740,8 +1140,14 @@
         [grad_attn_gain.reshape(-1, own_rows), grad_ffn_gain.reshape(-1, own_rows)], axis=1
     )
     part_gains = jnp.pad(part_gains[:, None], ((0, 0), (0, 15), (0, 128 - 2 * own_rows)))
-    grad_w_qkv, grad_gains = fold(
-        "fold_qkv", 5, [part_qkv, part_gains.reshape(-1, 128).astype(BF16)], (True, True), (5, 1), 80
+    grad_w_qkv, grad_gains, grad_w_gate, grad_w_up = fold(
+        "fold_qkv",
+        5,
+        [part_qkv, part_gains.reshape(-1, 128).astype(BF16)],
+        (True, True),
+        (5, 1),
+        80,
+        [rows_gate, rows_up],
     )
     return (
         output,

time: 814 us -> 675 us (0.83); the launches traced: 801 us -> 671 us
  matrix products: 144 us -> 41.9 us
  waiting for transfers between devices: 88.9 us -> 16.2 us
  Pallas kernels: 488 us -> 531 us
    dot_general x9 -> x0, matrix products: 102 us -> none  [the longest x1 16 us: local(): jnp.einsum('td,fd->tf', g_all, full_down, preferred_element_type=F32)]
    all_gather x4 -> x3, waiting for transfers between devices: 78.1 us -> 14.2 us  [gather(): return lax.all_gather(value, axes, axis=dim, tiled=True)]
    pallas_call x6 -> x5, Pallas kernels: 461 us -> 504 us  [the longest x2 211 us: fold(): pl.pallas_call(functools.partial(fold_kernel, tuple(plans), len(swaps), l...]
    all_to_all x2 -> x0, waiting for transfers between devices: 9.47 us -> none  [ffn_rows(): lax.all_to_all(mine, 'seq', 0, 0, tiled=True).transpose(1, 0, 2)]
  transfers between devices with their start and end apart: 10 -> 6, of which waited for: 4 -> 1; matrix products, arithmetic and copies ran while one was open for 21% -> 15% of each run, Pallas kernels for 50% -> 65%
where the time goes in v3:
time: 675 us; the launch traced here: 671 us
  Pallas kernels  531 us (79%)
  matrix products  41.9 us (6%)
  local copies, waits for them, and re-layouts  36.2 us (5%)
  other arithmetic  31.2 us (5%)
  waiting for transfers between devices  16.2 us (2%)
  between operations  14.7 us (2%)
    pallas_call x2, Pallas kernels, fold(): pl.pallas_call(functools.partial(fold_kernel, tuple(plans), len(swaps), l...  211 us
    pallas_call x2, Pallas kernels, spread(): pl.pallas_call(functools.partial(spread_kernel, scopes, tuple(halves), se...  197 us
    pallas_call x1, Pallas kernels, feed_forward(): pl.pallas_call(functools.partial(ffn_kernel, seq_count), out_shape=(jax.S...  95.3 us
    pallas_call x1, Pallas kernels, attend_backward(): pl.pallas_call(functools.partial(attend_backward_kernel, span_len, spans)...  16.2 us
    all_gather x3, waiting for transfers between devices, gather(): return lax.all_gather(value, axes, axis=dim, tiled=True)  14.2 us
  transfers between devices with their start and end apart: 6, of which 1 were waited for; matrix products, arithmetic and copies ran while one was open for 15% of the time, Pallas kernels for 65%

profile of v3, /device:TPU:0, one launch (start us, length us, event | category | flops | bytes accessed | tf_op | source)
XLA Modules:
  0.0 671.4 jit_solution(11433793602722903668)
XLA Ops:
  9.3 1.7 pad_maximum_fusion.4.refs_1_
  11.0 2.6 bitcast_bitcast_fusion
  13.6 84.6 %gather_qkv.1 = (bf16[4,8,16,128]{3,2,1,0:T(8,128)(2,1)}, bf16[4,8,64,2560]{3,2,1,0:T(8,128)(2,1)}, bf16[4,64,1408]{2,1,0:T(8,128)(2,1)}, bf16[4,64,1408]{2,1,0:T(8,128)(2,1)}) custom-call(bf16[16,128]{1,0:T(8,128)(2,1)} %pad.9.refs_0_, bf16[64,2560]{1,0:T(8,128)(2,1)} %pad_maximum_fusion.4.refs_1_, bf16[4,64,1408]{2,1,0:T(8,128)(2,1)} %get-tuple-element.91.refs_2_, ...), custom_call_target="tpu_custom_call" | custom-call | bytes 255000000 | tf_op jit(solution)/shard_map/gather_qkv/pallas_call | solution.py:439
  99.1 1.7 convert_reduce_fusion
  101.7 6.0 fusion.25
  108.4 0.9 slice.85
  111.7 1.1 copy.34
  113.6 1.7 copy.46
  115.2 1.8 copy.45
  117.0 1.0 slice_negate_fusion.3
  118.7 1.8 copy.36
  120.9 1.8 copy-done.6
  122.7 1.3 fusion.18.q_ref
  124.9 1.2 fusion.22.refs_2_
  126.1 112.0 %gather_kv_out.1 = (bf16[8,256,512]{2,1,0:T(8,128)(2,1)}, bf16[4,8,64,2048]{3,2,1,0:T(8,128)(2,1)}, bf16[4,256,2048]{2,1,0:T(8,128)(2,1)}) custom-call(bf16[256,512]{1,0:T(8,128)(2,1)} %maximum_bitcast_fusion.refs_0_, bf16[64,2048]{1,0:T(8,128)(2,1)} %refs_1_.1, bf16[256,2048]{1,0:T(8,128)(2,1)} %fusion.22.refs_2_), custom_call_target="tpu_custom_call" | custom-call | bytes 255000000 | tf_op jit(solution)/shard_map/gather_kv_out/pallas_call | solution.py:439
  238.1 10.9 %attend_forward.1 = (bf16[2048,256]{1,0:T(8,128)(2,1)}, f32[2,4,1024]{2,1,0:T(4,128)}) custom-call(s32[1]{0:T(128)} %bitcast.1.place_ref, s32[16]{0:T(128)} %order_ref.3, s32[1,8]{1,0:T(1,128)} %lens_ref.3, bf16[2048,256]{1,0:T(8,128)(2,1)} %fusion.18.q_ref, bf16[2048,512]{1,0:T(8,128)(2,1)} %bitcast.136), custom_call_target="tpu_custom_call" | custom-call | flops 2147483648 | bytes 4194304 | tf_op jit(solution)/shard_map/attend_forward/pallas_call | solution.py:195
  249.0 6.2 multiply_reduce_fusion.2
  256.4 1.2 multiply_convert_fusion.f_ref
  257.6 14.2 %all-gather.8.cloned.1.call-done = bf16[4,512,1408]{2,1,0:T(8,128)(2,1)} async-done(((bf16[4,64,1408]{2,1,0:T(8,128)(2,1)}), bf16[4,512,1408]{2,1,0:T(8,128)(2,1)}) %all-gather.8.cloned.1.call-update) | async-done | bytes 5767184 | tf_op jit(solution)/shard_map/all_gather | solution.py:978
  271.8 95.3 %feed_forward.1 = (f32[256,2048]{1,0:T(8,128)}, bf16[1024,2048]{1,0:T(8,128)(2,1)}, bf16[2048,1408]{1,0:T(8,128)(2,1)}, bf16[2048,1408]{1,0:T(8,128)(2,1)}, bf16[1408,2048]{1,0:T(8,128)(2,1)}) custom-call(bf16[256,2048]{1,0:T(8,128)(2,1)} %multiply_convert_fusion.f_ref, bf16[4,256,2048]{2,1,0:T(8,128)(2,1)} %get-tuple-element.43.g_ref, ...), custom_call_target="tpu_custom_call" | custom-call | flops 53150220288 | bytes 59768832 | tf_op jit(solution)/shard_map/feed_forward/pallas_call | solution.py:929
  368.4 2.9 multiply_reduce_fusion
  371.9 7.8 %convolution_convert_fusion.2.do_ref = bf16[2048,256]{1,0:T(8,128)(2,1)} fusion(bf16[2048,2048]{1,0:T(8,128)(2,1)} %bitcast.112, f32[256,2048]{1,0:T(8,128)S(1)} %fusion.21), kind=kOutput, calls=%fused_computation.11 | convolution fusion | flops 2148532224 | bytes 11534336 | tf_op jit(solution)/shard_map/td,hd->ht/dot_general | solution.py:1113
  379.7 16.2 %attend_backward.1 = (f32[2048,256]{1,0:T(8,128)}, bf16[2048,512]{1,0:T(8,128)(2,1)}) custom-call(s32[1]{0:T(128)} %bitcast.1.place_ref, s32[16]{0:T(128)} %order_ref.3, s32[1,8]{1,0:T(1,128)} %lens_ref.3, bf16[2048,256]{1,0:T(8,128)(2,1)} %fusion.18.q_ref, bf16[2048,512]{1,0:T(8,128)(2,1)} %bitcast.137, bf16[2048,256]{1,0:T(8,128)(2,1)} %get-tuple-element.40.o_ref, ...), custom_call_target="tpu_custom_call" | custom-call | flops 5368709120 | bytes 9437184 | tf_op jit(solution)/shard_map/attend_backward/pallas_call | solution.py:222
  395.9 5.6 convolution_convert_fusion.1
  401.5 118.2 %fold_kv_out.1 = (f32[256,512]{1,0:T(8,128)}, f32[64,2048]{1,0:T(8,128)}, f32[256,2048]{1,0:T(8,128)}) custom-call(bf16[1,4,2,256,512]{4,3,2,1,0:T(8,128)(2,1)} %bitcast.119, bf16[4,4,2,64,2048]{4,3,2,1,0:T(8,128)(2,1)} %bitcast.110, bf16[4,256,2048]{2,1,0:T(8,128)(2,1)} %bitcast.117), custom_call_target="tpu_custom_call" | custom-call | bytes 300000000 | tf_op jit(solution)/shard_map/fold_kv_out/pallas_call | solution.py:664
  519.8 1.6 slice.106
  521.4 1.7 slice.91
  523.8 1.8 broadcast_multiply_fusion
  526.1 1.4 copy-done.4
  527.5 1.4 fusion.20
  528.9 1.7 copy.42
  530.6 1.8 copy.39
  532.4 1.0 broadcast_multiply_fusion.1
  534.1 1.8 copy.40
  535.9 1.7 subtract_convert_fusion
  537.6 1.0 copy.41
  538.6 9.2 %fusion.8 = (bf16[2048]{0:T(1024)(128)(2,1)S(1)}, f32[256]{0:T(256)S(1)}, f32[256,2048]{1,0:T(8,128)}) fusion(bf16[1,256,2048]{2,1,0:T(8,128)(2,1)S(1)} %copy-done, f32[256]{0:T(256)} %copy-done.19, f32[2048]{0:T(1024)S(1)} %reshape.237, bf16[2048,2560]{1,0:T(8,128)(2,1)} %bitcast.133, bf16[256,256]{1,0:T(8,128)(2,1)S(1)} %copy-done.16, ...), kind=kOutput, calls=%fused_computation.15 | convolution fusion | flops 2691954432 | bytes 14956544 | tf_op jit(solution)/shard_map/ht,dh->td/dot_general | solution.py:1136
  548.8 3.0 fusion.23
  551.8 1.9 fusion.13
  553.7 7.1 %convolution_convert_fusion = bf16[2048,2560]{1,0:T(8,128)(2,1)} fusion(bf16[1,256,2048]{2,1,0:T(8,128)(2,1)S(1)} %copy-done, f32[2048]{0:T(1024)S(1)} %reshape.237, f32[256]{0:T(256)S(1)} %copy-done.20, bf16[256,256]{1,0:T(8,128)(2,1)S(1)} %copy-done.16, bf16[256,256]{1,0:T(8,128)(2,1)S(1)} %copy.41, bf16[2048,256]{1,0:T(8,128)(2,1)S(1)} %copy-done.8), kind=kOutput, calls=%fused_computation | convolution fusion | flops 2695626752 | bytes 12854272 | tf_op jit(solution)/shard_map/td,ht->dh/dot_general | solution.py:1135
  560.8 93.3 %fold_qkv.1 = (f32[64,2560]{1,0:T(8,128)}, f32[16,128]{1,0:T(8,128)}, f32[64,5632]{1,0:T(8,128)}, f32[64,5632]{1,0:T(8,128)}) custom-call(bf16[4,4,2,64,2560]{4,3,2,1,0:T(8,128)(2,1)} %bitcast.109, bf16[4,4,2,16,128]{4,3,2,1,0:T(8,128)(2,1)} %bitcast.129, bf16[4,64,1408]{2,1,0:T(8,128)(2,1)} %reduce-scatter.4.cloned.1.call-done.refs_2_, ...), custom_call_target="tpu_custom_call" | custom-call | bytes 240000000 | tf_op jit(solution)/shard_map/fold_qkv/pallas_call | solution.py:664
  654.1 2.0 slice.78
  656.1 1.3 slice_bitcast_fusion
  657.5 1.5 fusion.37
  659.0 2.4 convert_element_type.138
  661.4 0.8 copy.54
  662.2 1.1 copy.55
  663.3 1.1 copy.56
  (106 shorter events, 15.5 us)
Async XLA Ops:
  7.2 91.1 %all-gather.4.cloned.1.call-start = ((), (), s32[]{:S(2)}) async-start(), calls=%async_computation.3 | async-start | bytes 6488064 | tf_op jit(solution)/shard_map/all_gather | solution.py:978
  7.9 249.7 %all-gather.6.cloned.1.call-start = ((), (), s32[]{:S(2)}) async-start(), calls=%async_computation.4 | async-start | bytes 6488064 | tf_op jit(solution)/shard_map/all_gather | solution.py:978
  13.6 87.2 %copy-start = (bf16[1,256,2048]{2,1,0:T(8,128)(2,1)S(1)}, bf16[1,256,2048]{2,1,0:T(8,128)(2,1)}, u32[]{:S(2)}) copy-start(bf16[1,256,2048]{2,1,0:T(8,128)(2,1)} %param.14) | copy-start | bytes 3145732
  98.3 173.4 %all-gather.8.cloned.1.call-start = ((), (), s32[]{:S(2)}) async-start(), calls=%async_computation.5 | async-start | bytes 6488064 | tf_op jit(solution)/shard_map/all_gather | solution.py:978
  99.0 461.8 %reduce-scatter.4.cloned.1.call-start = ((), (), s32[]{:S(2)}) async-start(), calls=%async_computation.6 | async-start | bytes 6488064 | tf_op jit(solution)/shard_map/reduce_scatter | solution.py:982
  101.7 6.0 copy-start.19
  107.7 1.6 copy-start.5
  109.3 0.7 copy-start.27
  109.3 1.3 copy-start.28
  120.8 2.0 copy-start.6
  122.7 1.4 copy-start.14
  122.7 1.4 copy-start.15
  122.7 1.4 copy-start.18
  122.7 2.2 copy-start.9
  122.7 2.2 copy-start.23
  255.8 0.6 copy-start.21
  367.1 193.7 %reduce-scatter.6.cloned.1.call-start = ((), (), s32[]{:S(2)}) async-start(), calls=%async_computation.7 | async-start | bytes 6488064 | tf_op jit(solution)/shard_map/reduce_scatter | solution.py:982
  367.7 291.3 %reduce-scatter.8.cloned.1.call-start = ((), (), s32[]{:S(2)}) async-start(), calls=%async_computation.8 | async-start | bytes 6488064 | tf_op jit(solution)/shard_map/reduce_scatter | solution.py:982
  368.3 2.9 copy-start.3
  368.3 2.9 copy-start.10
  368.3 2.9 copy-start.22
  368.3 2.9 copy-start.24
  368.4 2.9 copy-start.26
  371.9 24.0 %copy-start.1 = (f32[256,2048]{1,0:T(8,128)}, f32[256,2048]{1,0:T(8,128)S(1)}, u32[]{:S(2)}) copy-start(f32[256,2048]{1,0:T(8,128)S(1)} %fusion.21) | copy-start | bytes 6291460
  379.7 16.2 %copy-start.7 = (bf16[2048,256]{1,0:T(8,128)(2,1)S(1)}, bf16[2048,256]{1,0:T(8,128)(2,1)}, u32[]{:S(2)}) copy-start(bf16[2048,256]{1,0:T(8,128)(2,1)} %get-tuple-element.40.o_ref) | copy-start | bytes 3145732
  525.9 1.7 copy-start.4
  533.4 5.3 copy-start.16
  548.8 3.0 copy-start.2
  548.8 3.0 copy-start.11
  548.8 3.0 copy-start.20
  548.8 3.0 copy-start.25
  551.8 2.0 copy-start.8
  654.1 7.3 %copy-start.17 = (f32[64,2048]{1,0:T(8,128)S(1)}, f32[64,2048]{1,0:T(8,128)}, u32[]{:S(2)}) copy-start(f32[64,2048]{1,0:T(8,128)} %get-tuple-element.111) | copy-start | bytes 1572868
  654.1 8.1 %copy-start.13 = (f32[64,5632]{1,0:T(8,128)S(1)}, f32[64,5632]{1,0:T(8,128)}, u32[]{:S(2)}) copy-start(f32[64,5632]{1,0:T(8,128)} %get-tuple-element.113) | copy-start | bytes 4325380
  661.4 1.9 copy-start.12
Sparse Core Ops, SparseCore 0:
  9.7 87.4 all-gather.3
  98.8 110.7 all-gather.5
  211.1 60.5 all-gather.7
  367.3 64.9 reduce-scatter.3
  434.4 92.6 reduce-scatter.5
  529.3 70.0 reduce-scatter.7

commit v4 on v1

--- a/solution.py
+++ b/solution.py
@@ -242,7 +242,1180 @@
     )(place, block_order, doc_lengths, q_t, kv, o_t, lse, do_t)
 
 
-EVERY = ("seq", "ctx")
+MESH = pl.DeviceIdType.MESH
+
+
+def coords():
+    ctx = lax.axis_index("ctx")
+    return lax.axis_index("seq"), ctx // 2, lax.rem(ctx, 2)
+
+
+def other(place, step, count):
+    return lax.rem(place + step, count)
+
+
+def meet(devices):
+    barrier = pltpu.get_barrier_semaphore()
+    for device in devices:
+        pl.semaphore_signal(barrier, inc=1, device_id=device, device_id_type=MESH)
+    pl.semaphore_wait(barrier, len(devices))
+
+
+def remote(source, target, send_sem, recv_sem, device):
+    return pltpu.make_async_remote_copy(
+        src_ref=source,
+        dst_ref=target,
+        send_sem=send_sem,
+        recv_sem=recv_sem,
+        device_id=device,
+        device_id_type=MESH,
+    )
+
+
+def plane_slots(seq_count):
+    seq = lax.axis_index("seq")
+    if seq_count == 4:
+        beside, above = seq + 1 - 2 * lax.rem(seq, 2), other(seq, 2, 4)
+        return [seq, beside, above, 3 - seq], [0, 1, 2, 3]
+    return [seq] + [other(seq, step, seq_count) for step in range(1, seq_count)], [0] + [
+        seq_count - step for step in range(1, seq_count)
+    ]
+
+
+def spread_kernel(scopes, halves, seq_count, chip_count, *refs):
+    count = len(scopes)
+    sources, results = refs[:count], refs[count : 2 * count]
+    sends, recvs, local_sem = refs[2 * count : 3 * count], refs[3 * count : 4 * count], refs[4 * count]
+    _, chip, core = coords()
+    ctx = lax.axis_index("ctx")
+    ctx_count = 2 * chip_count
+    slots, _ = plane_slots(seq_count)
+    seq, planes = slots[0], slots[1:]
+    sibling = {"ctx": chip * 2 + 1 - core}
+    last = chip_count - 1
+    sides = [
+        (chip < last, {"ctx": lax.rem(chip + 1, chip_count) * 2 + core}),
+        (chip > 0, {"ctx": lax.rem(chip + last, chip_count) * 2 + core}),
+    ]
+    use_lines = any(scope in ("ctx", "all") for scope in scopes)
+    peers = []
+    if any(scope != "ctx" for scope in scopes):
+        peers += [{"seq": place} for place in planes]
+    if use_lines:
+        peers += [{"ctx": other(chip, step, chip_count) * 2 + core} for step in range(1, chip_count)]
+        peers += [sibling]
+    meet(peers)
+
+    started = []
+
+    def part(ref, item, half):
+        if half is None:
+            return ref
+        rows = results[item].shape[-2] // 2
+        return ref.at[pl.ds(half * rows, rows)]
+
+    def block(item, at_seq, place, at_core):
+        scope = scopes[item]
+        at_ctx = place * 2 + at_core
+        if scope == "all":
+            return results[item].at[at_seq, at_ctx], at_seq * ctx_count + at_ctx
+        if scope == "ctx":
+            return results[item].at[at_ctx], at_ctx
+        return results[item].at[at_seq], at_seq
+
+    def descriptor(item, at_seq, place, half, kind, device, source=None):
+        target, number = block(item, at_seq, place, core)
+        row = place if scopes[item] in ("ctx", "all") else 0
+        return remote(
+            part(target if source is None else source, item, half),
+            part(target, item, half),
+            sends[item].at[row, kind],
+            recvs[item].at[2 * number + (half or 0)],
+            device,
+        )
+
+    def arrival(item, at_seq, place, half, at_core=None):
+        target, number = block(item, at_seq, place, core if at_core is None else at_core)
+        view = part(target, item, half)
+        return remote(
+            view, view, sends[item].at[0, 0], recvs[item].at[2 * number + (half or 0)], sibling
+        )
+
+    def start(copies, there=None):
+        for copy in copies:
+            copy.start()
+            started.append((there, copy))
+
+    def cut(item):
+        return (0, 1) if halves[item] else (None,)
+
+    def plane_copies(item, place, half, source=None):
+        if not halves[item]:
+            return [
+                descriptor(item, seq, place, None, 4 + number, {"seq": to}, source)
+                for number, to in enumerate(planes)
+            ]
+        order = (1, 2) if half == 0 else (2, 1)
+        return [
+            descriptor(item, seq, place, half, 2 + 2 * half + to + 1, {"seq": slots[to]}, source)
+            for to in order
+        ]
+
+    kinds_relay = 4 + max(4, seq_count - 1)
+
+    def plane_relay(item, place, there=None):
+        if not halves[item]:
+            return
+        steps = [
+            (
+                arrival(item, slots[give], place, half),
+                descriptor(
+                    item, slots[give], place, half, kinds_relay + half, {"seq": slots[3 - give]}
+                ),
+            )
+            for give, half in ((1, 0), (2, 1))
+        ]
+
+        def run():
+            for got, copy in steps:
+                got.wait_recv()
+                start([copy], there)
+
+        run() if there is None else pl.when(there)(run)
+
+    def plane_end(item, place, there=None):
+        if halves[item]:
+            ends = [
+                (arrival(item, slots[slot], place, half))
+                for slot, half in ((1, 1), (2, 0), (3, 0), (3, 1))
+            ]
+        else:
+            ends = [arrival(item, at_seq, place, None) for at_seq in planes]
+        copies = []
+        if scopes[item] == "all":
+            copies = [
+                descriptor(item, at_seq, place, None, kinds_relay + 3 + number, sibling)
+                for number, at_seq in enumerate(planes)
+            ]
+
+        def run():
+            for got in ends:
+                got.wait_recv()
+            start(copies, there)
+
+        run() if there is None else pl.when(there)(run)
+
+    items = range(count)
+    lines = [item for item in items if scopes[item] in ("ctx", "all")]
+    flats = [item for item in items if scopes[item] in ("seq", "all")]
+    everywhere = [item for item in items if scopes[item] == "all"]
+    swaps = [item for item in items if scopes[item] == "swap"]
+    locals_ = []
+    for item in items:
+        target, _ = block(item, seq, chip, core)
+        own = sources[item].at[seq] if scopes[item] == "swap" else sources[item]
+        copy = pltpu.make_async_copy(own, target, local_sem.at[item])
+        copy.start()
+        locals_.append(copy)
+    for item in lines:
+        for half in cut(item):
+            for side, (there, device) in enumerate(sides):
+                copy = descriptor(
+                    item, seq, chip, half, 2 * side + (half or 0), device, sources[item]
+                )
+                pl.when(there)(functools.partial(start, [copy], there))
+    for item in swaps:
+        start(
+            [
+                descriptor(item, seq, chip, None, number, {"seq": place}, sources[item].at[place])
+                for number, place in enumerate(planes)
+            ]
+        )
+    for item in flats:
+        for half in cut(item):
+            start(plane_copies(item, chip, half, sources[item]))
+    for item in lines:
+        start([descriptor(item, seq, chip, None, kinds_relay + 2, sibling, sources[item])])
+    for item in flats:
+        plane_relay(item, chip)
+
+    def pass_on(item, place, there, onward, device):
+        steps = []
+        for half in cut(item):
+            steps.append(
+                (
+                    arrival(item, seq, place, half),
+                    descriptor(item, seq, place, half, half or 0, device),
+                    plane_copies(item, place, half) if scopes[item] == "all" else [],
+                )
+            )
+        final = descriptor(item, seq, place, None, kinds_relay + 2, sibling)
+
+        def run():
+            for got, copy, copies in steps:
+                got.wait_recv()
+                pl.when(onward)(copy.start)
+                start(copies, there)
+            start([final], there)
+
+        pl.when(there)(run)
+        for _, copy, _ in steps:
+            started.append((there & onward, copy))
+
+    waves = []
+    for step in range(1, chip_count):
+        wave = [
+            (lax.rem(chip + chip_count - step, chip_count), chip >= step, *sides[0]),
+            (lax.rem(chip + step, chip_count), chip <= last - step, *sides[1]),
+        ]
+        for place, there, onward, device in wave:
+            for item in lines:
+                pass_on(item, place, there, onward, device)
+        for item in everywhere:
+            for place, there, _, _ in waves[-1] if waves else []:
+                plane_relay(item, place, there)
+        if step == 1:
+            for item in flats:
+                plane_end(item, chip)
+        elif step > 2:
+            for item in everywhere:
+                for place, there, _, _ in waves[-2]:
+                    plane_end(item, place, there)
+        waves.append(wave)
+    for item in everywhere:
+        for place, there, _, _ in waves[-1]:
+            plane_relay(item, place, there)
+        for wave in waves[-2:]:
+            for place, there, _, _ in wave:
+                plane_end(item, place, there)
+    for item in swaps:
+        for place in planes:
+            arrival(item, place, chip, None).wait_recv()
+    for item in lines:
+        for at_seq in [seq] + (planes if scopes[item] == "all" else []):
+            for step in range(chip_count):
+                arrival(item, at_seq, other(chip, step, chip_count), None, 1 - core).wait_recv()
+    for copy in locals_:
+        copy.wait()
+    for there, copy in started:
+        if there is None:
+            copy.wait_send()
+        else:
+            pl.when(there)(copy.wait_send)
+
+
+def spread(name, collective_id, arrays, scopes, micros):
+    seq_count, ctx_count = lax.axis_size("seq"), lax.axis_size("ctx")
+    chip_count = ctx_count // 2
+    shapes, send_sems, recv_sems, halves = [], [], [], []
+    kinds = 4 + max(4, seq_count - 1) + 3 + seq_count - 1
+    for array, scope in zip(arrays, scopes):
+        lead = {"all": (seq_count, ctx_count), "ctx": (ctx_count,)}.get(scope, (seq_count,))
+        halves.append(seq_count == 4 and scope in ("all", "seq") and array.shape[0] % 32 == 0)
+        shape = array.shape if scope == "swap" else lead + array.shape
+        shapes.append(jax.ShapeDtypeStruct(shape, array.dtype))
+        rows = chip_count if scope in ("all", "ctx") else 1
+        send_sems.append(pltpu.SemaphoreType.DMA((rows, kinds)))
+        recv_sems.append(pltpu.SemaphoreType.DMA((2 * math.prod(lead),)))
+    anywhere = pl.BlockSpec(memory_space=pl.ANY)
+    return pl.pallas_call(
+        functools.partial(spread_kernel, scopes, tuple(halves), seq_count, chip_count),
+        out_shape=tuple(shapes),
+        in_specs=[anywhere] * len(arrays),
+        out_specs=(anywhere,) * len(arrays),
+        scratch_shapes=send_sems + recv_sems + [pltpu.SemaphoreType.DMA((len(arrays),))],
+        compiler_params=pltpu.CompilerParams(collective_id=collective_id, has_side_effects=True),
+        cost_estimate=pl.CostEstimate(
+            flops=0, transcendentals=0, bytes_accessed=int(micros * 3_000_000)
+        ),
+        name=name,
+    )(*arrays)
+
+
+FOLD_SCRATCH = 9
+WINDOW = 4
+
+
+def fold_kernel(kinds, chunk_counts, swap_count, work, seq_count, chip_count, *refs):
+    count = len(kinds)
+    every = count + swap_count
+    sources, swap_sources = refs[:count], refs[count:every]
+    extra_in, extra_out = (work[0], work[1]) if work else (0, 0)
+    first_out = every + extra_in
+    results = refs[first_out : first_out + count]
+    swap_results = refs[first_out + count : first_out + every]
+    first_rest = first_out + every + extra_out
+    rest = refs[first_rest:]
+    swap_rest = rest[count * FOLD_SCRATCH : count * FOLD_SCRATCH + 4 * swap_count]
+    extra = (
+        refs[every:first_out],
+        refs[first_out + every : first_rest],
+        rest[count * FOLD_SCRATCH + 4 * swap_count :],
+    )
+    seq, chip, core = coords()
+    slots, there = plane_slots(seq_count)
+    planes = slots[1:]
+    chips = [other(chip, step, chip_count) for step in range(1, chip_count)]
+    sibling = {"ctx": chip * 2 + 1 - core}
+    peers = []
+    if any(kind != "seq" for kind in kinds):
+        peers += [{"ctx": place * 2 + core} for place in chips] + [sibling]
+    if swap_count or any(kind != "ctx" for kind in kinds):
+        peers += [{"seq": place} for place in planes]
+
+    def scratch(item):
+        return rest[item * FOLD_SCRATCH : (item + 1) * FOLD_SCRATCH]
+
+    def columns(item, chunk):
+        width = sources[item].shape[-1] // chunk_counts[item]
+        return slice(chunk * width, (chunk + 1) * width)
+
+    order = []
+    for chunk in range(max(chunk_counts, default=0)):
+        order += [(item, chunk) for item in range(count) if chunk < chunk_counts[item]]
+
+    loads = []
+    for item in range(count):
+        mine, sem_s = scratch(item)[0], scratch(item)[7]
+        if kinds[item] != "seq":
+            load = pltpu.make_async_copy(
+                sources[item].at[:, :, core], mine, sem_s.at[4, 0, 0]
+            )
+            load.start()
+            loads.append(load)
+    meet(peers)
+
+    waits = []
+
+    def go(source, target, send_sem, recv_sem, device):
+        copy = remote(source, target, send_sem, recv_sem, device)
+        copy.start()
+        waits.append(copy)
+        return copy
+
+    firsts = {}
+    for item, chunk in order:
+        if kinds[item] != "seq":
+            _, got1, _, _, _, _, _, sem_s, sem_r = scratch(item)
+            cols = columns(item, chunk)
+            firsts[item, chunk] = go(
+                sources[item].at[:, :, 1 - core, :, cols],
+                got1.at[:, :, :, cols],
+                sem_s.at[0, chunk, 0],
+                sem_r.at[0, chunk, 0],
+                sibling,
+            )
+    swapped = []
+    for item in range(swap_count):
+        got, sem_s, sem_r, sem_own = swap_rest[4 * item : 4 * item + 4]
+        own = pltpu.make_async_copy(swap_sources[item].at[seq], got.at[seq], sem_own)
+        own.start()
+        swapped.append(own)
+        for step, place in enumerate(planes):
+            go(swap_sources[item].at[place], got.at[seq], sem_s.at[step], sem_r.at[seq], {"seq": place})
+    for load in loads:
+        load.wait()
+
+    def block(item, slot, cols):
+        if kinds[item] == "seq":
+            return sources[item][slot, :, cols].astype(F32)[None]
+        mine, got1 = scratch(item)[:2]
+        place = slots[slot] if kinds[item] == "all" else 0
+        return mine[place, :, :, cols].astype(F32) + got1[place, :, :, cols].astype(F32)
+
+    def turn(chunk):
+        return (1, 2) if chunk % 2 == 0 else (2, 1)
+
+    seconds = {}
+
+    def plane_first(item, chunk):
+        _, got1, _, got2, keep, _, _, sem_s, sem_r = scratch(item)
+        cols = columns(item, chunk)
+        if kinds[item] == "all":
+            firsts[item, chunk].wait_recv()
+        first, _ = turn(chunk)
+        targets = [(slot, slot) for slot in range(1, seq_count)]
+        if seq_count == 4:
+            targets = [(3, first), (first, first)]
+        row = []
+        for number, (slot, to) in enumerate(targets):
+            if kinds[item] == "all":
+                held = got1.at[slots[slot], :, :, cols]
+                held[...] = block(item, slot, cols).astype(BF16)
+            else:
+                held = sources[item].at[pl.ds(slot, 1), :, cols]
+            index = number if seq_count == 4 else there[slot] - 1
+            row.append(
+                go(
+                    held,
+                    got2.at[index, :, :, cols],
+                    sem_s.at[1, chunk, number],
+                    sem_r.at[1, chunk, index],
+                    {"seq": slots[to]},
+                )
+            )
+        seconds[item, chunk] = row
+        keep[:, :, cols] = block(item, 0, cols)
+
+    def plane_second(item, chunk):
+        if seq_count != 4:
+            return
+        _, got1, spare, got2, keep, _, _, sem_s, sem_r = scratch(item)
+        cols = columns(item, chunk)
+        _, second = turn(chunk)
+        across, mine = seconds[item, chunk]
+        across.wait_recv()
+        if kinds[item] == "all":
+            held = got1.at[slots[second], :, :, cols]
+        else:
+            held = spare.at[:, :, cols]
+        held[...] = (block(item, second, cols) + got2[0, :, :, cols].astype(F32)).astype(BF16)
+        last = go(
+            held,
+            got2.at[2, :, :, cols],
+            sem_s.at[2, chunk, 0],
+            sem_r.at[2, chunk, 0],
+            {"seq": slots[second]},
+        )
+        mine.wait_recv()
+        keep[:, :, cols] = keep[:, :, cols] + got2[1, :, :, cols].astype(F32)
+        seconds[item, chunk] = [last]
+
+    thirds = {}
+
+    def line(item, chunk):
+        _, _, _, got2, keep, pass3, got3, sem_s, sem_r = scratch(item)
+        cols = columns(item, chunk)
+        if kinds[item] == "ctx":
+            firsts[item, chunk].wait_recv()
+            keep[:, :, cols] = block(item, 0, cols)
+        else:
+            for copy in seconds[item, chunk]:
+                copy.wait_recv()
+
+        def total(place):
+            value = keep[place, :, cols]
+            if kinds[item] != "ctx":
+                for index in (2,) if seq_count == 4 else range(seq_count - 1):
+                    value = value + got2[index, place, :, cols].astype(F32)
+            return value
+
+        if kinds[item] == "seq":
+            results[item][:, cols] = total(0)
+            return
+        row = []
+        for step, place in enumerate(chips):
+            pass3[step, :, cols] = total(place).astype(BF16)
+            row.append(
+                go(
+                    pass3.at[step, :, cols],
+                    got3.at[step, :, cols],
+                    sem_s.at[3, chunk, step],
+                    sem_r.at[3, chunk, step],
+                    {"ctx": place * 2 + core},
+                )
+            )
+        results[item][:, cols] = total(chip)
+        thirds[item, chunk] = row
+
+    lines = [step for step in order if kinds[step[0]] == "ctx"]
+    everywhere = [step for step in order if kinds[step[0]] == "all"]
+    flats = [step for step in order if kinds[step[0]] == "seq"]
+    for step in lines:
+        line(*step)
+    for step in everywhere[:WINDOW]:
+        plane_first(*step)
+    for number, step in enumerate(everywhere):
+        plane_second(*step)
+        for later in everywhere[number + WINDOW : number + WINDOW + 1]:
+            plane_first(*later)
+        if number:
+            line(*everywhere[number - 1])
+    for step in flats:
+        plane_first(*step)
+    if work:
+        work[2](*extra)
+    for step in everywhere[-1:]:
+        line(*step)
+    for step in flats:
+        plane_second(*step)
+    for step in flats:
+        line(*step)
+    for item, chunk in lines + everywhere:
+        got3 = scratch(item)[6]
+        cols = columns(item, chunk)
+        for copy in thirds[item, chunk]:
+            copy.wait_recv()
+        value = results[item][:, cols]
+        for step in range(chip_count - 1):
+            value = value + got3[step, :, cols].astype(F32)
+        results[item][:, cols] = value
+    if work:
+        work[3](results[0], *extra)
+    for item in range(swap_count):
+        got, sem_s, sem_r, _ = swap_rest[4 * item : 4 * item + 4]
+        swapped[item].wait()
+        for place in planes:
+            remote(got.at[place], got.at[place], sem_s.at[0], sem_r.at[place], sibling).wait_recv()
+        width = got.shape[-1]
+        for place in range(seq_count):
+            swap_results[item][:, place * width : (place + 1) * width] = got[place].astype(F32)
+    for copy in waits:
+        copy.wait_send()
+
+
+def fold(name, collective_id, arrays, kinds, chunk_counts, micros, swaps=(), work=None):
+    seq_count, ctx_count = lax.axis_size("seq"), lax.axis_size("ctx")
+    chip_count = ctx_count // 2
+    inputs, shapes, scratch, in_specs = [], [], [], []
+    small = (1, 1, 8, 128)
+    dma = pltpu.SemaphoreType.DMA
+    for array, kind, chunks in zip(arrays, kinds, chunk_counts):
+        parts = 1 if kind == "ctx" else seq_count
+        blocks = seq_count if kind == "seq" else parts * ctx_count
+        rows, cols = array.shape[0] // blocks, array.shape[1]
+        lines = 1 if kind == "seq" else chip_count
+        if kind == "seq":
+            inputs.append(array.reshape(seq_count, rows, cols))
+            in_specs.append(vmem())
+            got1, spare = small, (1, rows, cols)
+        else:
+            inputs.append(array.reshape(parts, chip_count, 2, rows, cols))
+            in_specs.append(pl.BlockSpec(memory_space=pl.ANY))
+            got1, spare = (parts, chip_count, rows, cols), small[1:]
+        shapes.append(jax.ShapeDtypeStruct((rows, cols), F32))
+        got2 = small if kind == "ctx" else (seq_count - 1, lines, rows, cols)
+        got3 = small[1:] if kind == "seq" else (chip_count - 1, rows, cols)
+        most = max(seq_count, chip_count)
+        scratch += [
+            pltpu.VMEM(got1, BF16),
+            pltpu.VMEM(got1, BF16),
+            pltpu.VMEM(spare, BF16),
+            pltpu.VMEM(got2, BF16),
+            pltpu.VMEM((lines, rows, cols), F32),
+            pltpu.VMEM(got3, BF16),
+            pltpu.VMEM(got3, BF16),
+            dma((5, chunks, most)),
+            dma((4, chunks, most)),
+        ]
+    for array in swaps:
+        inputs.append(array)
+        in_specs.append(pl.BlockSpec(memory_space=pl.ANY))
+        shapes.append(jax.ShapeDtypeStruct((array.shape[1], seq_count * array.shape[2]), F32))
+        scratch += [
+            pltpu.VMEM(array.shape, BF16),
+            dma((seq_count - 1,)),
+            dma((seq_count,)),
+            dma,
+        ]
+    out_specs = [vmem()] * len(inputs)
+    does = None
+    if work:
+        does = (len(work["inputs"]), len(work["shapes"]), work["during"], work["after"])
+        inputs += work["inputs"]
+        in_specs += work["in_specs"]
+        shapes += work["shapes"]
+        out_specs += work["out_specs"]
+        scratch += work["scratch"]
+    return pl.pallas_call(
+        functools.partial(
+            fold_kernel, tuple(kinds), tuple(chunk_counts), len(swaps), does, seq_count, chip_count
+        ),
+        out_shape=tuple(shapes),
+        in_specs=in_specs,
+        out_specs=tuple(out_specs),
+        scratch_shapes=scratch,
+        compiler_params=pltpu.CompilerParams(
+            collective_id=collective_id, has_side_effects=True, vmem_limit_bytes=VMEM_MOST
+        ),
+        cost_estimate=pl.CostEstimate(
+            flops=0, transcendentals=0, bytes_accessed=int(micros * 3_000_000)
+        ),
+        name=name,
+    )(*inputs)
+
+
+def tiles(extent, width, visit):
+    whole = extent // width
+
+    @pl.loop(0, whole)
+    def _(number):
+        visit(pl.ds(pl.multiple_of(number * width, width), width))
+
+    if extent % width:
+        visit(pl.ds(whole * width, extent % width))
+
+
+def stream_rows(extent, width, produce, stage, sem, target):
+    whole = extent // width
+
+    def leave(slot, rows, size):
+        return pltpu.make_async_copy(
+            stage.at[slot, pl.ds(0, size)], target.at[rows], sem.at[slot]
+        )
+
+    @pl.loop(0, whole)
+    def _(number):
+        slot = lax.rem(number, 2)
+        rows = pl.ds(pl.multiple_of(number * width, width), width)
+
+        @pl.when(number >= 2)
+        def _():
+            leave(slot, rows, width).wait()
+
+        stage[slot] = produce(rows).astype(stage.dtype)
+        leave(slot, rows, width).start()
+
+    for number in range(max(0, whole - 2), whole):
+        leave(number % 2, pl.ds(number * width, width), width).wait()
+    if extent % width:
+        size = extent % width
+        rows = pl.ds(whole * width, size)
+        stage[0, :size] = produce(rows).astype(stage.dtype)
+        leave(0, rows, size).start()
+        leave(0, rows, size).wait()
+
+
+def ffn_first_kernel(
+    seq_count, f_ref, g_ref, wg_ref, wd_ref, f_out, g_out, gate_ref, gh_ref, f_s, g_s, wg, wd, in_sem, f_send, f_recv, out_sem
+):
+    rows = f_ref.shape[0]
+    width = wg.shape[1]
+    places, there = plane_slots(seq_count)
+    load_f = pltpu.make_async_copy(f_ref, f_s.at[pl.ds(0, rows)], in_sem.at[seq_count])
+    load_wd = pltpu.make_async_copy(wd_ref, wd, in_sem.at[seq_count + 1])
+    load_wg = pltpu.make_async_copy(wg_ref, wg, in_sem.at[seq_count + 2])
+    loads = [load_wd]
+    for slot in range(seq_count):
+        loads.append(
+            pltpu.make_async_copy(
+                g_ref.at[places[slot]], g_s.at[pl.ds(slot * rows, rows)], in_sem.at[slot]
+            )
+        )
+    for load in [*loads, load_f, load_wg]:
+        load.start()
+    meet([{"seq": place} for place in places[1:]])
+
+    started = []
+
+    def f_block(slot, half):
+        if half is None:
+            return f_s.at[pl.ds(slot * rows, rows)]
+        return f_s.at[pl.ds(slot * rows + half * (rows // 2), rows // 2)]
+
+    def f_copy(source, to, slot, half):
+        copy = remote(
+            source,
+            f_block(slot, half),
+            f_send.at[len(started)],
+            f_recv.at[slot, half or 0],
+            {"seq": places[to]},
+        )
+        copy.start()
+        started.append(copy)
+
+    def f_arrive(slot, half):
+        block = f_block(slot, half)
+        remote(
+            block, block, f_send.at[0], f_recv.at[slot, half or 0], {"seq": places[1]}
+        ).wait_recv()
+
+    if seq_count == 4:
+        for half in (0, 1):
+            source = f_ref.at[pl.ds(half * (rows // 2), rows // 2)]
+            for to in (1, 2) if half == 0 else (2, 1):
+                f_copy(source, to, to, half)
+    else:
+        for to in range(1, seq_count):
+            f_copy(f_ref, to, there[to], None)
+
+    def gate_rows(first, count):
+        own = slice(first, first + count)
+
+        def visit(cols):
+            gate_ref[own, cols] = dot32(f_s[own, :], wg[:, cols], ((1,), (0,)))
+
+        tiles(width, 256, visit)
+
+    for load in loads:
+        load.wait()
+    leave_g = pltpu.make_async_copy(g_s, g_out, out_sem.at[1])
+    leave_g.start()
+
+    def grad_hidden(cols):
+        gh_ref[:, cols] = dot32(g_s[...], wd[cols, :], ((1,), (1,))).astype(gh_ref.dtype)
+
+    tiles(width, 256, grad_hidden)
+    for load in (load_f, load_wg):
+        load.wait()
+    gate_rows(0, rows)
+    if seq_count == 4:
+        f_arrive(1, 0)
+        f_copy(f_block(1, 0), 2, 3, 0)
+        f_arrive(2, 1)
+        f_copy(f_block(2, 1), 1, 3, 1)
+        f_arrive(1, 1)
+        f_arrive(2, 0)
+        gate_rows(rows, 2 * rows)
+        f_arrive(3, 0)
+        f_arrive(3, 1)
+        leave = pltpu.make_async_copy(f_s, f_out, out_sem.at[0])
+        leave.start()
+        gate_rows(3 * rows, rows)
+    else:
+        for slot in range(1, seq_count):
+            f_arrive(slot, None)
+        leave = pltpu.make_async_copy(f_s, f_out, out_sem.at[0])
+        leave.start()
+        gate_rows(rows, (seq_count - 1) * rows)
+    leave.wait()
+    leave_g.wait()
+    for copy in started:
+        copy.wait_send()
+
+
+def ffn_act_kernel(
+    f_ref, gate_ref, gh_ref, wu_ref, hid, gg, gu, pg_ref, f_s, gate_s, gh_s, wu, stage_f, in_sem, leave_sem
+):
+    model, width = wu.shape
+    loads = [
+        pltpu.make_async_copy(source, target, in_sem.at[number])
+        for number, (source, target) in enumerate(
+            [(f_ref, f_s), (wu_ref, wu), (gate_ref, gate_s), (gh_ref, gh_s)]
+        )
+    ]
+    for load in loads:
+        load.start()
+    for load in loads:
+        load.wait()
+
+    def act(cols):
+        up_val = dot32(f_s[...], wu[:, cols], ((1,), (0,)))
+        gate = gate_s[:, cols]
+        grad = gh_s[:, cols].astype(F32)
+        sigma = jax.nn.sigmoid(gate)
+        activated = gate * sigma
+        hid[:, cols] = (activated * up_val).astype(BF16)
+        gg[:, cols] = (grad * up_val * (sigma + activated * (1.0 - sigma))).astype(BF16)
+        gu[:, cols] = (grad * activated).astype(BF16)
+
+    tiles(width, 256, act)
+    stream_rows(
+        model,
+        256,
+        lambda own: dot32(f_s[:, own], gg[...], ((0,), (0,))),
+        stage_f,
+        leave_sem,
+        pg_ref,
+    )
+
+
+def ffn_grad_kernel(
+    seq_count,
+    f_ref,
+    hid_ref,
+    gg_ref,
+    gu_ref,
+    g_ref,
+    wg_ref,
+    wu_ref,
+    wd_ref,
+    gf_ref,
+    out_ref,
+    pu_ref,
+    pd_ref,
+    f_s,
+    g_s,
+    hid,
+    gg,
+    gu,
+    wg,
+    wu,
+    wd,
+    parts,
+    got,
+    stage_f,
+    stage_d,
+    in_sem,
+    x_send,
+    x_recv,
+    leave_sem,
+):
+    rows = gf_ref.shape[0]
+    model, width = wg.shape
+    places, there = plane_slots(seq_count)
+    loads = [
+        pltpu.make_async_copy(source, target, in_sem.at[number])
+        for number, (source, target) in enumerate(
+            [
+                (gg_ref, gg),
+                (gu_ref, gu),
+                (wg_ref, wg),
+                (wu_ref, wu),
+                (f_ref, f_s),
+                (hid_ref, hid),
+                (g_ref, g_s),
+                (wd_ref, wd),
+            ]
+        )
+    ]
+    for load in loads:
+        load.start()
+    meet([{"seq": place} for place in places[1:]])
+    for load in loads[:4]:
+        load.wait()
+
+    def part_copy(slot, cols):
+        return remote(
+            parts.at[pl.ds((slot - 1) * rows, rows), cols],
+            got.at[there[slot] - 1, :, cols],
+            x_send.at[slot],
+            x_recv.at[there[slot]],
+            {"seq": places[slot]},
+        )
+
+    def grad_f(cols):
+        part = dot32(gg[...], wg[cols, :], ((1,), (1,))) + dot32(gu[...], wu[cols, :], ((1,), (1,)))
+        gf_ref[:, cols] = part[:rows]
+        parts[:, cols] = part[rows:].astype(BF16)
+        for slot in range(1, seq_count):
+            part_copy(slot, cols).start()
+
+    tiles(model, 256, grad_f)
+    for load in loads[4:]:
+        load.wait()
+    stream_rows(
+        model,
+        256,
+        lambda own: dot32(f_s[:, own], gu[...], ((0,), (0,))),
+        stage_f,
+        leave_sem.at[0],
+        pu_ref,
+    )
+    stream_rows(
+        width,
+        256,
+        lambda own: dot32(hid[:, own], g_s[...], ((0,), (0,))),
+        stage_d,
+        leave_sem.at[2],
+        pd_ref,
+    )
+
+    def out_copy(cols):
+        return pltpu.make_async_copy(f_s.at[:, cols], out_ref.at[:, cols], leave_sem.at[1, 0])
+
+    def out_part(cols):
+        f_s[:, cols] = dot32(hid[...], wd[:, cols], ((1,), (0,))).astype(BF16)
+        out_copy(cols).start()
+
+    tiles(model, 256, out_part)
+    everything = pl.ds(0, model)
+    out_copy(everything).wait()
+    for slot in range(1, seq_count):
+        part_copy(slot, everything).wait_recv()
+    total = gf_ref[...]
+    for slot in range(seq_count - 1):
+        total = total + got[slot].astype(F32)
+    gf_ref[...] = total
+    for slot in range(1, seq_count):
+        part_copy(slot, everything).wait_send()
+
+
+def ffn_first(collective_id, f_norm, g_all, w_gate, w_down):
+    seq_count = lax.axis_size("seq")
+    rows, model = f_norm.shape
+    width = w_gate.shape[1]
+    count = seq_count * rows
+    anywhere = pl.BlockSpec(memory_space=pl.ANY)
+    dma = pltpu.SemaphoreType.DMA
+    return pl.pallas_call(
+        functools.partial(ffn_first_kernel, seq_count),
+        out_shape=(
+            jax.ShapeDtypeStruct((count, model), BF16),
+            jax.ShapeDtypeStruct((count, model), BF16),
+            jax.ShapeDtypeStruct((count, width), F32),
+            jax.ShapeDtypeStruct((count, width), BF16),
+        ),
+        in_specs=[anywhere] * 4,
+        out_specs=(anywhere, anywhere, vmem(), vmem()),
+        scratch_shapes=[
+            pltpu.VMEM((count, model), BF16),
+            pltpu.VMEM((count, model), BF16),
+            pltpu.VMEM((model, width), BF16),
+            pltpu.VMEM((width, model), BF16),
+            dma((seq_count + 3,)),
+            dma((max(6, seq_count),)),
+            dma((seq_count, 2)),
+            dma((2,)),
+        ],
+        compiler_params=pltpu.CompilerParams(
+            collective_id=collective_id, has_side_effects=True, vmem_limit_bytes=VMEM_MOST
+        ),
+        cost_estimate=pl.CostEstimate(
+            flops=8 * count * model * width,
+            transcendentals=0,
+            bytes_accessed=4 * (2 * width * model + 3 * count * model),
+        ),
+        name="ffn_first",
+    )(f_norm, g_all.reshape(seq_count, rows, model), w_gate, w_down)
+
+
+def ffn_act(f_all, gate, grad_hidden, w_up):
+    count, model = f_all.shape
+    width = w_up.shape[1]
+    anywhere = pl.BlockSpec(memory_space=pl.ANY)
+    dma = pltpu.SemaphoreType.DMA
+    return pl.pallas_call(
+        ffn_act_kernel,
+        out_shape=(
+            jax.ShapeDtypeStruct((count, width), BF16),
+            jax.ShapeDtypeStruct((count, width), BF16),
+            jax.ShapeDtypeStruct((count, width), BF16),
+            jax.ShapeDtypeStruct((model, width), BF16),
+        ),
+        in_specs=[anywhere] * 4,
+        out_specs=(vmem(), vmem(), vmem(), anywhere),
+        scratch_shapes=[
+            pltpu.VMEM((count, model), BF16),
+            pltpu.VMEM((count, width), F32),
+            pltpu.VMEM((count, width), BF16),
+            pltpu.VMEM((model, width), BF16),
+            pltpu.VMEM((2, 256, width), BF16),
+            dma((4,)),
+            dma((2,)),
+        ],
+        compiler_params=pltpu.CompilerParams(vmem_limit_bytes=VMEM_MOST),
+        cost_estimate=pl.CostEstimate(
+            flops=4 * count * model * width,
+            transcendentals=count * width,
+            bytes_accessed=4 * (width * model + 2 * count * model + 3 * count * width),
+        ),
+        name="ffn_act",
+    )(f_all, gate, grad_hidden, w_up)
+
+
+def ffn_grad(collective_id, rows, f_all, hidden_act, grad_gate, grad_up, g_all, w_gate, w_up, w_down):
+    seq_count = lax.axis_size("seq")
+    count, model = f_all.shape
+    width = w_gate.shape[1]
+    anywhere = pl.BlockSpec(memory_space=pl.ANY)
+    dma = pltpu.SemaphoreType.DMA
+    return pl.pallas_call(
+        functools.partial(ffn_grad_kernel, seq_count),
+        out_shape=(
+            jax.ShapeDtypeStruct((rows, model), F32),
+            jax.ShapeDtypeStruct((count, model), BF16),
+            jax.ShapeDtypeStruct((model, width), BF16),
+            jax.ShapeDtypeStruct((width, model), BF16),
+        ),
+        in_specs=[anywhere] * 8,
+        out_specs=(vmem(), anywhere, anywhere, anywhere),
+        scratch_shapes=[
+            pltpu.VMEM((count, model), BF16),
+            pltpu.VMEM((count, model), BF16),
+            pltpu.VMEM((count, width), BF16),
+            pltpu.VMEM((count, width), BF16),
+            pltpu.VMEM((count, width), BF16),
+            pltpu.VMEM((model, width), BF16),
+            pltpu.VMEM((model, width), BF16),
+            pltpu.VMEM((width, model), BF16),
+            pltpu.VMEM((count - rows, model), BF16),
+            pltpu.VMEM((seq_count - 1, rows, model), BF16),
+            pltpu.VMEM((2, 256, width), BF16),
+            pltpu.VMEM((2, 256, model), BF16),
+            dma((8,)),
+            dma((seq_count,)),
+            dma((seq_count,)),
+            dma((3, 2)),
+        ],
+        compiler_params=pltpu.CompilerParams(
+            collective_id=collective_id, has_side_effects=True, vmem_limit_bytes=VMEM_MOST
+        ),
+        cost_estimate=pl.CostEstimate(
+            flops=14 * count * model * width,
+            transcendentals=0,
+            bytes_accessed=4 * (3 * width * model + 3 * count * model),
+        ),
+        name="ffn_grad",
+    )(f_all, hidden_act, grad_gate, grad_up, g_all, w_gate, w_up, w_down)
+
+
+def half_turn(value):
+    half = HEAD_DIM // 2
+    return jnp.concatenate([-value[half:], value[:half]], axis=0)
+
+
+def project_kernel(
+    x_ref, gain_ref, cos_ref, sin_ref, w_ref, normed_ref, rms_ref, q_ref, kv_ref, w_s, sem
+):
+    tile = KV_HEADS * HEAD_DIM
+    count = w_ref.shape[1] // tile
+
+    def load(number):
+        cols = pl.ds(pl.multiple_of(number * tile, tile), tile)
+        return pltpu.make_async_copy(w_ref.at[:, cols], w_s.at[:, cols], sem.at[number])
+
+    for number in range(count):
+        load(number).start()
+    x = x_ref[...].astype(F32)
+    rms = lax.rsqrt(jnp.mean(x * x, axis=1, keepdims=True) + EPS)
+    rms_ref[...] = rms
+    normed_ref[...] = (x * rms * gain_ref[...]).astype(BF16)
+
+    def product(number):
+        load(number).wait()
+        cols = pl.ds(pl.multiple_of(number * tile, tile), tile)
+        return dot32(normed_ref[...], w_s[:, cols], ((1,), (0,)))
+
+    def rotated(value):
+        turned = value.T
+        pieces = []
+        for head in range(tile // HEAD_DIM):
+            one = turned[head * HEAD_DIM : (head + 1) * HEAD_DIM]
+            pieces.append(one * cos_ref[...] + half_turn(one) * sin_ref[...])
+        return jnp.concatenate(pieces, axis=0)
+
+    @pl.loop(0, count - 2)
+    def _(number):
+        own = pl.ds(pl.multiple_of(number * tile, tile), tile)
+        q_ref[own, :] = rotated(product(number)).astype(BF16)
+
+    kv_ref[:, :tile] = rotated(product(count - 2)).T.astype(BF16)
+    kv_ref[:, tile:] = product(count - 1).astype(BF16)
+
+
+def project(x, gain, cosine, sine, w_qkv):
+    rows, model = x.shape
+    width = w_qkv.shape[1]
+    tile = KV_HEADS * HEAD_DIM
+    return pl.pallas_call(
+        project_kernel,
+        out_shape=(
+            jax.ShapeDtypeStruct((rows, model), BF16),
+            jax.ShapeDtypeStruct((rows, 1), F32),
+            jax.ShapeDtypeStruct((width - 2 * tile, rows), BF16),
+            jax.ShapeDtypeStruct((rows, 2 * tile), BF16),
+        ),
+        in_specs=[vmem()] * 4 + [pl.BlockSpec(memory_space=pl.ANY)],
+        out_specs=(vmem(),) * 4,
+        scratch_shapes=[
+            pltpu.VMEM(w_qkv.shape, BF16),
+            pltpu.SemaphoreType.DMA((width // tile,)),
+        ],
+        compiler_params=pltpu.CompilerParams(vmem_limit_bytes=VMEM_MOST),
+        cost_estimate=pl.CostEstimate(
+            flops=2 * rows * model * width, transcendentals=0, bytes_accessed=2 * model * width
+        ),
+        name="project",
+    )(x, gain, cosine, sine, w_qkv)
+
+
+def rotated_back(value, cos_ref, sin_ref):
+    pieces = []
+    for head in range(value.shape[0] // HEAD_DIM):
+        one = value[head * HEAD_DIM : (head + 1) * HEAD_DIM]
+        pieces.append(one * cos_ref[...] - half_turn(one * sin_ref[...]))
+    return jnp.concatenate(pieces, axis=0).T.astype(BF16)
+
+
+def back_during(inputs, outputs, scratch):
+    dq_ref, o_ref, cos_ref, sin_ref, normed_ref, x_ref, rms_ref, gain_ref, grad_ref, w_ref = inputs
+    part_out, part_query, part_kv, out_ref, gain_out = outputs
+    w_s, g_s, gx_s, ga_s, stage, stage_kv, load_sem, leave_sem = scratch
+    tile = KV_HEADS * HEAD_DIM
+    q_width = dq_ref.shape[0]
+    model = x_ref.shape[1]
+    pltpu.make_async_copy(w_ref, w_s, load_sem).start()
+    ga_s[...] = grad_ref[...].astype(BF16)
+    stream_rows(
+        q_width,
+        256,
+        lambda own: dot32(o_ref[own, :], ga_s[...], ((1,), (0,))),
+        stage,
+        leave_sem,
+        part_out,
+    )
+
+    @pl.loop(0, q_width // tile)
+    def _(number):
+        own = pl.ds(pl.multiple_of(number * tile, tile), tile)
+        g_s[:, own] = rotated_back(dq_ref[own, :], cos_ref, sin_ref)
+
+    stream_rows(
+        model,
+        256,
+        lambda own: dot32(normed_ref[:, own], g_s[:, :q_width], ((0,), (0,))),
+        stage,
+        leave_sem,
+        part_query,
+    )
+    pltpu.make_async_copy(w_ref, w_s, load_sem).wait()
+
+    def grad_x(cols):
+        gx_s[:, cols] = dot32(g_s[:, :q_width], w_s[cols, :q_width], ((1,), (1,)))
+
+    tiles(model, 256, grad_x)
+
+
+def back_after(dkv_ref, inputs, outputs, scratch):
+    dq_ref, o_ref, cos_ref, sin_ref, normed_ref, x_ref, rms_ref, gain_ref, grad_ref, w_ref = inputs
+    part_out, part_query, part_kv, out_ref, gain_out = outputs
+    w_s, g_s, gx_s, ga_s, stage, stage_kv, load_sem, leave_sem = scratch
+    tile = KV_HEADS * HEAD_DIM
+    q_width = dq_ref.shape[0]
+    model = x_ref.shape[1]
+    g_s[:, q_width : q_width + tile] = rotated_back(dkv_ref[:, :tile].T, cos_ref, sin_ref)
+    g_s[:, q_width + tile :] = dkv_ref[:, tile:].astype(BF16)
+    stream_rows(
+        model,
+        256,
+        lambda own: dot32(normed_ref[:, own], g_s[:, q_width:], ((0,), (0,))),
+        stage_kv,
+        leave_sem,
+        part_kv,
+    )
+
+    def grad_x(cols):
+        gx_s[:, cols] = gx_s[:, cols] + dot32(g_s[:, q_width:], w_s[cols, q_width:], ((1,), (1,)))
+
+    tiles(model, 256, grad_x)
+    x = x_ref[...].astype(F32)
+    rms = rms_ref[...]
+    gain_out[...] = jnp.sum(gx_s[...] * (x * rms), axis=0, keepdims=True)
+    scaled = gx_s[...] * gain_ref[...]
+    mean = jnp.mean(scaled * x, axis=1, keepdims=True)
+    out_ref[...] = grad_ref[...] + (rms * scaled - x * (rms * rms * rms * mean))
+
+
+def back_work(dq_t, o_t, cosine, sine, normed, x, rms, gain, grad, w_qkv):
+    rows, model = x.shape
+    width = w_qkv.shape[1]
+    q_width = dq_t.shape[0]
+    anywhere = pl.BlockSpec(memory_space=pl.ANY)
+    return {
+        "inputs": [dq_t, o_t, cosine, sine, normed, x, rms, gain, grad, w_qkv],
+        "in_specs": [vmem()] * 9 + [anywhere],
+        "shapes": [
+            jax.ShapeDtypeStruct((q_width, model), BF16),
+            jax.ShapeDtypeStruct((model, q_width), BF16),
+            jax.ShapeDtypeStruct((model, width - q_width), BF16),
+            jax.ShapeDtypeStruct((rows, model), F32),
+            jax.ShapeDtypeStruct((1, model), F32),
+        ],
+        "out_specs": [anywhere, anywhere, anywhere, vmem(), vmem()],
+        "scratch": [
+            pltpu.VMEM(w_qkv.shape, BF16),
+            pltpu.VMEM((rows, width), BF16),
+            pltpu.VMEM((rows, model), F32),
+            pltpu.VMEM((rows, model), BF16),
+            pltpu.VMEM((2, 256, max(model, q_width)), BF16),
+            pltpu.VMEM((2, 256, width - q_width), BF16),
+            pltpu.SemaphoreType.DMA,
+            pltpu.SemaphoreType.DMA((2,)),
+        ],
+        "during": back_during,
+        "after": back_after,
+    }
 
 
 def gather(value, axes, dim=0):
@@ -251,23 +1424,6 @@
 
 def scatter_sum(value, axes, dim=0):
     return lax.psum_scatter(value, axes, scatter_dimension=dim, tiled=True)
-
-
-def rotate_t(value):
-    half = HEAD_DIM // 2
-    heads = value.reshape(-1, HEAD_DIM, value.shape[1])
-    return jnp.concatenate([-heads[:, half:], heads[:, :half]], axis=1)
-
-
-def rope_t(value, cosine, sine):
-    heads = value.reshape(-1, HEAD_DIM, value.shape[1])
-    return (heads * cosine[None] + rotate_t(value) * sine[None]).reshape(value.shape)
-
-
-def rope_back_t(value, cosine, sine):
-    heads = value.reshape(-1, HEAD_DIM, value.shape[1])
-    turned = rotate_t((heads * sine[None]).reshape(value.shape))
-    return (heads * cosine[None] - turned).reshape(value.shape)
 
 
 def norm_back(grad_normed, source, rms_val, gain_val, normed):
@@ -306,10 +1462,8 @@
     own_rows = w_gate.shape[0]
     ff_part = w_gate.shape[1] // seq_count
 
-    def ffn_columns(weight):
-        split = weight.reshape(own_rows, seq_count, ff_part).transpose(1, 0, 2)
-        mine = lax.all_to_all(split, "seq", 0, 0, tiled=True)
-        return gather(mine, "ctx", 1).reshape(model, ff_part)
+    def split_columns(weight):
+        return weight.reshape(own_rows, seq_count, ff_part).transpose(1, 0, 2)
 
     own_spans = lax.dynamic_slice_in_dim(block_order, place[0] * (rows // span_len), rows // span_len)
     local_pos = (
@@ -321,24 +1475,44 @@
     cosine = jnp.concatenate([jnp.cos(angle)] * 2, axis=0)
     sine = jnp.concatenate([jnp.sin(angle)] * 2, axis=0)
 
-    gains = gather(jnp.stack([attn_gain, ffn_gain])[None], EVERY)
-    gain_a = gains[:, 0].reshape(model).astype(F32)
-    gain_f = gains[:, 1].reshape(model).astype(F32)
-    w_qkv = gather(jnp.concatenate([w_query, w_key, w_value], axis=1), EVERY)
-    full_out = gather(w_out, EVERY)
-    full_gate = ffn_columns(w_gate)
-    full_up = ffn_columns(w_up)
     full_down = gather(w_down, "ctx")
-
+    gain_row = jnp.pad(jnp.concatenate([attn_gain, ffn_gain])[None], ((0, 15), (0, 128 - 2 * own_rows)))
+    gains, w_qkv, gate_mine, up_mine = spread(
+        "gather_qkv",
+        0,
+        [
+            gain_row,
+            jnp.concatenate([w_query, w_key, w_value], axis=1),
+            split_columns(w_gate),
+            split_columns(w_up),
+        ],
+        ("all", "all", "swap", "swap"),
+        85,
+    )
+    gain_a = gains[:, :, 0, :own_rows].reshape(1, model).astype(F32)
+    gain_f = gains[:, :, 0, own_rows : 2 * own_rows].reshape(1, model).astype(F32)
+    w_qkv = w_qkv.reshape(model, q_width + 2 * kv_width)
+    full_down, gate_mine, up_mine = lax.optimization_barrier((full_down, gate_mine, up_mine))
+    full_gate = gather(gate_mine, "ctx", 1).reshape(model, ff_part)
+    full_up = gather(up_mine, "ctx", 1).reshape(model, ff_part)
+
+    grad_y = (
+        cotangent.reshape(rows, model).astype(F32) * selected.reshape(rows).astype(F32)[:, None]
+    )
     tokens = hidden_in.reshape(rows, model).astype(F32)
-    rms_a = lax.rsqrt(jnp.mean(tokens * tokens, axis=1, keepdims=True) + EPS)
-    normed_a = tokens * rms_a
-    x_norm = (normed_a * gain_a).astype(BF16)
-    qkv_t = jnp.einsum("td,dh->ht", x_norm, w_qkv, preferred_element_type=F32)
-    q_t = rope_t(qkv_t[:q_width], cosine, sine).astype(BF16)
-    k_t = rope_t(qkv_t[q_width : q_width + kv_width], cosine, sine).astype(BF16)
-    v_t = qkv_t[q_width + kv_width :].astype(BF16)
-    kv = gather(jnp.concatenate([k_t, v_t], axis=0).T, "ctx")
+    x_norm, rms_a, q_t, kv_own = project(
+        hidden_in.reshape(rows, model), gain_a, cosine, sine, w_qkv
+    )
+    kv, full_out, g_all = spread(
+        "gather_kv_out",
+        1,
+        [kv_own, w_out, grad_y.astype(BF16)],
+        ("ctx", "all", "seq"),
+        85,
+    )
+    g_all = g_all.reshape(seq_count * rows, model)
+    kv = kv.reshape(length, 2 * kv_width)
+    full_out = full_out.reshape(q_width, model)
     o_t, lse = attend_forward(place, block_order, doc_lengths, q_t, kv)
 
     middle = tokens + jnp.einsum("ht,hd->td", o_t, full_out, preferred_element_type=F32)
@@ -346,76 +1520,67 @@
     normed_f = middle * rms_f
     f_norm = (normed_f * gain_f).astype(BF16)
 
-    grad_y = (
-        cotangent.reshape(rows, model).astype(F32) * selected.reshape(rows).astype(F32)[:, None]
-    )
-    g_all = gather(grad_y.astype(BF16), "seq")
-    f_all = gather(f_norm, "seq")
-    gate = jnp.dot(f_all, full_gate, preferred_element_type=F32)
-    up_val = jnp.dot(f_all, full_up, preferred_element_type=F32)
-    sigma = jax.nn.sigmoid(gate)
-    activated = gate * sigma
-    hidden_act = (activated * up_val).astype(BF16)
-    ffn_out = scatter_sum(
-        jnp.dot(hidden_act, full_down, preferred_element_type=F32).astype(BF16), "seq"
-    )
-    output = (middle + ffn_out.astype(F32)).astype(BF16).reshape(one, rows, model)
-
-    grad_hidden = jnp.einsum("td,fd->tf", g_all, full_down, preferred_element_type=F32)
-    grad_gate = (grad_hidden * up_val * (sigma + activated * (1.0 - sigma))).astype(BF16)
-    grad_up = (grad_hidden * activated).astype(BF16)
-    grad_f_part = jnp.einsum(
-        "tf,df->td", grad_gate, full_gate, preferred_element_type=F32
-    ) + jnp.einsum("tf,df->td", grad_up, full_up, preferred_element_type=F32)
-    grad_f_norm = scatter_sum(grad_f_part.astype(BF16), "seq").astype(F32)
-    part_down = jnp.einsum("tf,td->fd", hidden_act, g_all, preferred_element_type=F32).astype(BF16)
-    part_gate = jnp.einsum("td,tf->df", f_all, grad_gate, preferred_element_type=F32).astype(BF16)
-    part_up = jnp.einsum("td,tf->df", f_all, grad_up, preferred_element_type=F32).astype(BF16)
+    f_all, g_slots, gate, grad_hidden = ffn_first(2, f_norm, g_all, full_gate, full_down)
+    hidden_act, grad_gate, grad_up, part_gate = ffn_act(f_all, gate, grad_hidden, full_up)
+    grad_f_norm, ffn_part, part_up, part_down = ffn_grad(
+        3, rows, f_all, hidden_act, grad_gate, grad_up, g_slots, full_gate, full_up, full_down
+    )
 
     def ffn_rows(part):
-        mine = scatter_sum(part.reshape(seq_count, model // seq_count, ff_part), "ctx", 1)
-        return (
-            lax.all_to_all(mine, "seq", 0, 0, tiled=True)
-            .transpose(1, 0, 2)
-            .reshape(own_rows, seq_count * ff_part)
-            .astype(F32)
-        )
-
-    grad_w_down = scatter_sum(part_down, "ctx").astype(F32)
-    grad_w_gate = ffn_rows(part_gate)
-    grad_w_up = ffn_rows(part_up)
-
+        return scatter_sum(part.reshape(seq_count, model // seq_count, ff_part), "ctx", 1)
+
+    rows_gate = ffn_rows(part_gate)
+    rows_up = ffn_rows(part_up)
     grad_ffn_gain, grad_from_f = norm_back(grad_f_norm, middle, rms_f, gain_f, normed_f)
     grad_middle = grad_y + grad_from_f
     g_attn = grad_middle.astype(BF16)
     do_t = jnp.einsum("td,hd->ht", g_attn, full_out, preferred_element_type=F32).astype(BF16)
-    part_out = jnp.einsum("ht,td->hd", o_t, g_attn, preferred_element_type=F32).astype(BF16)
     dq_t, dkv = attend_backward(place, block_order, doc_lengths, q_t, kv, o_t, lse, do_t)
-    dkv_t = scatter_sum(dkv, "ctx").astype(F32).T
-    grad_qkv_t = jnp.concatenate(
-        [
-            rope_back_t(dq_t, cosine, sine).astype(BF16),
-            rope_back_t(dkv_t[:kv_width], cosine, sine).astype(BF16),
-            dkv_t[kv_width:].astype(BF16),
-        ],
-        axis=0,
-    )
-    part_qkv = jnp.einsum("td,ht->dh", x_norm, grad_qkv_t, preferred_element_type=F32).astype(BF16)
-    grad_x_norm = jnp.einsum("ht,dh->td", grad_qkv_t, w_qkv, preferred_element_type=F32)
-    grad_attn_gain, grad_from_a = norm_back(grad_x_norm, tokens, rms_a, gain_a, normed_a)
-    grad_input = (grad_middle + grad_from_a).reshape(one, rows, model)
-    grad_w_out = scatter_sum(part_out, EVERY).astype(F32)
-    grad_w_qkv = scatter_sum(part_qkv, EVERY).astype(F32)
-    grad_gains = scatter_sum(jnp.stack([grad_attn_gain, grad_ffn_gain], axis=1), EVERY)
+    part_down, rows_gate, dkv = lax.optimization_barrier((part_down, rows_gate, dkv))
+    grad_w_down = scatter_sum(part_down, "ctx").astype(F32)
+    _, ffn_out, part_out, part_query, part_kv, grad_input, grad_attn_gain = fold(
+        "fold_kv",
+        4,
+        [dkv, ffn_part],
+        ("ctx", "seq"),
+        (1, 2),
+        60,
+        work=back_work(
+            dq_t,
+            o_t,
+            cosine,
+            sine,
+            x_norm,
+            hidden_in.reshape(rows, model),
+            rms_a,
+            gain_a,
+            grad_middle,
+            w_qkv,
+        ),
+    )
+    output = (middle + ffn_out).astype(BF16).reshape(one, rows, model)
+    part_gains = jnp.concatenate(
+        [grad_attn_gain.reshape(-1, own_rows), grad_ffn_gain.reshape(-1, own_rows)], axis=1
+    )
+    part_gains = jnp.pad(part_gains[:, None], ((0, 0), (0, 15), (0, 128 - 2 * own_rows)))
+    grad_w_out, grad_w_query, grad_w_kv, grad_gains, grad_w_gate, grad_w_up = fold(
+        "fold_weights",
+        5,
+        [part_out, part_query, part_kv, part_gains.reshape(-1, 128).astype(BF16)],
+        ("all", "all", "all", "all"),
+        (8, 8, 2, 1),
+        110,
+        [rows_gate, rows_up],
+    )
     return (
         output,
-        grad_input,
-        grad_gains[:, 0],
-        grad_w_qkv[:, :q_width],
-        grad_w_qkv[:, q_width : q_width + kv_width],
-        grad_w_qkv[:, q_width + kv_width :],
+        grad_input.reshape(one, rows, model),
+        grad_gains[0, :own_rows],
+        grad_w_query,
+        grad_w_kv[:, :kv_width],
+        grad_w_kv[:, kv_width:],
         grad_w_out,
-        grad_gains[:, 1],
+        grad_gains[0, own_rows : 2 * own_rows],
         grad_w_gate,
         grad_w_up,
         grad_w_down,

time: 1400 us -> 609 us (0.43)
  waiting for transfers between devices: 1070 us -> 1.48 us
  Pallas kernels: 20.1 us -> 543 us
  matrix products: 144 us -> 13.8 us
  blocking collectives: 70 us -> 0 us
  local copies, waits for them, and re-layouts: 36.3 us -> 12.8 us
  other arithmetic: 28.9 us -> 14.5 us
    reduce_scatter x8 -> x3, waiting for transfers between devices: 581 us -> 0.01 us  [scatter_sum(): return lax.psum_scatter(value, axes, scatter_dimension=dim, tiled=True)]
    pallas_call x0 -> x8, Pallas kernels: none -> 481 us  [the longest x2 183 us: spread(): pl.pallas_call(functools.partial(spread_kernel, scopes, tuple(halves), se...]
    all_gather x8 -> x3, waiting for transfers between devices: 359 us -> 0.04 us  [gather(): return lax.all_gather(value, axes, axis=dim, tiled=True)]
    dot_general x13 -> x0, matrix products: 130 us -> none  [the longest x1 15.3 us: local(): jnp.einsum('td,fd->tf', g_all, full_down, preferred_element_type=F32)]
    unnamed x18 -> x6, waiting for transfers between devices: 128 us -> 1.43 us
    all_gather x1 -> x0, blocking collectives: 43.1 us -> none  [gather(): return lax.all_gather(value, axes, axis=dim, tiled=True)]
    all_to_all x2 -> x0, blocking collectives: 26.9 us -> none  [ffn_columns(): mine = lax.all_to_all(split, 'seq', 0, 0, tiled=True)]
    pallas_call x1, Pallas kernels: 12.1 us -> 36.1 us  [attend_backward(): pl.pallas_call(functools.partial(attend_backward_kernel, span_len, spans)...]
  transfers between devices with their start and end apart: 19 -> 6, of which waited for: 16 -> 0; matrix products, arithmetic and copies ran while one was open for 10% -> 6% of each run, Pallas kernels for 1% -> 86%
where the time goes in v4:
time: 609 us; the launch traced here: 600 us
  Pallas kernels  543 us (89%)
  other arithmetic  14.5 us (2%)
  between operations  14.5 us (2%)
  matrix products  13.8 us (2%)
  local copies, waits for them, and re-layouts  12.8 us (2%)
    pallas_call x2, Pallas kernels, spread(): pl.pallas_call(functools.partial(spread_kernel, scopes, tuple(halves), se...  183 us
    pallas_call x2, Pallas kernels, fold(): pl.pallas_call(functools.partial(fold_kernel, tuple(kinds), tuple(chunk_c...  177 us
    pallas_call x1, Pallas kernels, ffn_grad(): pl.pallas_call(functools.partial(ffn_grad_kernel, seq_count), out_shape=(...  49.9 us
    pallas_call x1, Pallas kernels, attend_backward(): pl.pallas_call(functools.partial(attend_backward_kernel, span_len, spans)...  36.1 us
    pallas_call x1, Pallas kernels, ffn_first(): pl.pallas_call(functools.partial(ffn_first_kernel, seq_count), out_shape=...  34.8 us
    pallas_call x1, Pallas kernels, ffn_act(): pl.pallas_call(ffn_act_kernel, out_shape=(jax.ShapeDtypeStruct((count, wi...  27.4 us
    pallas_call x1, Pallas kernels, attend_forward(): pl.pallas_call(functools.partial(attend_forward_kernel, span_len, spans),...  25.3 us
  transfers between devices with their start and end apart: 6, of which 0 were waited for; matrix products, arithmetic and copies ran while one was open for 6% of the time, Pallas kernels for 86%

profile of v4, /device:TPU:0, one launch (start us, length us, event | category | flops | bytes accessed | tf_op | source)
XLA Modules:
  0.0 599.9 jit_solution(8216332505706560303)
XLA Ops:
  7.2 0.7 all-gather.4.cloned.1.call-update
  7.9 0.0 all-gather.6.cloned.1.call-start
  8.0 0.7 maximum_bitcast_fusion.1
  8.7 0.6 pad.9.refs_0_
  9.3 1.7 pad_maximum_fusion.refs_1_
  11.0 2.6 bitcast_bitcast_fusion
  13.6 91.8 %gather_qkv.1 = (bf16[4,8,16,128]{3,2,1,0:T(8,128)(2,1)}, bf16[4,8,64,2560]{3,2,1,0:T(8,128)(2,1)}, bf16[4,64,1408]{2,1,0:T(8,128)(2,1)}, bf16[4,64,1408]{2,1,0:T(8,128)(2,1)}) custom-call(bf16[16,128]{1,0:T(8,128)(2,1)} %pad.9.refs_0_, bf16[64,2560]{1,0:T(8,128)(2,1)} %pad_maximum_fusion.refs_1_, bf16[4,64,1408]{2,1,0:T(8,128)(2,1)} %get-tuple-element.116.refs_2_, ...), custom_call_target="tpu_custom_call" | custom-call | bytes 255000000 | tf_op jit(solution)/shard_map/gather_qkv/pallas_call | solution.py:521
  105.6 0.7 all-gather.8.cloned.1.call-update
  106.2 0.0 reduce-scatter.4.cloned.1.call-start
  106.3 1.0 convert_reduce_fusion
  107.4 0.1 reshape.186
  107.4 0.7 reshape.184.gain_ref.refs_9_
  108.1 0.1 dynamic-slice_multiply_fusion
  108.2 0.1 convert_bitcast_fusion
  108.3 0.2 multiply_sine_fusion
  108.5 0.7 pad_maximum_fusion.1
  109.2 9.2 %project.1 = (bf16[256,2048]{1,0:T(8,128)(2,1)}, f32[256,1]{1,0:T(8,128)}, bf16[2048,256]{1,0:T(8,128)(2,1)}, bf16[256,512]{1,0:T(8,128)(2,1)}) custom-call(bf16[256,2048]{1,0:T(8,128)(2,1)} %bitcast.51, f32[1,2048]{1,0:T(1,128)} %reshape.184.gain_ref.refs_9_, f32[64,256]{1,0:T(8,128)} %get-tuple-element.117.cos_ref.refs_4_, ...), custom_call_target="tpu_custom_call" | custom-call | flops 2684354560 | bytes 10485760 | tf_op jit(solution)/shard_map/project/pallas_call | solution.py:1291
  118.3 1.2 fusion.1.refs_2_
  119.5 91.1 %gather_kv_out.1 = (bf16[8,256,512]{2,1,0:T(8,128)(2,1)}, bf16[4,8,64,2048]{3,2,1,0:T(8,128)(2,1)}, bf16[4,256,2048]{2,1,0:T(8,128)(2,1)}) custom-call(bf16[256,512]{1,0:T(8,128)(2,1)} %get-tuple-element.59.refs_0_, bf16[64,2048]{1,0:T(8,128)(2,1)} %refs_1_.1, bf16[256,2048]{1,0:T(8,128)(2,1)} %fusion.1.refs_2_), custom_call_target="tpu_custom_call" | custom-call | bytes 255000000 | tf_op jit(solution)/shard_map/gather_kv_out/pallas_call | solution.py:521
  210.7 25.3 %attend_forward.1 = (bf16[2048,256]{1,0:T(8,128)(2,1)}, f32[2,4,1024]{2,1,0:T(4,128)}) custom-call(s32[1]{0:T(128)} %bitcast.1.place_ref, s32[16]{0:T(128)} %order_ref.3, s32[1,8]{1,0:T(1,128)} %lens_ref.3, bf16[2048,256]{1,0:T(8,128)(2,1)} %get-tuple-element.58.q_ref, bf16[2048,512]{1,0:T(8,128)(2,1)} %bitcast.70), custom_call_target="tpu_custom_call" | custom-call | flops 2147483648 | bytes 4194304 | tf_op jit(solution)/shard_map/attend_forward/pallas_call | solution.py:195
  236.0 6.2 %multiply_reduce_fusion.2 = (f32[256]{0:T(256)S(1)}, f32[256,2048]{1,0:T(8,128)S(1)}) fusion(bf16[2048,256]{1,0:T(8,128)(2,1)} %get-tuple-element.61.o_ref.refs_3_, bf16[2048,2048]{1,0:T(8,128)(2,1)} %bitcast.49, bf16[1,256,2048]{2,1,0:T(8,128)(2,1)S(1)} %copy-done), kind=kOutput, calls=%fused_computation.9 | convolution fusion | flops 2149580544 | bytes 12583936 | tf_op jit(solution)/shard_map/ht,hd->td/dot_general | solution.py:1518
  242.3 1.2 multiply_convert_fusion.f_ref
  243.5 34.8 %ffn_first.1 = (bf16[1024,2048]{1,0:T(8,128)(2,1)}, bf16[1024,2048]{1,0:T(8,128)(2,1)}, f32[1024,1408]{1,0:T(8,128)}, bf16[1024,1408]{1,0:T(8,128)(2,1)}) custom-call(bf16[256,2048]{1,0:T(8,128)(2,1)} %multiply_convert_fusion.f_ref, bf16[4,256,2048]{2,1,0:T(8,128)(2,1)} %get-tuple-element.63.g_ref, bf16[2048,1408]{1,0:T(8,128)(2,1)} %bitcast.66, ...), custom_call_target="tpu_custom_call" | custom-call | flops 23622320128 | bytes 48234496 | tf_op jit(solution)/shard_map/ffn_first/pallas_call | solution.py:1131
  278.3 27.4 %ffn_act.1 = (bf16[1024,1408]{1,0:T(8,128)(2,1)}, bf16[1024,1408]{1,0:T(8,128)(2,1)}, bf16[1024,1408]{1,0:T(8,128)(2,1)}, bf16[2048,1408]{1,0:T(8,128)(2,1)}) custom-call(bf16[1024,2048]{1,0:T(8,128)(2,1)} %get-tuple-element.68.f_ref, f32[1024,1408]{1,0:T(8,128)} %get-tuple-element.69.gate_ref, bf16[1024,1408]{1,0:T(8,128)(2,1)} %get-tuple-element.70.gh_ref, ...), custom_call_target="tpu_custom_call" | custom-call | flops 11811160064 | bytes 45613056 | tf_op jit(solution)/shard_map/ffn_act/pallas_call | solution.py:1168
  305.8 0.0 reduce-scatter.6.cloned.1.call-start
  305.8 49.9 %ffn_grad.1 = (f32[256,2048]{1,0:T(8,128)}, bf16[1024,2048]{1,0:T(8,128)(2,1)}, bf16[2048,1408]{1,0:T(8,128)(2,1)}, bf16[1408,2048]{1,0:T(8,128)(2,1)}) custom-call(bf16[1024,2048]{1,0:T(8,128)(2,1)} %get-tuple-element.68.f_ref, bf16[1024,1408]{1,0:T(8,128)(2,1)} %get-tuple-element.72.hid_ref, bf16[1024,1408]{1,0:T(8,128)(2,1)} %get-tuple-element.73.gg_ref, ...), custom_call_target="tpu_custom_call" | custom-call | flops 41339060224 | bytes 59768832 | tf_op jit(solution)/shard_map/ffn_grad/pallas_call | solution.py:1203
  355.8 0.0 reduce-scatter.8.cloned.1.call-start
  355.8 2.3 multiply_reduce_fusion
  358.2 0.7 fusion.refs_10_
  358.9 7.6 %convolution_convert_fusion.do_ref = bf16[2048,256]{1,0:T(8,128)(2,1)} fusion(bf16[2048,2048]{1,0:T(8,128)(2,1)} %bitcast.50, f32[256,2048]{1,0:T(8,128)S(1)} %fusion.refs_10_), kind=kOutput, calls=%fused_computation.1 | convolution fusion | flops 2148532224 | bytes 11534336 | tf_op jit(solution)/shard_map/td,hd->ht/dot_general | solution.py:1537
  366.4 36.1 %attend_backward.1 = (f32[2048,256]{1,0:T(8,128)}, bf16[2048,512]{1,0:T(8,128)(2,1)}) custom-call(s32[1]{0:T(128)} %bitcast.1.place_ref, s32[16]{0:T(128)} %order_ref.3, s32[1,8]{1,0:T(1,128)} %lens_ref.3, bf16[2048,256]{1,0:T(8,128)(2,1)} %get-tuple-element.58.q_ref, bf16[2048,512]{1,0:T(8,128)(2,1)} %bitcast.71, ...), custom_call_target="tpu_custom_call" | custom-call | flops 5368709120 | bytes 9437184 | tf_op jit(solution)/shard_map/attend_backward/pallas_call | solution.py:222
  402.5 0.1 reshape.182
  402.6 56.2 %fold_kv.1 = (f32[256,512]{1,0:T(8,128)}, f32[256,2048]{1,0:T(8,128)}, bf16[2048,2048]{1,0:T(8,128)(2,1)}, bf16[2048,2048]{1,0:T(8,128)(2,1)}, bf16[2048,512]{1,...) custom-call(bf16[1,4,2,256,512]{4,3,2,1,0:T(8,128)(2,1)} %bitcast.60, bf16[4,256,2048]{2,1,0:T(8,128)(2,1)} %bitcast.57, ...), custom_call_target="tpu_custom_call" | custom-call | bytes 180000000 | tf_op jit(solution)/shard_map/fold_kv/pallas_call | solution.py:820
  458.8 0.7 convert_reduce_fusion.2
  459.6 0.1 reshape.181
  459.6 0.1 maximum_bitcast_fusion
  459.7 0.7 pad.10.clone
  460.4 120.7 %fold_weights.1 = (f32[64,2048]{1,0:T(8,128)}, f32[64,2048]{1,0:T(8,128)}, f32[64,512]{1,0:T(8,128)}, f32[16,128]{1,0:T(8,128)}, f32[64,5632]{1,0:T(8,128)}, /*index=5*/f32[64,5632]{1,0:T(8,128)}) custom-call(bf16[4,4,2,64,2048]{4,3,2,1,0:T(8,128)(2,1)} %bitcast.53, bf16[4,4,2,64,2048]{4,3,2,1,0:T(8,128)(2,1)} %bitcast.54, ...), custom_call_target="tpu_custom_call" | custom-call | bytes 330000000 | tf_op jit(solution)/shard_map/fold_weights/pallas_call | solution.py:820
  581.1 1.3 slice_bitcast_fusion
  582.5 1.5 fusion.4
  584.0 1.2 fusion.2
  585.2 2.5 convert_element_type.89
  587.7 1.3 copy.38
  589.1 0.1 copy-done.9
  589.1 0.8 copy.39
  589.9 0.8 copy.40
  590.7 1.1 copy.41
  591.8 1.1 copy.42
  (40 shorter events, 0.3 us)
Async XLA Ops:
  7.2 98.3 %all-gather.4.cloned.1.call-start = ((), (), s32[]{:S(2)}) async-start(), calls=%async_computation.3 | async-start | bytes 6488064 | tf_op jit(solution)/shard_map/all_gather | solution.py:1422
  7.9 235.6 %all-gather.6.cloned.1.call-start = ((), (), s32[]{:S(2)}) async-start(), calls=%async_computation.4 | async-start | bytes 6488064 | tf_op jit(solution)/shard_map/all_gather | solution.py:1422
  13.6 92.7 %copy-start.10 = (s32[1,256]{1,0:T(1,128)S(1)}, s32[1,256]{1,0:T(1,128)}, u32[]{:S(2)}) copy-start(s32[1,256]{1,0:T(1,128)} %param.26) | copy-start | bytes 3076
  13.6 94.5 %copy-start.11 = (s32[16]{0:T(128)S(1)}, s32[16]{0:T(128)}, u32[]{:S(2)}) copy-start(s32[16]{0:T(128)} %order_ref.3) | copy-start | bytes 196
  105.5 172.8 %all-gather.8.cloned.1.call-start = ((), (), s32[]{:S(2)}) async-start(), calls=%async_computation.5 | async-start | bytes 6488064 | tf_op jit(solution)/shard_map/all_gather | solution.py:1422
  106.2 296.2 %reduce-scatter.4.cloned.1.call-start = ((), (), s32[]{:S(2)}) async-start(), calls=%async_computation.6 | async-start | bytes 6488064 | tf_op jit(solution)/shard_map/reduce_scatter | solution.py:1426
  109.2 9.2 %copy-start.3 = (bf16[1,256,2048]{2,1,0:T(8,128)(2,1)S(1)}, bf16[1,256,2048]{2,1,0:T(8,128)(2,1)}, u32[]{:S(2)}) copy-start(bf16[1,256,2048]{2,1,0:T(8,128)(2,1)} %param.24) | copy-start | bytes 3145732
  210.7 25.4 %copy-start = (bf16[1,256,2048]{2,1,0:T(8,128)(2,1)S(1)}, bf16[1,256,2048]{2,1,0:T(8,128)(2,1)}, u32[]{:S(2)}) copy-start(bf16[1,256,2048]{2,1,0:T(8,128)(2,1)} %param.14) | copy-start | bytes 3145732
  305.8 154.7 %reduce-scatter.6.cloned.1.call-start = ((), (), s32[]{:S(2)}) async-start(), calls=%async_computation.7 | async-start | bytes 6488064 | tf_op jit(solution)/shard_map/reduce_scatter | solution.py:1426
  355.8 229.4 %reduce-scatter.8.cloned.1.call-start = ((), (), s32[]{:S(2)}) async-start(), calls=%async_computation.8 | async-start | bytes 6488064 | tf_op jit(solution)/shard_map/reduce_scatter | solution.py:1426
  355.8 2.3 copy-start.1
  358.8 7.6 %copy-start.2 = (f32[256,2048]{1,0:T(8,128)}, f32[256,2048]{1,0:T(8,128)S(1)}, u32[]{:S(2)}) copy-start(f32[256,2048]{1,0:T(8,128)S(1)} %fusion.refs_10_) | copy-start | bytes 6291460
  460.4 123.6 %copy-start.5 = (f32[256,2048]{1,0:T(8,128)S(1)}, f32[256,2048]{1,0:T(8,128)}, u32[]{:S(2)}) copy-start(f32[256,2048]{1,0:T(8,128)} %get-tuple-element.86) | copy-start | bytes 6291460
  585.2 2.5 copy-start.4
  587.7 1.4 copy-start.9
  587.7 2.2 copy-start.8
  589.1 1.6 copy-start.7
  589.9 1.9 copy-start.6
Sparse Core Ops, SparseCore 0:
  9.7 78.7 all-gather.3
  105.6 77.2 all-gather.5
  184.6 60.4 all-gather.7
  305.9 62.1 reduce-scatter.3
  370.2 80.1 reduce-scatter.5
  452.6 82.5 reduce-scatter.7

commit v5 on v4

--- a/solution.py
+++ b/solution.py
@@ -282,10 +282,7 @@
     ]
 
 
-def spread_kernel(scopes, halves, seq_count, chip_count, *refs):
-    count = len(scopes)
-    sources, results = refs[:count], refs[count : 2 * count]
-    sends, recvs, local_sem = refs[2 * count : 3 * count], refs[3 * count : 4 * count], refs[4 * count]
+def spread_tools(scopes, halves, seq_count, chip_count, sources, results, sends, recvs, local_sem):
     _, chip, core = coords()
     ctx = lax.axis_index("ctx")
     ctx_count = 2 * chip_count
@@ -297,14 +294,16 @@
         (chip < last, {"ctx": lax.rem(chip + 1, chip_count) * 2 + core}),
         (chip > 0, {"ctx": lax.rem(chip + last, chip_count) * 2 + core}),
     ]
-    use_lines = any(scope in ("ctx", "all") for scope in scopes)
     peers = []
     if any(scope != "ctx" for scope in scopes):
         peers += [{"seq": place} for place in planes]
-    if use_lines:
+    if any(scope in ("ctx", "all") for scope in scopes):
         peers += [{"ctx": other(chip, step, chip_count) * 2 + core} for step in range(1, chip_count)]
         peers += [sibling]
-    meet(peers)
+    locals_ = {}
+
+    def pick(items, *names):
+        return [item for item in items if scopes[item] in names]
 
     started = []
 
@@ -405,40 +404,6 @@
 
         run() if there is None else pl.when(there)(run)
 
-    items = range(count)
-    lines = [item for item in items if scopes[item] in ("ctx", "all")]
-    flats = [item for item in items if scopes[item] in ("seq", "all")]
-    everywhere = [item for item in items if scopes[item] == "all"]
-    swaps = [item for item in items if scopes[item] == "swap"]
-    locals_ = []
-    for item in items:
-        target, _ = block(item, seq, chip, core)
-        own = sources[item].at[seq] if scopes[item] == "swap" else sources[item]
-        copy = pltpu.make_async_copy(own, target, local_sem.at[item])
-        copy.start()
-        locals_.append(copy)
-    for item in lines:
-        for half in cut(item):
-            for side, (there, device) in enumerate(sides):
-                copy = descriptor(
-                    item, seq, chip, half, 2 * side + (half or 0), device, sources[item]
-                )
-                pl.when(there)(functools.partial(start, [copy], there))
-    for item in swaps:
-        start(
-            [
-                descriptor(item, seq, chip, None, number, {"seq": place}, sources[item].at[place])
-                for number, place in enumerate(planes)
-            ]
-        )
-    for item in flats:
-        for half in cut(item):
-            start(plane_copies(item, chip, half, sources[item]))
-    for item in lines:
-        start([descriptor(item, seq, chip, None, kinds_relay + 2, sibling, sources[item])])
-    for item in flats:
-        plane_relay(item, chip)
-
     def pass_on(item, place, there, onward, device):
         steps = []
         for half in cut(item):
@@ -462,73 +427,137 @@
         for _, copy, _ in steps:
             started.append((there & onward, copy))
 
-    waves = []
-    for step in range(1, chip_count):
-        wave = [
-            (lax.rem(chip + chip_count - step, chip_count), chip >= step, *sides[0]),
-            (lax.rem(chip + step, chip_count), chip <= last - step, *sides[1]),
-        ]
-        for place, there, onward, device in wave:
-            for item in lines:
-                pass_on(item, place, there, onward, device)
+    def begin(items):
+        for item in items:
+            target, _ = block(item, seq, chip, core)
+            own = sources[item].at[seq] if scopes[item] == "swap" else sources[item]
+            locals_[item] = pltpu.make_async_copy(own, target, local_sem.at[item])
+            locals_[item].start()
+        for item in pick(items, "ctx", "all"):
+            for half in cut(item):
+                for side, (there, device) in enumerate(sides):
+                    copy = descriptor(
+                        item, seq, chip, half, 2 * side + (half or 0), device, sources[item]
+                    )
+                    pl.when(there)(functools.partial(start, [copy], there))
+        for item in pick(items, "swap"):
+            start(
+                [
+                    descriptor(
+                        item, seq, chip, None, number, {"seq": place}, sources[item].at[place]
+                    )
+                    for number, place in enumerate(planes)
+                ]
+            )
+        for item in pick(items, "seq", "all"):
+            for half in cut(item):
+                start(plane_copies(item, chip, half, sources[item]))
+        for item in pick(items, "ctx", "all"):
+            start([descriptor(item, seq, chip, None, kinds_relay + 2, sibling, sources[item])])
+
+    def relays(items):
+        for item in pick(items, "seq", "all"):
+            plane_relay(item, chip)
+
+    def waves(items):
+        lines, everywhere = pick(items, "ctx", "all"), pick(items, "all")
+        done = []
+        for step in range(1, chip_count):
+            wave = [
+                (lax.rem(chip + chip_count - step, chip_count), chip >= step, *sides[0]),
+                (lax.rem(chip + step, chip_count), chip <= last - step, *sides[1]),
+            ]
+            for place, there, onward, device in wave:
+                for item in lines:
+                    pass_on(item, place, there, onward, device)
+            for item in everywhere:
+                for place, there, _, _ in done[-1] if done else []:
+                    plane_relay(item, place, there)
+            if step == 1:
+                for item in pick(items, "seq", "all"):
+                    plane_end(item, chip)
+            elif step > 2:
+                for item in everywhere:
+                    for place, there, _, _ in done[-2]:
+                        plane_end(item, place, there)
+            done.append(wave)
         for item in everywhere:
-            for place, there, _, _ in waves[-1] if waves else []:
+            for place, there, _, _ in done[-1]:
                 plane_relay(item, place, there)
-        if step == 1:
-            for item in flats:
-                plane_end(item, chip)
-        elif step > 2:
-            for item in everywhere:
-                for place, there, _, _ in waves[-2]:
+            for wave in done[-2:]:
+                for place, there, _, _ in wave:
                     plane_end(item, place, there)
-        waves.append(wave)
-    for item in everywhere:
-        for place, there, _, _ in waves[-1]:
-            plane_relay(item, place, there)
-        for wave in waves[-2:]:
-            for place, there, _, _ in wave:
-                plane_end(item, place, there)
-    for item in swaps:
-        for place in planes:
-            arrival(item, place, chip, None).wait_recv()
-    for item in lines:
-        for at_seq in [seq] + (planes if scopes[item] == "all" else []):
-            for step in range(chip_count):
-                arrival(item, at_seq, other(chip, step, chip_count), None, 1 - core).wait_recv()
-    for copy in locals_:
-        copy.wait()
-    for there, copy in started:
-        if there is None:
-            copy.wait_send()
-        else:
-            pl.when(there)(copy.wait_send)
-
-
-def spread(name, collective_id, arrays, scopes, micros):
-    seq_count, ctx_count = lax.axis_size("seq"), lax.axis_size("ctx")
-    chip_count = ctx_count // 2
-    shapes, send_sems, recv_sems, halves = [], [], [], []
+
+    def settle(items):
+        for item in pick(items, "swap"):
+            for place in planes:
+                arrival(item, place, chip, None).wait_recv()
+        for item in pick(items, "ctx", "all"):
+            for at_seq in [seq] + (planes if scopes[item] == "all" else []):
+                for step in range(chip_count):
+                    arrival(item, at_seq, other(chip, step, chip_count), None, 1 - core).wait_recv()
+        for item in items:
+            locals_[item].wait()
+
+    def end():
+        for there, copy in started:
+            if there is None:
+                copy.wait_send()
+            else:
+                pl.when(there)(copy.wait_send)
+
+    return peers, begin, relays, waves, settle, end
+
+
+def spread_sems(arrays, scopes, seq_count, chip_count):
     kinds = 4 + max(4, seq_count - 1) + 3 + seq_count - 1
+    sends, recvs, halves, shapes = [], [], [], []
     for array, scope in zip(arrays, scopes):
-        lead = {"all": (seq_count, ctx_count), "ctx": (ctx_count,)}.get(scope, (seq_count,))
+        lead = {"all": (seq_count, 2 * chip_count), "ctx": (2 * chip_count,)}.get(scope, (seq_count,))
         halves.append(seq_count == 4 and scope in ("all", "seq") and array.shape[0] % 32 == 0)
         shape = array.shape if scope == "swap" else lead + array.shape
         shapes.append(jax.ShapeDtypeStruct(shape, array.dtype))
         rows = chip_count if scope in ("all", "ctx") else 1
-        send_sems.append(pltpu.SemaphoreType.DMA((rows, kinds)))
-        recv_sems.append(pltpu.SemaphoreType.DMA((2 * math.prod(lead),)))
+        sends.append(pltpu.SemaphoreType.DMA((rows, kinds)))
+        recvs.append(pltpu.SemaphoreType.DMA((2 * math.prod(lead),)))
+    return shapes, tuple(halves), sends + recvs + [pltpu.SemaphoreType.DMA((len(arrays),))]
+
+
+def swap_kernel(scopes, halves, seq_count, chip_count, *refs):
+    count = len(scopes)
+    peers, begin, _, _, settle, end = spread_tools(
+        scopes,
+        halves,
+        seq_count,
+        chip_count,
+        refs[:count],
+        refs[count : 2 * count],
+        refs[2 * count : 3 * count],
+        refs[3 * count : 4 * count],
+        refs[4 * count],
+    )
+    meet(peers)
+    begin(range(count))
+    settle(range(count))
+    end()
+
+
+def swap(collective_id, arrays):
+    seq_count, chip_count = lax.axis_size("seq"), lax.axis_size("ctx") // 2
+    scopes = ("swap",) * len(arrays)
+    shapes, halves, sems = spread_sems(arrays, scopes, seq_count, chip_count)
     anywhere = pl.BlockSpec(memory_space=pl.ANY)
     return pl.pallas_call(
-        functools.partial(spread_kernel, scopes, tuple(halves), seq_count, chip_count),
+        functools.partial(swap_kernel, scopes, halves, seq_count, chip_count),
         out_shape=tuple(shapes),
         in_specs=[anywhere] * len(arrays),
         out_specs=(anywhere,) * len(arrays),
-        scratch_shapes=send_sems + recv_sems + [pltpu.SemaphoreType.DMA((len(arrays),))],
+        scratch_shapes=sems,
         compiler_params=pltpu.CompilerParams(collective_id=collective_id, has_side_effects=True),
         cost_estimate=pl.CostEstimate(
-            flops=0, transcendentals=0, bytes_accessed=int(micros * 3_000_000)
-        ),
-        name=name,
+            flops=0, transcendentals=0, bytes_accessed=20 * 3_000_000
+        ),
+        name="swap",
     )(*arrays)
 
 
@@ -623,8 +652,8 @@
         place = slots[slot] if kinds[item] == "all" else 0
         return mine[place, :, :, cols].astype(F32) + got1[place, :, :, cols].astype(F32)
 
-    def turn(chunk):
-        return (1, 2) if chunk % 2 == 0 else (2, 1)
+    def turn(item, chunk):
+        return (1, 2) if (item + chunk) % 2 == 0 else (2, 1)
 
     seconds = {}
 
@@ -633,7 +662,7 @@
         cols = columns(item, chunk)
         if kinds[item] == "all":
             firsts[item, chunk].wait_recv()
-        first, _ = turn(chunk)
+        first, _ = turn(item, chunk)
         targets = [(slot, slot) for slot in range(1, seq_count)]
         if seq_count == 4:
             targets = [(3, first), (first, first)]
@@ -662,7 +691,7 @@
             return
         _, got1, spare, got2, keep, _, _, sem_s, sem_r = scratch(item)
         cols = columns(item, chunk)
-        _, second = turn(chunk)
+        _, second = turn(item, chunk)
         across, mine = seconds[item, chunk]
         across.wait_recv()
         if kinds[item] == "all":
@@ -835,10 +864,10 @@
     )(*inputs)
 
 
-def tiles(extent, width, visit):
+def tiles(extent, width, visit, first=0):
     whole = extent // width
 
-    @pl.loop(0, whole)
+    @pl.loop(first, whole)
     def _(number):
         visit(pl.ds(pl.multiple_of(number * width, width), width))
 
@@ -986,11 +1015,13 @@
     ]
     for load in loads:
         load.start()
-    for load in loads:
+    for load in loads[:2]:
         load.wait()
 
-    def act(cols):
+    def act(cols, ready=None):
         up_val = dot32(f_s[...], wu[:, cols], ((1,), (0,)))
+        if ready is not None:
+            ready()
         gate = gate_s[:, cols]
         grad = gh_s[:, cols].astype(F32)
         sigma = jax.nn.sigmoid(gate)
@@ -999,7 +1030,12 @@
         gg[:, cols] = (grad * up_val * (sigma + activated * (1.0 - sigma))).astype(BF16)
         gu[:, cols] = (grad * activated).astype(BF16)
 
-    tiles(width, 256, act)
+    def ready():
+        for load in loads[2:]:
+            load.wait()
+
+    act(pl.ds(0, 256), ready)
+    tiles(width, 256, act, 1)
     stream_rows(
         model,
         256,
@@ -1059,11 +1095,13 @@
             ]
         )
     ]
-    for load in loads:
+    for load in loads[:4]:
         load.start()
     meet([{"seq": place} for place in places[1:]])
     for load in loads[:4]:
         load.wait()
+    for load in loads[4:]:
+        load.start()
 
     def part_copy(slot, cols):
         return remote(
@@ -1245,27 +1283,83 @@
     return jnp.concatenate([-value[half:], value[:half]], axis=0)
 
 
+GATHER_SCOPES = ("all", "all", "ctx", "all", "seq")
+
+
 def project_kernel(
-    x_ref, gain_ref, cos_ref, sin_ref, w_ref, normed_ref, rms_ref, q_ref, kv_ref, w_s, sem
+    halves,
+    seq_count,
+    chip_count,
+    gain_src,
+    w_src,
+    wo_src,
+    g_src,
+    x_ref,
+    cos_ref,
+    sin_ref,
+    gains_ref,
+    w_ref,
+    kv_ref,
+    wo_ref,
+    g_ref,
+    normed_ref,
+    rms_ref,
+    q_ref,
+    gain_a_ref,
+    gain_f_ref,
+    kv_own,
+    w_s,
+    gains_s,
+    load_sem,
+    *sems,
 ):
     tile = KV_HEADS * HEAD_DIM
-    count = w_ref.shape[1] // tile
-
-    def load(number):
-        cols = pl.ds(pl.multiple_of(number * tile, tile), tile)
-        return pltpu.make_async_copy(w_ref.at[:, cols], w_s.at[:, cols], sem.at[number])
-
-    for number in range(count):
-        load(number).start()
+    model, own_rows, width = x_ref.shape[1], w_src.shape[0], w_src.shape[1]
+    count = width // tile
+    peers, begin, relays, waves, settle, end = spread_tools(
+        GATHER_SCOPES,
+        halves,
+        seq_count,
+        chip_count,
+        (gain_src, w_src, kv_own, wo_src, g_src),
+        (gains_ref, w_ref, kv_ref, wo_ref, g_ref),
+        sems[:5],
+        sems[5:10],
+        sems[10],
+    )
+    meet(peers)
+    begin((0, 1))
     x = x_ref[...].astype(F32)
     rms = lax.rsqrt(jnp.mean(x * x, axis=1, keepdims=True) + EPS)
     rms_ref[...] = rms
-    normed_ref[...] = (x * rms * gain_ref[...]).astype(BF16)
+    relays((0, 1))
+    waves((0, 1))
+    begin((3, 4))
+    settle((0, 1))
+
+    def load(number):
+        cols = pl.ds(pl.multiple_of(number * tile, tile), tile)
+        return pltpu.make_async_copy(
+            w_ref.at[:, :, :, cols], w_s.at[:, :, :, cols], load_sem.at[number]
+        )
+
+    load_gains = pltpu.make_async_copy(gains_ref, gains_s, load_sem.at[count])
+    load_gains.start()
+    for number in range(count):
+        load(number).start()
+    load_gains.wait()
+    for number in range(seq_count * 2 * chip_count):
+        at_seq, at_ctx = divmod(number, 2 * chip_count)
+        row = gains_s[at_seq, at_ctx, 0:1, :].astype(F32)
+        own = slice(number * own_rows, (number + 1) * own_rows)
+        gain_a_ref[:, own] = row[:, :own_rows]
+        gain_f_ref[:, own] = row[:, own_rows : 2 * own_rows]
+    normed_ref[...] = (x_ref[...].astype(F32) * rms_ref[...] * gain_a_ref[...]).astype(BF16)
 
     def product(number):
         load(number).wait()
         cols = pl.ds(pl.multiple_of(number * tile, tile), tile)
-        return dot32(normed_ref[...], w_s[:, cols], ((1,), (0,)))
+        return dot32(normed_ref[...], w_s[:, :, :, cols].reshape(model, tile), ((1,), (0,)))
 
     def rotated(value):
         turned = value.T
@@ -1275,39 +1369,60 @@
             pieces.append(one * cos_ref[...] + half_turn(one) * sin_ref[...])
         return jnp.concatenate(pieces, axis=0)
 
+    kv_own[:, :tile] = rotated(product(count - 2)).T.astype(BF16)
+    kv_own[:, tile:] = product(count - 1).astype(BF16)
+    begin((2,))
+    relays((3, 4))
+
     @pl.loop(0, count - 2)
     def _(number):
         own = pl.ds(pl.multiple_of(number * tile, tile), tile)
         q_ref[own, :] = rotated(product(number)).astype(BF16)
 
-    kv_ref[:, :tile] = rotated(product(count - 2)).T.astype(BF16)
-    kv_ref[:, tile:] = product(count - 1).astype(BF16)
-
-
-def project(x, gain, cosine, sine, w_qkv):
+    waves((3, 4))
+    waves((2,))
+    settle((3, 4, 2))
+    end()
+
+
+def project(collective_id, gain_row, w_qkv, w_out, g_own, x, cosine, sine):
+    seq_count, ctx_count = lax.axis_size("seq"), lax.axis_size("ctx")
+    chip_count = ctx_count // 2
     rows, model = x.shape
     width = w_qkv.shape[1]
     tile = KV_HEADS * HEAD_DIM
+    kv_like = jax.ShapeDtypeStruct((rows, 2 * tile), BF16)
+    shapes, halves, sems = spread_sems(
+        [gain_row, w_qkv, kv_like, w_out, g_own], GATHER_SCOPES, seq_count, chip_count
+    )
+    anywhere = pl.BlockSpec(memory_space=pl.ANY)
     return pl.pallas_call(
-        project_kernel,
+        functools.partial(project_kernel, halves, seq_count, chip_count),
         out_shape=(
+            *shapes,
             jax.ShapeDtypeStruct((rows, model), BF16),
             jax.ShapeDtypeStruct((rows, 1), F32),
             jax.ShapeDtypeStruct((width - 2 * tile, rows), BF16),
-            jax.ShapeDtypeStruct((rows, 2 * tile), BF16),
-        ),
-        in_specs=[vmem()] * 4 + [pl.BlockSpec(memory_space=pl.ANY)],
-        out_specs=(vmem(),) * 4,
+            jax.ShapeDtypeStruct((1, model), F32),
+            jax.ShapeDtypeStruct((1, model), F32),
+        ),
+        in_specs=[anywhere] * 4 + [vmem()] * 3,
+        out_specs=(anywhere,) * 5 + (vmem(),) * 5,
         scratch_shapes=[
-            pltpu.VMEM(w_qkv.shape, BF16),
-            pltpu.SemaphoreType.DMA((width // tile,)),
+            pltpu.VMEM((rows, 2 * tile), BF16),
+            pltpu.VMEM(shapes[1].shape, BF16),
+            pltpu.VMEM(shapes[0].shape, BF16),
+            pltpu.SemaphoreType.DMA((width // tile + 1,)),
+            *sems,
         ],
-        compiler_params=pltpu.CompilerParams(vmem_limit_bytes=VMEM_MOST),
+        compiler_params=pltpu.CompilerParams(
+            collective_id=collective_id, has_side_effects=True, vmem_limit_bytes=VMEM_MOST
+        ),
         cost_estimate=pl.CostEstimate(
-            flops=2 * rows * model * width, transcendentals=0, bytes_accessed=2 * model * width
+            flops=0, transcendentals=0, bytes_accessed=140 * 3_000_000
         ),
         name="project",
-    )(x, gain, cosine, sine, w_qkv)
+    )(gain_row, w_qkv, w_out, g_own, x, cosine, sine)
 
 
 def rotated_back(value, cos_ref, sin_ref):
@@ -1477,22 +1592,7 @@
 
     full_down = gather(w_down, "ctx")
     gain_row = jnp.pad(jnp.concatenate([attn_gain, ffn_gain])[None], ((0, 15), (0, 128 - 2 * own_rows)))
-    gains, w_qkv, gate_mine, up_mine = spread(
-        "gather_qkv",
-        0,
-        [
-            gain_row,
-            jnp.concatenate([w_query, w_key, w_value], axis=1),
-            split_columns(w_gate),
-            split_columns(w_up),
-        ],
-        ("all", "all", "swap", "swap"),
-        85,
-    )
-    gain_a = gains[:, :, 0, :own_rows].reshape(1, model).astype(F32)
-    gain_f = gains[:, :, 0, own_rows : 2 * own_rows].reshape(1, model).astype(F32)
-    w_qkv = w_qkv.reshape(model, q_width + 2 * kv_width)
-    full_down, gate_mine, up_mine = lax.optimization_barrier((full_down, gate_mine, up_mine))
+    gate_mine, up_mine = swap(0, [split_columns(w_gate), split_columns(w_up)])
     full_gate = gather(gate_mine, "ctx", 1).reshape(model, ff_part)
     full_up = gather(up_mine, "ctx", 1).reshape(model, ff_part)
 
@@ -1500,17 +1600,17 @@
         cotangent.reshape(rows, model).astype(F32) * selected.reshape(rows).astype(F32)[:, None]
     )
     tokens = hidden_in.reshape(rows, model).astype(F32)
-    x_norm, rms_a, q_t, kv_own = project(
-        hidden_in.reshape(rows, model), gain_a, cosine, sine, w_qkv
-    )
-    kv, full_out, g_all = spread(
-        "gather_kv_out",
+    _, w_qkv, kv, full_out, g_all, x_norm, rms_a, q_t, gain_a, gain_f = project(
         1,
-        [kv_own, w_out, grad_y.astype(BF16)],
-        ("ctx", "all", "seq"),
-        85,
-    )
-    g_all = g_all.reshape(seq_count * rows, model)
+        gain_row,
+        jnp.concatenate([w_query, w_key, w_value], axis=1),
+        w_out,
+        grad_y.astype(BF16),
+        hidden_in.reshape(rows, model),
+        cosine,
+        sine,
+    )
+    w_qkv = w_qkv.reshape(model, q_width + 2 * kv_width)
     kv = kv.reshape(length, 2 * kv_width)
     full_out = full_out.reshape(q_width, model)
     o_t, lse = attend_forward(place, block_order, doc_lengths, q_t, kv)

time: 609 us -> 589 us (0.967)
  Pallas kernels: 543 us -> 527 us
    pallas_call x1, Pallas kernels: 36.1 us -> 18.4 us  [attend_backward(): pl.pallas_call(functools.partial(attend_backward_kernel, span_len, spans)...]
    pallas_call x1, Pallas kernels: 25.3 us -> 12.6 us  [attend_forward(): pl.pallas_call(functools.partial(attend_forward_kernel, span_len, spans),...]
    pallas_call x2, Pallas kernels: 177 us -> 190 us  [fold(): pl.pallas_call(functools.partial(fold_kernel, tuple(kinds), tuple(chunk_c...]
    pallas_call x3 -> x2, Pallas kernels: 192 us -> 186 us  [the longest x1 165 us: project(): pl.pallas_call(functools.partial(project_kernel, halves, seq_count, chip_...]
  transfers between devices with their start and end apart: 6 -> 6, of which waited for: 0 -> 0; matrix products, arithmetic and copies ran while one was open for 6% -> 5% of each run, Pallas kernels for 86% -> 86%
where the time goes in v5:
time: 589 us; the launch traced here: 581 us
  Pallas kernels  527 us (89%)
  between operations  14.5 us (2%)
  matrix products  13.8 us (2%)
  local copies, waits for them, and re-layouts  12.1 us (2%)
  other arithmetic  11.7 us (2%)
    pallas_call x2, Pallas kernels, fold(): pl.pallas_call(functools.partial(fold_kernel, tuple(kinds), tuple(chunk_c...  190 us
    pallas_call x1, Pallas kernels, project(): pl.pallas_call(functools.partial(project_kernel, halves, seq_count, chip_...  165 us
    pallas_call x1, Pallas kernels, ffn_grad(): pl.pallas_call(functools.partial(ffn_grad_kernel, seq_count), out_shape=(...  54.3 us
    pallas_call x1, Pallas kernels, ffn_first(): pl.pallas_call(functools.partial(ffn_first_kernel, seq_count), out_shape=...  39.7 us
    pallas_call x1, Pallas kernels, ffn_act(): pl.pallas_call(ffn_act_kernel, out_shape=(jax.ShapeDtypeStruct((count, wi...  26.7 us
    pallas_call x1, Pallas kernels, swap(): pl.pallas_call(functools.partial(swap_kernel, scopes, halves, seq_count,...  21.1 us
    pallas_call x1, Pallas kernels, attend_backward(): pl.pallas_call(functools.partial(attend_backward_kernel, span_len, spans)...  18.4 us
    pallas_call x1, Pallas kernels, attend_forward(): pl.pallas_call(functools.partial(attend_forward_kernel, span_len, spans),...  12.6 us
  transfers between devices with their start and end apart: 6, of which 0 were waited for; matrix products, arithmetic and copies ran while one was open for 5% of the time, Pallas kernels for 86%

profile of v5, /device:TPU:0, one launch (start us, length us, event | category | flops | bytes accessed | tf_op | source)
XLA Modules:
  0.0 581.3 jit_solution(18211197555765934113)
XLA Ops:
  7.2 0.0 all-gather.6.cloned.1.call-start
  7.2 0.7 all-gather.6.cloned.1.call-update
  7.9 0.0 all-gather.4.cloned.1.call-start
  8.0 2.6 bitcast_bitcast_fusion
  10.6 21.1 %swap.1 = (bf16[4,64,1408]{2,1,0:T(8,128)(2,1)}, bf16[4,64,1408]{2,1,0:T(8,128)(2,1)}) custom-call(bf16[4,64,1408]{2,1,0:T(8,128)(2,1)} %get-tuple-element.110.refs_0_, bf16[4,64,1408]{2,1,0:T(8,128)(2,1)} %get-tuple-element.109.refs_1_), custom_call_target="tpu_custom_call" | custom-call | bytes 60000000 | tf_op jit(solution)/shard_map/swap/pallas_call | solution.py:550
  31.7 0.0 all-gather.4.cloned.1.call-update
  31.7 0.0 all-gather.8.cloned.1.call-start
  31.8 0.7 all-gather.8.cloned.1.call-update
  32.5 0.0 reduce-scatter.4.cloned.1.call-start
  32.5 0.1 maximum_bitcast_fusion.1
  32.6 0.6 pad.9.gain_src
  33.2 0.1 dynamic-slice_multiply_fusion
  33.3 0.1 convert_bitcast_fusion
  33.4 0.2 multiply_sine_fusion
  33.6 0.7 pad_maximum_fusion.1
  34.3 0.7 pad_maximum_fusion.w_src
  35.0 1.2 fusion.1.g_src
  36.2 165.0 %project.1 = (bf16[4,8,16,128]{3,2,1,0:T(8,128)(2,1)}, bf16[4,8,64,2560]{3,2,1,0:T(8,128)(2,1)}, bf16[8,256,512]{2,1,0:T(8,128)(2,1)}, bf16[4,8,64,2048]{3,2,1,0...) custom-call(bf16[16,128]{1,0:T(8,128)(2,1)} %pad.9.gain_src, ...), custom_call_target="tpu_custom_call" | custom-call | bytes 420000000 | tf_op jit(solution)/shard_map/project/pallas_call | solution.py:1399
  201.2 12.6 %attend_forward.1 = (bf16[2048,256]{1,0:T(8,128)(2,1)}, f32[2,4,1024]{2,1,0:T(4,128)}) custom-call(s32[1]{0:T(128)} %bitcast.1.place_ref, s32[16]{0:T(128)} %order_ref.3, s32[1,8]{1,0:T(1,128)} %lens_ref.3, bf16[2048,256]{1,0:T(8,128)(2,1)} %get-tuple-element.53.q_ref, bf16[2048,512]{1,0:T(8,128)(2,1)} %bitcast.73), custom_call_target="tpu_custom_call" | custom-call | flops 2147483648 | bytes 4194304 | tf_op jit(solution)/shard_map/attend_forward/pallas_call | solution.py:195
  213.8 6.3 %multiply_reduce_fusion.2 = (f32[256]{0:T(256)S(1)}, f32[256,2048]{1,0:T(8,128)S(1)}) fusion(bf16[2048,256]{1,0:T(8,128)(2,1)} %get-tuple-element.55.o_ref.refs_3_, bf16[2048,2048]{1,0:T(8,128)(2,1)} %bitcast.48, bf16[1,256,2048]{2,1,0:T(8,128)(2,1)S(1)} %copy-done), kind=kOutput, calls=%fused_computation.9 | convolution fusion | flops 2149580544 | bytes 12583936 | tf_op jit(solution)/shard_map/ht,hd->td/dot_general | solution.py:1618
  220.1 1.2 multiply_convert_fusion.f_ref
  221.3 39.7 %ffn_first.1 = (bf16[1024,2048]{1,0:T(8,128)(2,1)}, bf16[1024,2048]{1,0:T(8,128)(2,1)}, f32[1024,1408]{1,0:T(8,128)}, bf16[1024,1408]{1,0:T(8,128)(2,1)}) custom-call(bf16[256,2048]{1,0:T(8,128)(2,1)} %multiply_convert_fusion.f_ref, bf16[4,256,2048]{2,1,0:T(8,128)(2,1)} %get-tuple-element.58.g_ref, bf16[2048,1408]{1,0:T(8,128)(2,1)} %bitcast.69, ...), custom_call_target="tpu_custom_call" | custom-call | flops 23622320128 | bytes 48234496 | tf_op jit(solution)/shard_map/ffn_first/pallas_call | solution.py:1169
  261.0 0.0 all-gather.8.cloned.1.call-done
  261.0 26.7 %ffn_act.1 = (bf16[1024,1408]{1,0:T(8,128)(2,1)}, bf16[1024,1408]{1,0:T(8,128)(2,1)}, bf16[1024,1408]{1,0:T(8,128)(2,1)}, bf16[2048,1408]{1,0:T(8,128)(2,1)}) custom-call(bf16[1024,2048]{1,0:T(8,128)(2,1)} %get-tuple-element.60.f_ref, f32[1024,1408]{1,0:T(8,128)} %get-tuple-element.61.gate_ref, bf16[1024,1408]{1,0:T(8,128)(2,1)} %get-tuple-element.62.gh_ref, ...), custom_call_target="tpu_custom_call" | custom-call | flops 11811160064 | bytes 45613056 | tf_op jit(solution)/shard_map/ffn_act/pallas_call | solution.py:1206
  287.8 0.0 reduce-scatter.6.cloned.1.call-start
  287.8 54.3 %ffn_grad.1 = (f32[256,2048]{1,0:T(8,128)}, bf16[1024,2048]{1,0:T(8,128)(2,1)}, bf16[2048,1408]{1,0:T(8,128)(2,1)}, bf16[1408,2048]{1,0:T(8,128)(2,1)}) custom-call(bf16[1024,2048]{1,0:T(8,128)(2,1)} %get-tuple-element.60.f_ref, bf16[1024,1408]{1,0:T(8,128)(2,1)} %get-tuple-element.64.hid_ref, bf16[1024,1408]{1,0:T(8,128)(2,1)} %get-tuple-element.65.gg_ref, ...), custom_call_target="tpu_custom_call" | custom-call | flops 41339060224 | bytes 59768832 | tf_op jit(solution)/shard_map/ffn_grad/pallas_call | solution.py:1241
  342.2 0.0 reduce-scatter.8.cloned.1.call-start
  342.2 2.3 multiply_reduce_fusion
  344.5 0.7 fusion.refs_10_
  345.2 7.6 %convolution_convert_fusion.do_ref = bf16[2048,256]{1,0:T(8,128)(2,1)} fusion(bf16[2048,2048]{1,0:T(8,128)(2,1)} %bitcast.49, f32[256,2048]{1,0:T(8,128)S(1)} %fusion.refs_10_), kind=kOutput, calls=%fused_computation.1 | convolution fusion | flops 2148532224 | bytes 11534336 | tf_op jit(solution)/shard_map/td,hd->ht/dot_general | solution.py:1637
  352.8 18.4 %attend_backward.1 = (f32[2048,256]{1,0:T(8,128)}, bf16[2048,512]{1,0:T(8,128)(2,1)}) custom-call(s32[1]{0:T(128)} %bitcast.1.place_ref, s32[16]{0:T(128)} %order_ref.3, s32[1,8]{1,0:T(1,128)} %lens_ref.3, bf16[2048,256]{1,0:T(8,128)(2,1)} %get-tuple-element.53.q_ref, bf16[2048,512]{1,0:T(8,128)(2,1)} %bitcast.74, ...), custom_call_target="tpu_custom_call" | custom-call | flops 5368709120 | bytes 9437184 | tf_op jit(solution)/shard_map/attend_backward/pallas_call | solution.py:222
  371.2 0.1 reshape.159
  371.3 65.7 %fold_kv.1 = (f32[256,512]{1,0:T(8,128)}, f32[256,2048]{1,0:T(8,128)}, bf16[2048,2048]{1,0:T(8,128)(2,1)}, bf16[2048,2048]{1,0:T(8,128)(2,1)}, bf16[2048,512]{1,...) custom-call(bf16[1,4,2,256,512]{4,3,2,1,0:T(8,128)(2,1)} %bitcast.60, bf16[4,256,2048]{2,1,0:T(8,128)(2,1)} %bitcast.57, ...), custom_call_target="tpu_custom_call" | custom-call | bytes 180000000 | tf_op jit(solution)/shard_map/fold_kv/pallas_call | solution.py:849
  437.0 0.7 convert_reduce_fusion
  437.7 0.1 reshape.158
  437.8 0.1 maximum_bitcast_fusion
  437.9 0.7 pad.10.clone
  438.6 123.9 %fold_weights.1 = (f32[64,2048]{1,0:T(8,128)}, f32[64,2048]{1,0:T(8,128)}, f32[64,512]{1,0:T(8,128)}, f32[16,128]{1,0:T(8,128)}, f32[64,5632]{1,0:T(8,128)}, /*index=5*/f32[64,5632]{1,0:T(8,128)}) custom-call(bf16[4,4,2,64,2048]{4,3,2,1,0:T(8,128)(2,1)} %bitcast.53, bf16[4,4,2,64,2048]{4,3,2,1,0:T(8,128)(2,1)} %bitcast.54, ...), custom_call_target="tpu_custom_call" | custom-call | bytes 330000000 | tf_op jit(solution)/shard_map/fold_weights/pallas_call | solution.py:849
  562.5 1.3 slice_bitcast_fusion
  563.9 1.5 fusion.4
  565.4 1.2 fusion.2
  566.6 2.5 convert_element_type.69
  569.1 1.3 copy.38
  570.5 0.1 copy-done.9
  570.5 0.8 copy.39
  571.3 0.8 copy.40
  572.1 1.1 copy.41
  573.2 1.1 copy.42
  (48 shorter events, 0.2 us)
Async XLA Ops:
  7.2 214.1 %all-gather.6.cloned.1.call-start = ((), (), s32[]{:S(2)}) async-start(), calls=%async_computation.4 | async-start | bytes 6488064 | tf_op jit(solution)/shard_map/all_gather | solution.py:1537
  7.9 213.4 %all-gather.4.cloned.1.call-start = ((), (), s32[]{:S(2)}) async-start(), calls=%async_computation.3 | async-start | bytes 6488064 | tf_op jit(solution)/shard_map/all_gather | solution.py:1537
  10.5 22.0 %copy-start.14 = (s32[1,256]{1,0:T(1,128)S(1)}, s32[1,256]{1,0:T(1,128)}, u32[]{:S(2)}) copy-start(s32[1,256]{1,0:T(1,128)} %param.26) | copy-start | bytes 3076
  10.5 22.0 %copy-start.15 = (bf16[64]{0:T(256)(128)(2,1)S(1)}, bf16[64]{0:T(256)(128)(2,1)}, u32[]{:S(2)}) copy-start(bf16[64]{0:T(256)(128)(2,1)} %param.20) | copy-start | bytes 388
  10.5 22.0 %copy-start.16 = (bf16[64]{0:T(256)(128)(2,1)S(1)}, bf16[64]{0:T(256)(128)(2,1)}, u32[]{:S(2)}) copy-start(bf16[64]{0:T(256)(128)(2,1)} %param.15) | copy-start | bytes 388
  10.5 22.7 %copy-start.17 = (s32[16]{0:T(128)S(1)}, s32[16]{0:T(128)}, u32[]{:S(2)}) copy-start(s32[16]{0:T(128)} %order_ref.3) | copy-start | bytes 196
  10.5 23.7 %copy-start.10 = (bf16[64,2048]{1,0:T(8,128)(2,1)S(1)}, bf16[64,2048]{1,0:T(8,128)(2,1)}, u32[]{:S(2)}) copy-start(bf16[64,2048]{1,0:T(8,128)(2,1)} %param.16) | copy-start | bytes 786436
  10.5 23.7 %copy-start.12 = (bf16[64,256]{1,0:T(8,128)(2,1)S(1)}, bf16[64,256]{1,0:T(8,128)(2,1)}, u32[]{:S(2)}) copy-start(bf16[64,256]{1,0:T(8,128)(2,1)} %param.18) | copy-start | bytes 98308
  10.6 23.7 %copy-start.13 = (bf16[64,256]{1,0:T(8,128)(2,1)S(1)}, bf16[64,256]{1,0:T(8,128)(2,1)}, u32[]{:S(2)}) copy-start(bf16[64,256]{1,0:T(8,128)(2,1)} %param.17) | copy-start | bytes 98308
  10.6 24.4 %copy-start.3 = (bf16[1,256,2048]{2,1,0:T(8,128)(2,1)S(1)}, bf16[1,256,2048]{2,1,0:T(8,128)(2,1)}, u32[]{:S(2)}) copy-start(bf16[1,256,2048]{2,1,0:T(8,128)(2,1)} %param.24) | copy-start | bytes 3145732
  31.7 229.3 %all-gather.8.cloned.1.call-start = ((), (), s32[]{:S(2)}) async-start(), calls=%async_computation.5 | async-start | bytes 6488064 | tf_op jit(solution)/shard_map/all_gather | solution.py:1537
  32.5 338.7 %reduce-scatter.4.cloned.1.call-start = ((), (), s32[]{:S(2)}) async-start(), calls=%async_computation.6 | async-start | bytes 6488064 | tf_op jit(solution)/shard_map/reduce_scatter | solution.py:1541
  201.2 12.6 %copy-start = (bf16[1,256,2048]{2,1,0:T(8,128)(2,1)S(1)}, bf16[1,256,2048]{2,1,0:T(8,128)(2,1)}, u32[]{:S(2)}) copy-start(bf16[1,256,2048]{2,1,0:T(8,128)(2,1)} %param.14) | copy-start | bytes 3145732
  213.8 6.3 %copy-start.11 = (f32[1,2048]{1,0:T(1,128)S(1)}, f32[1,2048]{1,0:T(1,128)}, u32[]{:S(2)}) copy-start(f32[1,2048]{1,0:T(1,128)} %get-tuple-element.57) | copy-start | bytes 24580
  287.8 150.8 %reduce-scatter.6.cloned.1.call-start = ((), (), s32[]{:S(2)}) async-start(), calls=%async_computation.7 | async-start | bytes 6488064 | tf_op jit(solution)/shard_map/reduce_scatter | solution.py:1541
  342.2 224.4 %reduce-scatter.8.cloned.1.call-start = ((), (), s32[]{:S(2)}) async-start(), calls=%async_computation.8 | async-start | bytes 6488064 | tf_op jit(solution)/shard_map/reduce_scatter | solution.py:1541
  342.2 2.3 copy-start.1
  345.2 7.6 %copy-start.2 = (f32[256,2048]{1,0:T(8,128)}, f32[256,2048]{1,0:T(8,128)S(1)}, u32[]{:S(2)}) copy-start(f32[256,2048]{1,0:T(8,128)S(1)} %fusion.refs_10_) | copy-start | bytes 6291460
  438.6 126.8 %copy-start.5 = (f32[256,2048]{1,0:T(8,128)S(1)}, f32[256,2048]{1,0:T(8,128)}, u32[]{:S(2)}) copy-start(f32[256,2048]{1,0:T(8,128)} %get-tuple-element.80) | copy-start | bytes 6291460
  566.6 2.5 copy-start.4
  569.1 1.4 copy-start.9
  569.1 2.2 copy-start.8
  570.5 1.6 copy-start.7
  571.3 1.9 copy-start.6
Sparse Core Ops, SparseCore 0:
  9.7 76.4 all-gather.5
  87.7 77.1 all-gather.3
  166.5 63.4 all-gather.7
  287.9 65.6 reduce-scatter.3
  355.7 80.0 reduce-scatter.5
  438.0 90.7 reduce-scatter.7

commit v6 on v5

--- a/solution.py
+++ b/solution.py
@@ -66,8 +66,30 @@
 
 
 def attend_forward_kernel(
-    span_len, spans, place_ref, order_ref, lens_ref, q_ref, kv_ref, o_ref, lse_ref, top_ref, sum_ref, acc_ref
+    span_len,
+    spans,
+    place_ref,
+    order_ref,
+    lens_ref,
+    q_ref,
+    kv_ref,
+    x_ref,
+    gain_ref,
+    wo_ref,
+    o_ref,
+    lse_ref,
+    middle_ref,
+    rms_ref,
+    f_ref,
+    top_ref,
+    sum_ref,
+    acc_ref,
+    o_s,
+    wo_s,
+    load_sem,
 ):
+    load = pltpu.make_async_copy(wo_ref, wo_s, load_sem)
+    load.start()
     own_count = q_ref.shape[1] // span_len
     own_first = place_ref[0] * own_count
     width = KV_HEADS * HEAD_DIM
@@ -110,6 +132,19 @@
             mixed = acc_ref[head] / total
             unstack_heads(o_ref, mixed, head, own, span_len)
             lse_ref[own, head : head + 1, :] = top_ref[head : head + 1, :] + jnp.log2(total)
+    o_s[...] = o_ref[...].T
+    load.wait()
+
+    def out(cols):
+        middle_ref[:, cols] = x_ref[:, cols].astype(F32) + dot32(
+            o_s[...], wo_s[:, cols], ((1,), (0,))
+        )
+
+    tiles(x_ref.shape[1], 256, out)
+    middle = middle_ref[...]
+    rms = lax.rsqrt(jnp.mean(middle * middle, axis=1, keepdims=True) + EPS)
+    rms_ref[...] = rms
+    f_ref[...] = (middle * rms * gain_ref[...]).astype(BF16)
 
 
 def attend_backward_kernel(
@@ -122,13 +157,40 @@
     kv_ref,
     o_ref,
     lse_ref,
-    do_ref,
+    gf_ref,
+    middle_ref,
+    rms_ref,
+    gain_ref,
+    g_ref,
+    wo_ref,
     dq_ref,
     dkv_ref,
+    grad_ref,
+    gain_out,
     dkv_acc,
     dq_acc,
     delta_ref,
+    ga_s,
+    do_ref,
+    wo_s,
+    load_sem,
 ):
+    load = pltpu.make_async_copy(wo_ref, wo_s, load_sem)
+    load.start()
+    rms = rms_ref[...]
+    gain_out[...] = jnp.sum(gf_ref[...] * (middle_ref[...] * rms), axis=0, keepdims=True)
+    scaled = gf_ref[...] * gain_ref[...]
+    mean = jnp.mean(scaled * middle_ref[...], axis=1, keepdims=True)
+    grad_ref[...] = g_ref[...].astype(F32) + (
+        rms * scaled - middle_ref[...] * (rms * rms * rms * mean)
+    )
+    ga_s[...] = grad_ref[...].astype(BF16)
+    load.wait()
+
+    def grad_mix(own):
+        do_ref[own, :] = dot32(wo_s[own, :], ga_s[...], ((1,), (1,))).astype(BF16)
+
+    tiles(do_ref.shape[0], 256, grad_mix)
     own_count = q_ref.shape[1] // span_len
     own_first = place_ref[0] * own_count
     width = KV_HEADS * HEAD_DIM
@@ -187,59 +249,75 @@
     return pl.BlockSpec(memory_space=pltpu.VMEM)
 
 
-def attend_forward(place, block_order, doc_lengths, q_t, kv):
+def attend_forward(place, block_order, doc_lengths, q_t, kv, x, gain, w_out):
     spans = block_order.shape[0]
     span_len = kv.shape[0] // spans
     own_count = q_t.shape[1] // span_len
     lanes = GROUP * span_len
+    rows, model = x.shape
     return pl.pallas_call(
         functools.partial(attend_forward_kernel, span_len, spans),
         out_shape=(
             jax.ShapeDtypeStruct(q_t.shape, BF16),
             jax.ShapeDtypeStruct((own_count, KV_HEADS, lanes), F32),
-        ),
-        in_specs=[smem(), smem(), smem(), vmem(), vmem()],
-        out_specs=(vmem(), vmem()),
+            jax.ShapeDtypeStruct((rows, model), F32),
+            jax.ShapeDtypeStruct((rows, 1), F32),
+            jax.ShapeDtypeStruct((rows, model), BF16),
+        ),
+        in_specs=[smem(), smem(), smem()] + [vmem()] * 4 + [pl.BlockSpec(memory_space=pl.ANY)],
+        out_specs=(vmem(),) * 5,
         scratch_shapes=[
             pltpu.VMEM((KV_HEADS, lanes), F32),
             pltpu.VMEM((KV_HEADS, lanes), F32),
             pltpu.VMEM((KV_HEADS, HEAD_DIM, lanes), F32),
+            pltpu.VMEM(q_t.shape[::-1], BF16),
+            pltpu.VMEM(w_out.shape, BF16),
+            pltpu.SemaphoreType.DMA,
         ],
         compiler_params=pltpu.CompilerParams(vmem_limit_bytes=VMEM_MOST),
         cost_estimate=pl.CostEstimate(
-            flops=2 * HEADS * HEAD_DIM * kv.shape[0] * q_t.shape[1],
-            transcendentals=HEADS * kv.shape[0] * q_t.shape[1] // 2,
-            bytes_accessed=4 * q_t.size + 2 * kv.size,
+            flops=2 * HEADS * HEAD_DIM * kv.shape[0] * rows + 2 * w_out.size * rows,
+            transcendentals=HEADS * kv.shape[0] * rows // 2,
+            bytes_accessed=4 * q_t.size + 2 * kv.size + 2 * w_out.size + 8 * rows * model,
         ),
         name="attend_forward",
-    )(place, block_order, doc_lengths, q_t, kv)
-
-
-def attend_backward(place, block_order, doc_lengths, q_t, kv, o_t, lse, do_t):
+    )(place, block_order, doc_lengths, q_t, kv, x, gain, w_out)
+
+
+def attend_backward(
+    place, block_order, doc_lengths, q_t, kv, o_t, lse, grad_f, middle, rms, gain, g_own, w_out
+):
     spans = block_order.shape[0]
     span_len = kv.shape[0] // spans
     lanes = GROUP * span_len
+    rows, model = middle.shape
     return pl.pallas_call(
         functools.partial(attend_backward_kernel, span_len, spans),
         out_shape=(
             jax.ShapeDtypeStruct(q_t.shape, F32),
             jax.ShapeDtypeStruct(kv.shape, BF16),
-        ),
-        in_specs=[smem(), smem(), smem(), vmem(), vmem(), vmem(), vmem(), vmem()],
-        out_specs=(vmem(), vmem()),
+            jax.ShapeDtypeStruct((rows, model), F32),
+            jax.ShapeDtypeStruct((1, model), F32),
+        ),
+        in_specs=[smem(), smem(), smem()] + [vmem()] * 9 + [pl.BlockSpec(memory_space=pl.ANY)],
+        out_specs=(vmem(),) * 4,
         scratch_shapes=[
             pltpu.VMEM(kv.shape, F32),
             pltpu.VMEM((KV_HEADS, HEAD_DIM, lanes), F32),
             pltpu.VMEM((KV_HEADS, lanes), F32),
+            pltpu.VMEM((rows, model), BF16),
+            pltpu.VMEM(q_t.shape, BF16),
+            pltpu.VMEM(w_out.shape, BF16),
+            pltpu.SemaphoreType.DMA,
         ],
         compiler_params=pltpu.CompilerParams(vmem_limit_bytes=VMEM_MOST),
         cost_estimate=pl.CostEstimate(
-            flops=5 * HEADS * HEAD_DIM * kv.shape[0] * q_t.shape[1],
-            transcendentals=HEADS * kv.shape[0] * q_t.shape[1] // 2,
-            bytes_accessed=10 * q_t.size + 4 * kv.size,
+            flops=5 * HEADS * HEAD_DIM * kv.shape[0] * rows + 2 * w_out.size * rows,
+            transcendentals=HEADS * kv.shape[0] * rows // 2,
+            bytes_accessed=10 * q_t.size + 4 * kv.size + 2 * w_out.size + 14 * rows * model,
         ),
         name="attend_backward",
-    )(place, block_order, doc_lengths, q_t, kv, o_t, lse, do_t)
+    )(place, block_order, doc_lengths, q_t, kv, o_t, lse, grad_f, middle, rms, gain, g_own, w_out)
 
 
 MESH = pl.DeviceIdType.MESH
@@ -1541,15 +1619,6 @@
     return lax.psum_scatter(value, axes, scatter_dimension=dim, tiled=True)
 
 
-def norm_back(grad_normed, source, rms_val, gain_val, normed):
-    grad_gain = jnp.sum(grad_normed * normed, axis=0)
-    scaled = grad_normed * gain_val
-    grad_source = rms_val * scaled - source * (rms_val * rms_val * rms_val) * jnp.mean(
-        scaled * source, axis=1, keepdims=True
-    )
-    return (grad_gain, grad_source)
-
-
 def local(
     hidden_in,
     attn_gain,
@@ -1596,16 +1665,15 @@
     full_gate = gather(gate_mine, "ctx", 1).reshape(model, ff_part)
     full_up = gather(up_mine, "ctx", 1).reshape(model, ff_part)
 
-    grad_y = (
-        cotangent.reshape(rows, model).astype(F32) * selected.reshape(rows).astype(F32)[:, None]
-    )
-    tokens = hidden_in.reshape(rows, model).astype(F32)
+    g_own = jnp.where(
+        selected.reshape(rows)[:, None] != 0, cotangent.reshape(rows, model), jnp.zeros((), BF16)
+    )
     _, w_qkv, kv, full_out, g_all, x_norm, rms_a, q_t, gain_a, gain_f = project(
         1,
         gain_row,
         jnp.concatenate([w_query, w_key, w_value], axis=1),
         w_out,
-        grad_y.astype(BF16),
+        g_own,
         hidden_in.reshape(rows, model),
         cosine,
         sine,
@@ -1613,13 +1681,9 @@
     w_qkv = w_qkv.reshape(model, q_width + 2 * kv_width)
     kv = kv.reshape(length, 2 * kv_width)
     full_out = full_out.reshape(q_width, model)
-    o_t, lse = attend_forward(place, block_order, doc_lengths, q_t, kv)
-
-    middle = tokens + jnp.einsum("ht,hd->td", o_t, full_out, preferred_element_type=F32)
-    rms_f = lax.rsqrt(jnp.mean(middle * middle, axis=1, keepdims=True) + EPS)
-    normed_f = middle * rms_f
-    f_norm = (normed_f * gain_f).astype(BF16)
-
+    o_t, lse, middle, rms_f, f_norm = attend_forward(
+        place, block_order, doc_lengths, q_t, kv, hidden_in.reshape(rows, model), gain_f, full_out
+    )
     f_all, g_slots, gate, grad_hidden = ffn_first(2, f_norm, g_all, full_gate, full_down)
     hidden_act, grad_gate, grad_up, part_gate = ffn_act(f_all, gate, grad_hidden, full_up)
     grad_f_norm, ffn_part, part_up, part_down = ffn_grad(
@@ -1631,20 +1695,31 @@
 
     rows_gate = ffn_rows(part_gate)
     rows_up = ffn_rows(part_up)
-    grad_ffn_gain, grad_from_f = norm_back(grad_f_norm, middle, rms_f, gain_f, normed_f)
-    grad_middle = grad_y + grad_from_f
-    g_attn = grad_middle.astype(BF16)
-    do_t = jnp.einsum("td,hd->ht", g_attn, full_out, preferred_element_type=F32).astype(BF16)
-    dq_t, dkv = attend_backward(place, block_order, doc_lengths, q_t, kv, o_t, lse, do_t)
+    dq_t, dkv, grad_middle, grad_ffn_gain = attend_backward(
+        place,
+        block_order,
+        doc_lengths,
+        q_t,
+        kv,
+        o_t,
+        lse,
+        grad_f_norm,
+        middle,
+        rms_f,
+        gain_f,
+        g_own,
+        full_out,
+    )
     part_down, rows_gate, dkv = lax.optimization_barrier((part_down, rows_gate, dkv))
     grad_w_down = scatter_sum(part_down, "ctx").astype(F32)
-    _, ffn_out, part_out, part_query, part_kv, grad_input, grad_attn_gain = fold(
+    _, ffn_out, grad_w_gate, part_out, part_query, part_kv, grad_input, grad_attn_gain = fold(
         "fold_kv",
         4,
         [dkv, ffn_part],
         ("ctx", "seq"),
         (1, 2),
         60,
+        [rows_gate],
         work=back_work(
             dq_t,
             o_t,
@@ -1663,14 +1738,14 @@
         [grad_attn_gain.reshape(-1, own_rows), grad_ffn_gain.reshape(-1, own_rows)], axis=1
     )
     part_gains = jnp.pad(part_gains[:, None], ((0, 0), (0, 15), (0, 128 - 2 * own_rows)))
-    grad_w_out, grad_w_query, grad_w_kv, grad_gains, grad_w_gate, grad_w_up = fold(
+    grad_w_out, grad_w_query, grad_w_kv, grad_gains, grad_w_up = fold(
         "fold_weights",
         5,
         [part_out, part_query, part_kv, part_gains.reshape(-1, 128).astype(BF16)],
         ("all", "all", "all", "all"),
         (8, 8, 2, 1),
         110,
-        [rows_gate, rows_up],
+        [rows_up],
     )
     return (
         output,

time: 589 us -> 587 us (level)
  Pallas kernels: 527 us -> 542 us
  matrix products: 13.8 us -> 0 us
    pallas_call x1, Pallas kernels: 18.4 us -> 35.5 us  [attend_backward(): pl.pallas_call(functools.partial(attend_backward_kernel, span_len, spans)...]
    dot_general x2 -> x0, matrix products: 13.8 us -> none  [the longest x1 7.57 us: local(): jnp.einsum('td,hd->ht', g_attn, full_out, preferred_element_type=F32)]
    pallas_call x2, Pallas kernels: 190 us -> 176 us  [fold(): pl.pallas_call(functools.partial(fold_kernel, tuple(kinds), tuple(chunk_c...]
    pallas_call x1, Pallas kernels: 12.6 us -> 23.2 us  [attend_forward(): pl.pallas_call(functools.partial(attend_forward_kernel, span_len, spans),...]
  transfers between devices with their start and end apart: 6 -> 6, of which waited for: 0 -> 0; matrix products, arithmetic and copies ran while one was open for 5% -> 2% of each run, Pallas kernels for 86% -> 89%
where the time goes in v6:
time: 587 us; the launch traced here: 579 us
  Pallas kernels  542 us (92%)
  between operations  14.8 us (3%)
  local copies, waits for them, and re-layouts  12.8 us (2%)
  other arithmetic  7.48 us (1%)
    pallas_call x2, Pallas kernels, fold(): pl.pallas_call(functools.partial(fold_kernel, tuple(kinds), tuple(chunk_c...  176 us
    pallas_call x1, Pallas kernels, project(): pl.pallas_call(functools.partial(project_kernel, halves, seq_count, chip_...  165 us
    pallas_call x1, Pallas kernels, ffn_grad(): pl.pallas_call(functools.partial(ffn_grad_kernel, seq_count), out_shape=(...  53.7 us
    pallas_call x1, Pallas kernels, ffn_first(): pl.pallas_call(functools.partial(ffn_first_kernel, seq_count), out_shape=...  41.3 us
    pallas_call x1, Pallas kernels, attend_backward(): pl.pallas_call(functools.partial(attend_backward_kernel, span_len, spans)...  35.5 us
    pallas_call x1, Pallas kernels, ffn_act(): pl.pallas_call(ffn_act_kernel, out_shape=(jax.ShapeDtypeStruct((count, wi...  26.5 us
    pallas_call x1, Pallas kernels, attend_forward(): pl.pallas_call(functools.partial(attend_forward_kernel, span_len, spans),...  23.2 us
    pallas_call x1, Pallas kernels, swap(): pl.pallas_call(functools.partial(swap_kernel, scopes, halves, seq_count,...  21.1 us
  transfers between devices with their start and end apart: 6, of which 0 were waited for; matrix products, arithmetic and copies ran while one was open for 2% of the time, Pallas kernels for 89%

profile of v6, /device:TPU:0, one launch (start us, length us, event | category | flops | bytes accessed | tf_op | source)
XLA Modules:
  0.0 578.9 jit_solution(924790424402392330)
XLA Ops:
  7.2 0.0 all-gather.6.cloned.1.call-start
  7.2 0.7 all-gather.6.cloned.1.call-update
  7.9 0.0 all-gather.4.cloned.1.call-start
  8.0 2.7 bitcast_bitcast_fusion
  10.7 21.1 %swap.1 = (bf16[4,64,1408]{2,1,0:T(8,128)(2,1)}, bf16[4,64,1408]{2,1,0:T(8,128)(2,1)}) custom-call(bf16[4,64,1408]{2,1,0:T(8,128)(2,1)} %get-tuple-element.114.refs_0_, bf16[4,64,1408]{2,1,0:T(8,128)(2,1)} %get-tuple-element.113.refs_1_), custom_call_target="tpu_custom_call" | custom-call | bytes 60000000 | tf_op jit(solution)/shard_map/swap/pallas_call | solution.py:628
  31.8 0.0 all-gather.4.cloned.1.call-update
  31.8 0.0 all-gather.8.cloned.1.call-start
  31.8 0.7 all-gather.8.cloned.1.call-update
  32.5 0.0 reduce-scatter.4.cloned.1.call-start
  32.6 0.1 maximum_bitcast_fusion.1
  32.7 0.6 pad.9.gain_src
  33.3 0.1 dynamic-slice_multiply_fusion
  33.4 0.1 convert_bitcast_fusion
  33.5 0.2 multiply_sine_fusion
  33.7 0.7 pad_maximum_fusion.1
  34.3 0.7 pad_maximum_fusion.w_src
  35.1 1.1 bitcast_select_fusion.g_src.g_ref
  36.2 165.0 %project.1 = (bf16[4,8,16,128]{3,2,1,0:T(8,128)(2,1)}, bf16[4,8,64,2560]{3,2,1,0:T(8,128)(2,1)}, bf16[8,256,512]{2,1,0:T(8,128)(2,1)}, bf16[4,8,64,2048]{3,2,1,0...) custom-call(bf16[16,128]{1,0:T(8,128)(2,1)} %pad.9.gain_src, ...), custom_call_target="tpu_custom_call" | custom-call | bytes 420000000 | tf_op jit(solution)/shard_map/project/pallas_call | solution.py:1477
  201.2 23.2 %attend_forward.1 = (bf16[2048,256]{1,0:T(8,128)(2,1)}, f32[2,4,1024]{2,1,0:T(4,128)}, f32[256,2048]{1,0:T(8,128)}, f32[256,1]{1,0:T(8,128)}, bf16[256,2048]{1,0:T(8,128)(2,1)}) custom-call(s32[1]{0:T(128)} %bitcast.place_ref, s32[16]{0:T(128)} %order_ref.3, s32[1,8]{1,0:T(1,128)} %lens_ref.3, bf16[2048,256]{1,0:T(8,128)(2,1)} %get-tuple-element.58.q_ref, ...), custom_call_target="tpu_custom_call" | custom-call | flops 4294967296 | bytes 16777216 | tf_op jit(solution)/shard_map/attend_forward/pallas_call | solution.py:258
  224.3 0.0 all-gather.6.cloned.1.call-done.wd_ref
  224.4 0.0 all-gather.4.cloned.1.call-done
  224.4 41.3 %ffn_first.1 = (bf16[1024,2048]{1,0:T(8,128)(2,1)}, bf16[1024,2048]{1,0:T(8,128)(2,1)}, f32[1024,1408]{1,0:T(8,128)}, bf16[1024,1408]{1,0:T(8,128)(2,1)}) custom-call(bf16[256,2048]{1,0:T(8,128)(2,1)} %get-tuple-element.63.f_ref, bf16[4,256,2048]{2,1,0:T(8,128)(2,1)} %get-tuple-element.64.g_ref, bf16[2048,1408]{1,0:T(8,128)(2,1)} %bitcast.57, ...), custom_call_target="tpu_custom_call" | custom-call | flops 23622320128 | bytes 48234496 | tf_op jit(solution)/shard_map/ffn_first/pallas_call | solution.py:1247
  265.7 0.0 all-gather.8.cloned.1.call-done
  265.7 26.5 %ffn_act.1 = (bf16[1024,1408]{1,0:T(8,128)(2,1)}, bf16[1024,1408]{1,0:T(8,128)(2,1)}, bf16[1024,1408]{1,0:T(8,128)(2,1)}, bf16[2048,1408]{1,0:T(8,128)(2,1)}) custom-call(bf16[1024,2048]{1,0:T(8,128)(2,1)} %get-tuple-element.66.f_ref, f32[1024,1408]{1,0:T(8,128)} %get-tuple-element.67.gate_ref, bf16[1024,1408]{1,0:T(8,128)(2,1)} %get-tuple-element.68.gh_ref, ...), custom_call_target="tpu_custom_call" | custom-call | flops 11811160064 | bytes 45613056 | tf_op jit(solution)/shard_map/ffn_act/pallas_call | solution.py:1284
  292.3 0.0 reduce-scatter.4.cloned.1.call-update
  292.3 0.0 reduce-scatter.6.cloned.1.call-start
  292.3 53.7 %ffn_grad.1 = (f32[256,2048]{1,0:T(8,128)}, bf16[1024,2048]{1,0:T(8,128)(2,1)}, bf16[2048,1408]{1,0:T(8,128)(2,1)}, bf16[1408,2048]{1,0:T(8,128)(2,1)}) custom-call(bf16[1024,2048]{1,0:T(8,128)(2,1)} %get-tuple-element.66.f_ref, bf16[1024,1408]{1,0:T(8,128)(2,1)} %get-tuple-element.70.hid_ref, bf16[1024,1408]{1,0:T(8,128)(2,1)} %get-tuple-element.71.gg_ref, ...), custom_call_target="tpu_custom_call" | custom-call | flops 41339060224 | bytes 59768832 | tf_op jit(solution)/shard_map/ffn_grad/pallas_call | solution.py:1319
  346.1 0.0 reduce-scatter.6.cloned.1.call-update
  346.1 0.0 reduce-scatter.8.cloned.1.call-start
  346.2 35.5 %attend_backward.1 = (f32[2048,256]{1,0:T(8,128)}, bf16[2048,512]{1,0:T(8,128)(2,1)}, f32[256,2048]{1,0:T(8,128)}, f32[1,2048]{1,0:T(1,128)}) custom-call(s32[1]{0:T(128)} %bitcast.place_ref, s32[16]{0:T(128)} %order_ref.3, s32[1,8]{1,0:T(1,128)} %lens_ref.3, bf16[2048,256]{1,0:T(8,128)(2,1)} %get-tuple-element.58.q_ref, bf16[2048,512]{1,0:T(8,128)(2,1)} %bitcast.62, ...), custom_call_target="tpu_custom_call" | custom-call | flops 7516192768 | bytes 25165824 | tf_op jit(solution)/shard_map/attend_backward/pallas_call | solution.py:294
  381.6 0.0 reduce-scatter.4.cloned.1.call-done.refs_2_
  381.7 0.7 copy-done.11
  382.4 0.1 reshape.144
  382.5 62.7 %fold_kv.1 = (f32[256,512]{1,0:T(8,128)}, f32[256,2048]{1,0:T(8,128)}, f32[64,5632]{1,0:T(8,128)}, bf16[2048,2048]{1,0:T(8,128)(2,1)}, bf16[2048,2048]{1,0:T(8,1...) custom-call(bf16[1,4,2,256,512]{4,3,2,1,0:T(8,128)(2,1)} %bitcast.49, ...), custom_call_target="tpu_custom_call" | custom-call | bytes 180000000 | tf_op jit(solution)/shard_map/fold_kv/pallas_call | solution.py:927
  445.1 0.7 convert_reduce_fusion.1
  445.9 0.1 reshape.143
  445.9 0.1 maximum_bitcast_fusion
  446.0 0.7 pad.10.clone
  446.7 113.2 %fold_weights.1 = (f32[64,2048]{1,0:T(8,128)}, f32[64,2048]{1,0:T(8,128)}, f32[64,512]{1,0:T(8,128)}, f32[16,128]{1,0:T(8,128)}, f32[64,5632]{1,0:T(8,128)}) custom-call(bf16[4,4,2,64,2048]{4,3,2,1,0:T(8,128)(2,1)} %bitcast.41, bf16[4,4,2,64,2048]{4,3,2,1,0:T(8,128)(2,1)} %bitcast.42, bf16[4,4,2,64,512]{4,3,2,1,0:T(8,128)(2,1)} %bitcast.50, ...), custom_call_target="tpu_custom_call" | custom-call | bytes 330000000 | tf_op jit(solution)/shard_map/fold_weights/pallas_call | solution.py:927
  559.9 1.3 slice_bitcast_fusion
  561.3 1.5 fusion.1
  562.8 1.2 fusion
  564.1 2.4 convert_element_type.29
  566.5 1.3 copy.38
  567.8 0.8 copy.39
  568.6 0.8 copy.40
  569.4 1.1 copy.41
  570.5 1.1 copy.42
  (38 shorter events, 0.2 us)
Async XLA Ops:
  7.2 217.2 %all-gather.6.cloned.1.call-start = ((), (), s32[]{:S(2)}) async-start(), calls=%async_computation.4 | async-start | bytes 6488064 | tf_op jit(solution)/shard_map/all_gather | solution.py:1615
  7.9 216.5 %all-gather.4.cloned.1.call-start = ((), (), s32[]{:S(2)}) async-start(), calls=%async_computation.3 | async-start | bytes 6488064 | tf_op jit(solution)/shard_map/all_gather | solution.py:1615
  8.0 24.6 %copy-start.13 = (bf16[64]{0:T(256)(128)(2,1)S(1)}, bf16[64]{0:T(256)(128)(2,1)}, u32[]{:S(2)}) copy-start(bf16[64]{0:T(256)(128)(2,1)} %param.20) | copy-start | bytes 388
  8.0 24.6 %copy-start.14 = (bf16[64]{0:T(256)(128)(2,1)S(1)}, bf16[64]{0:T(256)(128)(2,1)}, u32[]{:S(2)}) copy-start(bf16[64]{0:T(256)(128)(2,1)} %param.15) | copy-start | bytes 388
  8.0 25.3 %copy-start.15 = (s32[16]{0:T(128)S(1)}, s32[16]{0:T(128)}, u32[]{:S(2)}) copy-start(s32[16]{0:T(128)} %order_ref.3) | copy-start | bytes 196
  8.0 25.4 %copy-start.12 = (s32[1,256]{1,0:T(1,128)S(1)}, s32[1,256]{1,0:T(1,128)}, u32[]{:S(2)}) copy-start(s32[1,256]{1,0:T(1,128)} %param.26) | copy-start | bytes 3076
  8.0 26.3 %copy-start.8 = (bf16[64,2048]{1,0:T(8,128)(2,1)S(1)}, bf16[64,2048]{1,0:T(8,128)(2,1)}, u32[]{:S(2)}) copy-start(bf16[64,2048]{1,0:T(8,128)(2,1)} %param.16) | copy-start | bytes 786436
  8.0 26.3 %copy-start.9 = (bf16[64,256]{1,0:T(8,128)(2,1)S(1)}, bf16[64,256]{1,0:T(8,128)(2,1)}, u32[]{:S(2)}) copy-start(bf16[64,256]{1,0:T(8,128)(2,1)} %param.18) | copy-start | bytes 98308
  8.0 26.3 %copy-start.10 = (bf16[64,256]{1,0:T(8,128)(2,1)S(1)}, bf16[64,256]{1,0:T(8,128)(2,1)}, u32[]{:S(2)}) copy-start(bf16[64,256]{1,0:T(8,128)(2,1)} %param.17) | copy-start | bytes 98308
  8.0 27.1 %copy-start.5 = (bf16[1,256,2048]{2,1,0:T(8,128)(2,1)S(1)}, bf16[1,256,2048]{2,1,0:T(8,128)(2,1)}, u32[]{:S(2)}) copy-start(bf16[1,256,2048]{2,1,0:T(8,128)(2,1)} %param.24) | copy-start | bytes 3145732
  31.8 233.9 %all-gather.8.cloned.1.call-start = ((), (), s32[]{:S(2)}) async-start(), calls=%async_computation.5 | async-start | bytes 6488064 | tf_op jit(solution)/shard_map/all_gather | solution.py:1615
  32.5 349.1 %reduce-scatter.4.cloned.1.call-start = ((), (), s32[]{:S(2)}) async-start(), calls=%async_computation.6 | async-start | bytes 6488064 | tf_op jit(solution)/shard_map/reduce_scatter | solution.py:1619
  292.3 154.4 %reduce-scatter.6.cloned.1.call-start = ((), (), s32[]{:S(2)}) async-start(), calls=%async_computation.7 | async-start | bytes 6488064 | tf_op jit(solution)/shard_map/reduce_scatter | solution.py:1619
  346.1 218.0 %reduce-scatter.8.cloned.1.call-start = ((), (), s32[]{:S(2)}) async-start(), calls=%async_computation.8 | async-start | bytes 6488064 | tf_op jit(solution)/shard_map/reduce_scatter | solution.py:1619
  381.7 0.7 copy-start.11
  446.7 116.1 %copy-start = (f32[256,2048]{1,0:T(8,128)S(1)}, f32[256,2048]{1,0:T(8,128)}, u32[]{:S(2)}) copy-start(f32[256,2048]{1,0:T(8,128)} %get-tuple-element.62.middle_ref) | copy-start | bytes 6291460
  446.7 116.1 %copy-start.2 = (f32[256,2048]{1,0:T(8,128)S(1)}, f32[256,2048]{1,0:T(8,128)}, u32[]{:S(2)}) copy-start(f32[256,2048]{1,0:T(8,128)} %get-tuple-element.90) | copy-start | bytes 6291460
  562.8 3.7 copy-start.1
  564.1 3.8 copy-start.7
  566.5 2.1 copy-start.6
  566.5 2.9 copy-start.3
  567.8 2.7 copy-start.4
Sparse Core Ops, SparseCore 0:
  9.7 76.4 all-gather.5
  87.7 77.2 all-gather.3
  166.7 63.4 all-gather.7
  292.4 61.6 reduce-scatter.3
  356.3 80.2 reduce-scatter.5
  438.7 95.0 reduce-scatter.7

commit v7 on v6

--- a/solution.py
+++ b/solution.py
@@ -1457,8 +1457,7 @@
         own = pl.ds(pl.multiple_of(number * tile, tile), tile)
         q_ref[own, :] = rotated(product(number)).astype(BF16)
 
-    waves((3, 4))
-    waves((2,))
+    waves((3, 4, 2))
     settle((3, 4, 2))
     end()
 

time: 587 us -> 579 us (0.986)
  Pallas kernels: 542 us -> 536 us
    pallas_call x2, Pallas kernels: 176 us -> 185 us  [fold(): pl.pallas_call(functools.partial(fold_kernel, tuple(kinds), tuple(chunk_c...]
    pallas_call x1, Pallas kernels: 165 us -> 158 us  [project(): pl.pallas_call(functools.partial(project_kernel, halves, seq_count, chip_...]
where the time goes in v7:
time: 579 us; the launch traced here: 573 us
  Pallas kernels  536 us (93%)
  between operations  14.8 us (3%)
  local copies, waits for them, and re-layouts  12.8 us (2%)
  other arithmetic  7.48 us (1%)
    pallas_call x2, Pallas kernels, fold(): pl.pallas_call(functools.partial(fold_kernel, tuple(kinds), tuple(chunk_c...  185 us
    pallas_call x1, Pallas kernels, project(): pl.pallas_call(functools.partial(project_kernel, halves, seq_count, chip_...  158 us
    pallas_call x1, Pallas kernels, ffn_grad(): pl.pallas_call(functools.partial(ffn_grad_kernel, seq_count), out_shape=(...  49.9 us
    pallas_call x1, Pallas kernels, ffn_first(): pl.pallas_call(functools.partial(ffn_first_kernel, seq_count), out_shape=...  40.4 us
    pallas_call x1, Pallas kernels, attend_backward(): pl.pallas_call(functools.partial(attend_backward_kernel, span_len, spans)...  33.5 us
    pallas_call x1, Pallas kernels, ffn_act(): pl.pallas_call(ffn_act_kernel, out_shape=(jax.ShapeDtypeStruct((count, wi...  26.5 us
    pallas_call x1, Pallas kernels, attend_forward(): pl.pallas_call(functools.partial(attend_forward_kernel, span_len, spans),...  21.8 us
    pallas_call x1, Pallas kernels, swap(): pl.pallas_call(functools.partial(swap_kernel, scopes, halves, seq_count,...  21.1 us
  transfers between devices with their start and end apart: 6, of which 0 were waited for; matrix products, arithmetic and copies ran while one was open for 2% of the time, Pallas kernels for 89%

profile of v7, /device:TPU:0, one launch (start us, length us, event | category | flops | bytes accessed | tf_op | source)
XLA Modules:
  0.0 572.8 jit_solution(3913730880426188707)
XLA Ops:
  7.2 0.0 all-gather.6.cloned.1.call-start
  7.2 0.7 all-gather.6.cloned.1.call-update
  7.9 0.0 all-gather.4.cloned.1.call-start
  8.0 2.7 bitcast_bitcast_fusion
  10.7 21.1 %swap.1 = (bf16[4,64,1408]{2,1,0:T(8,128)(2,1)}, bf16[4,64,1408]{2,1,0:T(8,128)(2,1)}) custom-call(bf16[4,64,1408]{2,1,0:T(8,128)(2,1)} %get-tuple-element.114.refs_0_, bf16[4,64,1408]{2,1,0:T(8,128)(2,1)} %get-tuple-element.113.refs_1_), custom_call_target="tpu_custom_call" | custom-call | bytes 60000000 | tf_op jit(solution)/shard_map/swap/pallas_call | solution.py:628
  31.8 0.0 all-gather.4.cloned.1.call-update
  31.8 0.0 all-gather.8.cloned.1.call-start
  31.8 0.7 all-gather.8.cloned.1.call-update
  32.5 0.0 reduce-scatter.4.cloned.1.call-start
  32.6 0.1 maximum_bitcast_fusion.1
  32.7 0.6 pad.9.gain_src
  33.3 0.1 dynamic-slice_multiply_fusion
  33.4 0.1 convert_bitcast_fusion
  33.5 0.2 multiply_sine_fusion
  33.7 0.7 pad_maximum_fusion.1
  34.3 0.7 pad_maximum_fusion.w_src
  35.1 1.1 bitcast_select_fusion.g_src.g_ref
  36.2 157.7 %project.1 = (bf16[4,8,16,128]{3,2,1,0:T(8,128)(2,1)}, bf16[4,8,64,2560]{3,2,1,0:T(8,128)(2,1)}, bf16[8,256,512]{2,1,0:T(8,128)(2,1)}, bf16[4,8,64,2048]{3,2,1,0...) custom-call(bf16[16,128]{1,0:T(8,128)(2,1)} %pad.9.gain_src, ...), custom_call_target="tpu_custom_call" | custom-call | bytes 420000000 | tf_op jit(solution)/shard_map/project/pallas_call | solution.py:1476
  193.9 21.8 %attend_forward.1 = (bf16[2048,256]{1,0:T(8,128)(2,1)}, f32[2,4,1024]{2,1,0:T(4,128)}, f32[256,2048]{1,0:T(8,128)}, f32[256,1]{1,0:T(8,128)}, bf16[256,2048]{1,0:T(8,128)(2,1)}) custom-call(s32[1]{0:T(128)} %bitcast.place_ref, s32[16]{0:T(128)} %order_ref.3, s32[1,8]{1,0:T(1,128)} %lens_ref.3, bf16[2048,256]{1,0:T(8,128)(2,1)} %get-tuple-element.58.q_ref, ...), custom_call_target="tpu_custom_call" | custom-call | flops 4294967296 | bytes 16777216 | tf_op jit(solution)/shard_map/attend_forward/pallas_call | solution.py:258
  215.8 0.0 all-gather.6.cloned.1.call-done.wd_ref
  215.8 0.0 all-gather.4.cloned.1.call-done
  215.8 40.4 %ffn_first.1 = (bf16[1024,2048]{1,0:T(8,128)(2,1)}, bf16[1024,2048]{1,0:T(8,128)(2,1)}, f32[1024,1408]{1,0:T(8,128)}, bf16[1024,1408]{1,0:T(8,128)(2,1)}) custom-call(bf16[256,2048]{1,0:T(8,128)(2,1)} %get-tuple-element.63.f_ref, bf16[4,256,2048]{2,1,0:T(8,128)(2,1)} %get-tuple-element.64.g_ref, bf16[2048,1408]{1,0:T(8,128)(2,1)} %bitcast.57, ...), custom_call_target="tpu_custom_call" | custom-call | flops 23622320128 | bytes 48234496 | tf_op jit(solution)/shard_map/ffn_first/pallas_call | solution.py:1247
  256.2 0.0 all-gather.8.cloned.1.call-done
  256.3 26.5 %ffn_act.1 = (bf16[1024,1408]{1,0:T(8,128)(2,1)}, bf16[1024,1408]{1,0:T(8,128)(2,1)}, bf16[1024,1408]{1,0:T(8,128)(2,1)}, bf16[2048,1408]{1,0:T(8,128)(2,1)}) custom-call(bf16[1024,2048]{1,0:T(8,128)(2,1)} %get-tuple-element.66.f_ref, f32[1024,1408]{1,0:T(8,128)} %get-tuple-element.67.gate_ref, bf16[1024,1408]{1,0:T(8,128)(2,1)} %get-tuple-element.68.gh_ref, ...), custom_call_target="tpu_custom_call" | custom-call | flops 11811160064 | bytes 45613056 | tf_op jit(solution)/shard_map/ffn_act/pallas_call | solution.py:1284
  282.8 0.0 reduce-scatter.4.cloned.1.call-update
  282.8 0.0 reduce-scatter.6.cloned.1.call-start
  282.9 49.9 %ffn_grad.1 = (f32[256,2048]{1,0:T(8,128)}, bf16[1024,2048]{1,0:T(8,128)(2,1)}, bf16[2048,1408]{1,0:T(8,128)(2,1)}, bf16[1408,2048]{1,0:T(8,128)(2,1)}) custom-call(bf16[1024,2048]{1,0:T(8,128)(2,1)} %get-tuple-element.66.f_ref, bf16[1024,1408]{1,0:T(8,128)(2,1)} %get-tuple-element.70.hid_ref, bf16[1024,1408]{1,0:T(8,128)(2,1)} %get-tuple-element.71.gg_ref, ...), custom_call_target="tpu_custom_call" | custom-call | flops 41339060224 | bytes 59768832 | tf_op jit(solution)/shard_map/ffn_grad/pallas_call | solution.py:1319
  332.7 0.0 reduce-scatter.6.cloned.1.call-update
  332.8 0.0 reduce-scatter.8.cloned.1.call-start
  332.8 33.5 %attend_backward.1 = (f32[2048,256]{1,0:T(8,128)}, bf16[2048,512]{1,0:T(8,128)(2,1)}, f32[256,2048]{1,0:T(8,128)}, f32[1,2048]{1,0:T(1,128)}) custom-call(s32[1]{0:T(128)} %bitcast.place_ref, s32[16]{0:T(128)} %order_ref.3, s32[1,8]{1,0:T(1,128)} %lens_ref.3, bf16[2048,256]{1,0:T(8,128)(2,1)} %get-tuple-element.58.q_ref, bf16[2048,512]{1,0:T(8,128)(2,1)} %bitcast.62, ...), custom_call_target="tpu_custom_call" | custom-call | flops 7516192768 | bytes 25165824 | tf_op jit(solution)/shard_map/attend_backward/pallas_call | solution.py:294
  366.3 0.0 reduce-scatter.4.cloned.1.call-done.refs_2_
  366.4 0.7 copy-done.11
  367.1 0.1 reshape.144
  367.2 67.9 %fold_kv.1 = (f32[256,512]{1,0:T(8,128)}, f32[256,2048]{1,0:T(8,128)}, f32[64,5632]{1,0:T(8,128)}, bf16[2048,2048]{1,0:T(8,128)(2,1)}, bf16[2048,2048]{1,0:T(8,1...) custom-call(bf16[1,4,2,256,512]{4,3,2,1,0:T(8,128)(2,1)} %bitcast.49, ...), custom_call_target="tpu_custom_call" | custom-call | bytes 180000000 | tf_op jit(solution)/shard_map/fold_kv/pallas_call | solution.py:927
  435.1 0.7 convert_reduce_fusion.1
  435.8 0.1 reshape.143
  435.9 0.1 maximum_bitcast_fusion
  436.0 0.7 pad.10.clone
  436.7 117.1 %fold_weights.1 = (f32[64,2048]{1,0:T(8,128)}, f32[64,2048]{1,0:T(8,128)}, f32[64,512]{1,0:T(8,128)}, f32[16,128]{1,0:T(8,128)}, f32[64,5632]{1,0:T(8,128)}) custom-call(bf16[4,4,2,64,2048]{4,3,2,1,0:T(8,128)(2,1)} %bitcast.41, bf16[4,4,2,64,2048]{4,3,2,1,0:T(8,128)(2,1)} %bitcast.42, bf16[4,4,2,64,512]{4,3,2,1,0:T(8,128)(2,1)} %bitcast.50, ...), custom_call_target="tpu_custom_call" | custom-call | bytes 330000000 | tf_op jit(solution)/shard_map/fold_weights/pallas_call | solution.py:927
  553.8 1.3 slice_bitcast_fusion
  555.2 1.5 fusion.1
  556.7 1.2 fusion
  557.9 2.4 convert_element_type.29
  560.4 1.3 copy.38
  561.7 0.8 copy.39
  562.5 0.8 copy.40
  563.3 1.1 copy.41
  564.4 1.1 copy.42
  (38 shorter events, 0.2 us)
Async XLA Ops:
  7.2 208.6 %all-gather.6.cloned.1.call-start = ((), (), s32[]{:S(2)}) async-start(), calls=%async_computation.4 | async-start | bytes 6488064 | tf_op jit(solution)/shard_map/all_gather | solution.py:1614
  7.9 207.9 %all-gather.4.cloned.1.call-start = ((), (), s32[]{:S(2)}) async-start(), calls=%async_computation.3 | async-start | bytes 6488064 | tf_op jit(solution)/shard_map/all_gather | solution.py:1614
  8.0 24.6 %copy-start.13 = (bf16[64]{0:T(256)(128)(2,1)S(1)}, bf16[64]{0:T(256)(128)(2,1)}, u32[]{:S(2)}) copy-start(bf16[64]{0:T(256)(128)(2,1)} %param.20) | copy-start | bytes 388
  8.0 24.6 %copy-start.14 = (bf16[64]{0:T(256)(128)(2,1)S(1)}, bf16[64]{0:T(256)(128)(2,1)}, u32[]{:S(2)}) copy-start(bf16[64]{0:T(256)(128)(2,1)} %param.15) | copy-start | bytes 388
  8.0 25.3 %copy-start.15 = (s32[16]{0:T(128)S(1)}, s32[16]{0:T(128)}, u32[]{:S(2)}) copy-start(s32[16]{0:T(128)} %order_ref.3) | copy-start | bytes 196
  8.0 25.4 %copy-start.12 = (s32[1,256]{1,0:T(1,128)S(1)}, s32[1,256]{1,0:T(1,128)}, u32[]{:S(2)}) copy-start(s32[1,256]{1,0:T(1,128)} %param.26) | copy-start | bytes 3076
  8.0 26.3 %copy-start.8 = (bf16[64,2048]{1,0:T(8,128)(2,1)S(1)}, bf16[64,2048]{1,0:T(8,128)(2,1)}, u32[]{:S(2)}) copy-start(bf16[64,2048]{1,0:T(8,128)(2,1)} %param.16) | copy-start | bytes 786436
  8.0 26.3 %copy-start.9 = (bf16[64,256]{1,0:T(8,128)(2,1)S(1)}, bf16[64,256]{1,0:T(8,128)(2,1)}, u32[]{:S(2)}) copy-start(bf16[64,256]{1,0:T(8,128)(2,1)} %param.18) | copy-start | bytes 98308
  8.0 26.3 %copy-start.10 = (bf16[64,256]{1,0:T(8,128)(2,1)S(1)}, bf16[64,256]{1,0:T(8,128)(2,1)}, u32[]{:S(2)}) copy-start(bf16[64,256]{1,0:T(8,128)(2,1)} %param.17) | copy-start | bytes 98308
  8.0 27.1 %copy-start.5 = (bf16[1,256,2048]{2,1,0:T(8,128)(2,1)S(1)}, bf16[1,256,2048]{2,1,0:T(8,128)(2,1)}, u32[]{:S(2)}) copy-start(bf16[1,256,2048]{2,1,0:T(8,128)(2,1)} %param.24) | copy-start | bytes 3145732
  31.8 224.5 %all-gather.8.cloned.1.call-start = ((), (), s32[]{:S(2)}) async-start(), calls=%async_computation.5 | async-start | bytes 6488064 | tf_op jit(solution)/shard_map/all_gather | solution.py:1614
  32.5 333.8 %reduce-scatter.4.cloned.1.call-start = ((), (), s32[]{:S(2)}) async-start(), calls=%async_computation.6 | async-start | bytes 6488064 | tf_op jit(solution)/shard_map/reduce_scatter | solution.py:1618
  282.8 153.9 %reduce-scatter.6.cloned.1.call-start = ((), (), s32[]{:S(2)}) async-start(), calls=%async_computation.7 | async-start | bytes 6488064 | tf_op jit(solution)/shard_map/reduce_scatter | solution.py:1618
  332.8 225.2 %reduce-scatter.8.cloned.1.call-start = ((), (), s32[]{:S(2)}) async-start(), calls=%async_computation.8 | async-start | bytes 6488064 | tf_op jit(solution)/shard_map/reduce_scatter | solution.py:1618
  366.3 0.7 copy-start.11
  436.7 120.0 %copy-start = (f32[256,2048]{1,0:T(8,128)S(1)}, f32[256,2048]{1,0:T(8,128)}, u32[]{:S(2)}) copy-start(f32[256,2048]{1,0:T(8,128)} %get-tuple-element.62.middle_ref) | copy-start | bytes 6291460
  436.7 120.0 %copy-start.2 = (f32[256,2048]{1,0:T(8,128)S(1)}, f32[256,2048]{1,0:T(8,128)}, u32[]{:S(2)}) copy-start(f32[256,2048]{1,0:T(8,128)} %get-tuple-element.90) | copy-start | bytes 6291460
  556.7 3.7 copy-start.1
  557.9 3.8 copy-start.7
  560.4 2.1 copy-start.6
  560.4 2.9 copy-start.3
  561.7 2.7 copy-start.4
Sparse Core Ops, SparseCore 0:
  9.7 76.4 all-gather.5
  87.7 79.6 all-gather.3
  169.1 60.1 all-gather.7
  282.9 65.7 reduce-scatter.3
  350.8 80.0 reduce-scatter.5
  433.1 96.4 reduce-scatter.7

commit v8 on v7

--- a/solution.py
+++ b/solution.py
@@ -505,10 +505,16 @@
         for _, copy, _ in steps:
             started.append((there & onward, copy))
 
+    def piece(item, place):
+        if len(sources[item].shape) == 3:
+            return sources[item].at[place]
+        width = results[item].shape[-1]
+        return sources[item].at[:, pl.ds(pl.multiple_of(place * width, 128), width)]
+
     def begin(items):
         for item in items:
             target, _ = block(item, seq, chip, core)
-            own = sources[item].at[seq] if scopes[item] == "swap" else sources[item]
+            own = piece(item, seq) if scopes[item] == "swap" else sources[item]
             locals_[item] = pltpu.make_async_copy(own, target, local_sem.at[item])
             locals_[item].start()
         for item in pick(items, "ctx", "all"):
@@ -522,7 +528,7 @@
             start(
                 [
                     descriptor(
-                        item, seq, chip, None, number, {"seq": place}, sources[item].at[place]
+                        item, seq, chip, None, number, {"seq": place}, piece(item, place)
                     )
                     for number, place in enumerate(planes)
                 ]
@@ -594,6 +600,8 @@
         lead = {"all": (seq_count, 2 * chip_count), "ctx": (2 * chip_count,)}.get(scope, (seq_count,))
         halves.append(seq_count == 4 and scope in ("all", "seq") and array.shape[0] % 32 == 0)
         shape = array.shape if scope == "swap" else lead + array.shape
+        if scope == "swap" and array.ndim == 2:
+            shape = (seq_count, array.shape[0], array.shape[1] // seq_count)
         shapes.append(jax.ShapeDtypeStruct(shape, array.dtype))
         rows = chip_count if scope in ("all", "ctx") else 1
         sends.append(pltpu.SemaphoreType.DMA((rows, kinds)))
@@ -1412,7 +1420,7 @@
     rms_ref[...] = rms
     relays((0, 1))
     waves((0, 1))
-    begin((3, 4))
+    begin((3,))
     settle((0, 1))
 
     def load(number):
@@ -1450,6 +1458,7 @@
     kv_own[:, :tile] = rotated(product(count - 2)).T.astype(BF16)
     kv_own[:, tile:] = product(count - 1).astype(BF16)
     begin((2,))
+    begin((4,))
     relays((3, 4))
 
     @pl.loop(0, count - 2)
@@ -1646,6 +1655,8 @@
     ff_part = w_gate.shape[1] // seq_count
 
     def split_columns(weight):
+        if ff_part % 128 == 0:
+            return weight
         return weight.reshape(own_rows, seq_count, ff_part).transpose(1, 0, 2)
 
     own_spans = lax.dynamic_slice_in_dim(block_order, place[0] * (rows // span_len), rows // span_len)

time: 579 us -> 588 us (1.016)
  Pallas kernels: 536 us -> 549 us
    pallas_call x2, Pallas kernels: 185 us -> 174 us  [fold(): pl.pallas_call(functools.partial(fold_kernel, tuple(kinds), tuple(chunk_c...]
    pallas_call x1, Pallas kernels: 33.5 us -> 41.4 us  [attend_backward(): pl.pallas_call(functools.partial(attend_backward_kernel, span_len, spans)...]
    pallas_call x1, Pallas kernels: 49.9 us -> 57.1 us  [ffn_grad(): pl.pallas_call(functools.partial(ffn_grad_kernel, seq_count), out_shape=(...]
  transfers between devices with their start and end apart: 6 -> 6, of which waited for: 0 -> 0; matrix products, arithmetic and copies ran while one was open for 2% -> 2% of each run, Pallas kernels for 89% -> 90%
where the time goes in v8:
time: 588 us; the launch traced here: 583 us
  Pallas kernels  549 us (93%)
  between operations  14.8 us (3%)
  local copies, waits for them, and re-layouts  10.2 us (2%)
  other arithmetic  7.48 us (1%)
    pallas_call x2, Pallas kernels, fold(): pl.pallas_call(functools.partial(fold_kernel, tuple(kinds), tuple(chunk_c...  174 us
    pallas_call x1, Pallas kernels, project(): pl.pallas_call(functools.partial(project_kernel, halves, seq_count, chip_...  161 us
    pallas_call x1, Pallas kernels, ffn_grad(): pl.pallas_call(functools.partial(ffn_grad_kernel, seq_count), out_shape=(...  57.1 us
    pallas_call x1, Pallas kernels, attend_backward(): pl.pallas_call(functools.partial(attend_backward_kernel, span_len, spans)...  41.4 us
    pallas_call x1, Pallas kernels, ffn_first(): pl.pallas_call(functools.partial(ffn_first_kernel, seq_count), out_shape=...  40.3 us
    pallas_call x1, Pallas kernels, attend_forward(): pl.pallas_call(functools.partial(attend_forward_kernel, span_len, spans),...  27.4 us
    pallas_call x1, Pallas kernels, ffn_act(): pl.pallas_call(ffn_act_kernel, out_shape=(jax.ShapeDtypeStruct((count, wi...  26.5 us
    pallas_call x1, Pallas kernels, swap(): pl.pallas_call(functools.partial(swap_kernel, scopes, halves, seq_count,...  21.1 us
  transfers between devices with their start and end apart: 6, of which 0 were waited for; matrix products, arithmetic and copies ran while one was open for 2% of the time, Pallas kernels for 90%

profile of v8, /device:TPU:0, one launch (start us, length us, event | category | flops | bytes accessed | tf_op | source)
XLA Modules:
  0.0 583.2 jit_solution(14791185984632380840)
XLA Ops:
  7.3 0.0 all-gather.6.cloned.1.call-start
  7.3 0.7 all-gather.6.cloned.1.call-update
  8.0 0.0 all-gather.4.cloned.1.call-start
  8.0 21.1 %swap.1 = (bf16[4,64,1408]{2,1,0:T(8,128)(2,1)}, bf16[4,64,1408]{2,1,0:T(8,128)(2,1)}) custom-call(bf16[64,5632]{1,0:T(8,128)(2,1)} %refs_0_.1, bf16[64,5632]{1,0:T(8,128)(2,1)} %refs_1_.1), custom_call_target="tpu_custom_call" | custom-call | bytes 60000000 | tf_op jit(solution)/shard_map/swap/pallas_call | solution.py:636
  29.2 0.0 all-gather.4.cloned.1.call-update
  29.2 0.0 all-gather.8.cloned.1.call-start
  29.2 0.7 all-gather.8.cloned.1.call-update
  29.9 0.0 reduce-scatter.4.cloned.1.call-start
  30.0 0.1 maximum_bitcast_fusion.1
  30.1 0.6 pad.9.gain_src
  30.7 0.1 dynamic-slice_multiply_fusion
  30.8 0.1 convert_bitcast_fusion
  30.9 0.2 multiply_sine_fusion
  31.1 0.7 pad_maximum_fusion.1
  31.7 0.7 pad_maximum_fusion.w_src
  32.5 1.1 bitcast_select_fusion.g_src.g_ref
  33.6 161.3 %project.1 = (bf16[4,8,16,128]{3,2,1,0:T(8,128)(2,1)}, bf16[4,8,64,2560]{3,2,1,0:T(8,128)(2,1)}, bf16[8,256,512]{2,1,0:T(8,128)(2,1)}, bf16[4,8,64,2048]{3,2,1,0...) custom-call(bf16[16,128]{1,0:T(8,128)(2,1)} %pad.9.gain_src, ...), custom_call_target="tpu_custom_call" | custom-call | bytes 420000000 | tf_op jit(solution)/shard_map/project/pallas_call | solution.py:1485
  194.9 27.4 %attend_forward.1 = (bf16[2048,256]{1,0:T(8,128)(2,1)}, f32[2,4,1024]{2,1,0:T(4,128)}, f32[256,2048]{1,0:T(8,128)}, f32[256,1]{1,0:T(8,128)}, bf16[256,2048]{1,0:T(8,128)(2,1)}) custom-call(s32[1]{0:T(128)} %bitcast.place_ref, s32[16]{0:T(128)} %order_ref.3, s32[1,8]{1,0:T(1,128)} %lens_ref.3, bf16[2048,256]{1,0:T(8,128)(2,1)} %get-tuple-element.58.q_ref, ...), custom_call_target="tpu_custom_call" | custom-call | flops 4294967296 | bytes 16777216 | tf_op jit(solution)/shard_map/attend_forward/pallas_call | solution.py:258
  222.3 0.0 all-gather.6.cloned.1.call-done.wd_ref
  222.4 0.0 all-gather.4.cloned.1.call-done
  222.4 40.3 %ffn_first.1 = (bf16[1024,2048]{1,0:T(8,128)(2,1)}, bf16[1024,2048]{1,0:T(8,128)(2,1)}, f32[1024,1408]{1,0:T(8,128)}, bf16[1024,1408]{1,0:T(8,128)(2,1)}) custom-call(bf16[256,2048]{1,0:T(8,128)(2,1)} %get-tuple-element.63.f_ref, bf16[4,256,2048]{2,1,0:T(8,128)(2,1)} %get-tuple-element.64.g_ref, bf16[2048,1408]{1,0:T(8,128)(2,1)} %bitcast.45, ...), custom_call_target="tpu_custom_call" | custom-call | flops 23622320128 | bytes 48234496 | tf_op jit(solution)/shard_map/ffn_first/pallas_call | solution.py:1255
  262.7 0.0 all-gather.8.cloned.1.call-done
  262.8 26.5 %ffn_act.1 = (bf16[1024,1408]{1,0:T(8,128)(2,1)}, bf16[1024,1408]{1,0:T(8,128)(2,1)}, bf16[1024,1408]{1,0:T(8,128)(2,1)}, bf16[2048,1408]{1,0:T(8,128)(2,1)}) custom-call(bf16[1024,2048]{1,0:T(8,128)(2,1)} %get-tuple-element.66.f_ref, f32[1024,1408]{1,0:T(8,128)} %get-tuple-element.67.gate_ref, bf16[1024,1408]{1,0:T(8,128)(2,1)} %get-tuple-element.68.gh_ref, ...), custom_call_target="tpu_custom_call" | custom-call | flops 11811160064 | bytes 45613056 | tf_op jit(solution)/shard_map/ffn_act/pallas_call | solution.py:1292
  289.3 0.0 reduce-scatter.4.cloned.1.call-update
  289.3 0.0 reduce-scatter.6.cloned.1.call-start
  289.4 57.1 %ffn_grad.1 = (f32[256,2048]{1,0:T(8,128)}, bf16[1024,2048]{1,0:T(8,128)(2,1)}, bf16[2048,1408]{1,0:T(8,128)(2,1)}, bf16[1408,2048]{1,0:T(8,128)(2,1)}) custom-call(bf16[1024,2048]{1,0:T(8,128)(2,1)} %get-tuple-element.66.f_ref, bf16[1024,1408]{1,0:T(8,128)(2,1)} %get-tuple-element.70.hid_ref, bf16[1024,1408]{1,0:T(8,128)(2,1)} %get-tuple-element.71.gg_ref, ...), custom_call_target="tpu_custom_call" | custom-call | flops 41339060224 | bytes 59768832 | tf_op jit(solution)/shard_map/ffn_grad/pallas_call | solution.py:1327
  346.5 0.0 reduce-scatter.6.cloned.1.call-update
  346.5 0.0 reduce-scatter.8.cloned.1.call-start
  346.5 41.4 %attend_backward.1 = (f32[2048,256]{1,0:T(8,128)}, bf16[2048,512]{1,0:T(8,128)(2,1)}, f32[256,2048]{1,0:T(8,128)}, f32[1,2048]{1,0:T(1,128)}) custom-call(s32[1]{0:T(128)} %bitcast.place_ref, s32[16]{0:T(128)} %order_ref.3, s32[1,8]{1,0:T(1,128)} %lens_ref.3, bf16[2048,256]{1,0:T(8,128)(2,1)} %get-tuple-element.58.q_ref, bf16[2048,512]{1,0:T(8,128)(2,1)} %bitcast.50, ...), custom_call_target="tpu_custom_call" | custom-call | flops 7516192768 | bytes 25165824 | tf_op jit(solution)/shard_map/attend_backward/pallas_call | solution.py:294
  387.9 0.0 reduce-scatter.4.cloned.1.call-done.refs_2_
  388.0 0.0 reduce-scatter.8.cloned.1.call-update
  388.0 0.7 copy-done.11
  388.7 0.1 reshape.136
  388.8 65.3 %fold_kv.1 = (f32[256,512]{1,0:T(8,128)}, f32[256,2048]{1,0:T(8,128)}, f32[64,5632]{1,0:T(8,128)}, bf16[2048,2048]{1,0:T(8,128)(2,1)}, bf16[2048,2048]{1,0:T(8,1...) custom-call(bf16[1,4,2,256,512]{4,3,2,1,0:T(8,128)(2,1)} %bitcast.39, ...), custom_call_target="tpu_custom_call" | custom-call | bytes 180000000 | tf_op jit(solution)/shard_map/fold_kv/pallas_call | solution.py:935
  454.1 0.7 convert_reduce_fusion.1
  454.9 0.1 reshape.135
  454.9 0.1 maximum_bitcast_fusion
  455.0 0.7 pad.10.clone
  455.7 108.5 %fold_weights.1 = (f32[64,2048]{1,0:T(8,128)}, f32[64,2048]{1,0:T(8,128)}, f32[64,512]{1,0:T(8,128)}, f32[16,128]{1,0:T(8,128)}, f32[64,5632]{1,0:T(8,128)}) custom-call(bf16[4,4,2,64,2048]{4,3,2,1,0:T(8,128)(2,1)} %bitcast.31, bf16[4,4,2,64,2048]{4,3,2,1,0:T(8,128)(2,1)} %bitcast.32, bf16[4,4,2,64,512]{4,3,2,1,0:T(8,128)(2,1)} %bitcast.40, ...), custom_call_target="tpu_custom_call" | custom-call | bytes 330000000 | tf_op jit(solution)/shard_map/fold_weights/pallas_call | solution.py:935
  564.2 1.3 slice_bitcast_fusion
  565.6 1.5 fusion.1
  567.1 1.2 fusion
  568.3 2.4 convert_element_type.29
  570.8 1.3 copy.32
  572.1 0.8 copy.33
  572.9 0.8 copy.34
  573.7 1.1 copy.35
  574.8 1.1 copy.36
  (37 shorter events, 0.1 us)
Async XLA Ops:
  7.2 22.8 %copy-start.13 = (bf16[64]{0:T(256)(128)(2,1)S(1)}, bf16[64]{0:T(256)(128)(2,1)}, u32[]{:S(2)}) copy-start(bf16[64]{0:T(256)(128)(2,1)} %param.20) | copy-start | bytes 388
  7.2 22.8 %copy-start.14 = (bf16[64]{0:T(256)(128)(2,1)S(1)}, bf16[64]{0:T(256)(128)(2,1)}, u32[]{:S(2)}) copy-start(bf16[64]{0:T(256)(128)(2,1)} %param.15) | copy-start | bytes 388
  7.2 23.5 %copy-start.15 = (s32[16]{0:T(128)S(1)}, s32[16]{0:T(128)}, u32[]{:S(2)}) copy-start(s32[16]{0:T(128)} %order_ref.3) | copy-start | bytes 196
  7.2 23.6 %copy-start.12 = (s32[1,256]{1,0:T(1,128)S(1)}, s32[1,256]{1,0:T(1,128)}, u32[]{:S(2)}) copy-start(s32[1,256]{1,0:T(1,128)} %param.26) | copy-start | bytes 3076
  7.2 24.5 %copy-start.9 = (bf16[64,256]{1,0:T(8,128)(2,1)S(1)}, bf16[64,256]{1,0:T(8,128)(2,1)}, u32[]{:S(2)}) copy-start(bf16[64,256]{1,0:T(8,128)(2,1)} %param.18) | copy-start | bytes 98308
  7.2 24.5 %copy-start.10 = (bf16[64,256]{1,0:T(8,128)(2,1)S(1)}, bf16[64,256]{1,0:T(8,128)(2,1)}, u32[]{:S(2)}) copy-start(bf16[64,256]{1,0:T(8,128)(2,1)} %param.17) | copy-start | bytes 98308
  7.2 24.5 %copy-start.8 = (bf16[64,2048]{1,0:T(8,128)(2,1)S(1)}, bf16[64,2048]{1,0:T(8,128)(2,1)}, u32[]{:S(2)}) copy-start(bf16[64,2048]{1,0:T(8,128)(2,1)} %param.16) | copy-start | bytes 786436
  7.3 25.2 %copy-start.5 = (bf16[1,256,2048]{2,1,0:T(8,128)(2,1)S(1)}, bf16[1,256,2048]{2,1,0:T(8,128)(2,1)}, u32[]{:S(2)}) copy-start(bf16[1,256,2048]{2,1,0:T(8,128)(2,1)} %param.24) | copy-start | bytes 3145732
  7.3 215.1 %all-gather.6.cloned.1.call-start = ((), (), s32[]{:S(2)}) async-start(), calls=%async_computation.4 | async-start | bytes 6488064 | tf_op jit(solution)/shard_map/all_gather | solution.py:1623
  8.0 214.4 %all-gather.4.cloned.1.call-start = ((), (), s32[]{:S(2)}) async-start(), calls=%async_computation.3 | async-start | bytes 6488064 | tf_op jit(solution)/shard_map/all_gather | solution.py:1623
  29.2 233.6 %all-gather.8.cloned.1.call-start = ((), (), s32[]{:S(2)}) async-start(), calls=%async_computation.5 | async-start | bytes 6488064 | tf_op jit(solution)/shard_map/all_gather | solution.py:1623
  29.9 358.1 %reduce-scatter.4.cloned.1.call-start = ((), (), s32[]{:S(2)}) async-start(), calls=%async_computation.6 | async-start | bytes 6488064 | tf_op jit(solution)/shard_map/reduce_scatter | solution.py:1627
  289.3 166.4 %reduce-scatter.6.cloned.1.call-start = ((), (), s32[]{:S(2)}) async-start(), calls=%async_computation.7 | async-start | bytes 6488064 | tf_op jit(solution)/shard_map/reduce_scatter | solution.py:1627
  346.5 221.8 %reduce-scatter.8.cloned.1.call-start = ((), (), s32[]{:S(2)}) async-start(), calls=%async_computation.8 | async-start | bytes 6488064 | tf_op jit(solution)/shard_map/reduce_scatter | solution.py:1627
  388.0 0.7 copy-start.11
  455.7 111.4 %copy-start = (f32[256,2048]{1,0:T(8,128)S(1)}, f32[256,2048]{1,0:T(8,128)}, u32[]{:S(2)}) copy-start(f32[256,2048]{1,0:T(8,128)} %get-tuple-element.62.middle_ref) | copy-start | bytes 6291460
  455.7 111.4 %copy-start.2 = (f32[256,2048]{1,0:T(8,128)S(1)}, f32[256,2048]{1,0:T(8,128)}, u32[]{:S(2)}) copy-start(f32[256,2048]{1,0:T(8,128)} %get-tuple-element.90) | copy-start | bytes 6291460
  567.1 3.7 copy-start.1
  568.3 3.8 copy-start.7
  570.8 2.1 copy-start.6
  570.8 2.9 copy-start.3
  572.1 2.7 copy-start.4
Sparse Core Ops, SparseCore 0:
  9.7 77.0 all-gather.5
  88.5 79.7 all-gather.3
  169.9 59.3 all-gather.7
  289.4 65.0 reduce-scatter.3
  356.7 80.1 reduce-scatter.5
  439.0 88.1 reduce-scatter.7
